TPU v7x, 32 devices: a whole 2x2x4 slice. The times are simulated.
32 devices in a mesh: bead: 2 (over x), space: 16 (over z, y, core).
Axes of the slice: x: 2, y: 2, z: 4, core: 2. Of those that a mesh axis runs over, the one named last changes fastest.
Arguments:
- positions: float32 [32, 3, 6144], P('bead', None, 'space'), as said below
- charges: float32 [6144], P('space'), may hold values from -3 to 3
- polar: float32 [6144], P('space'), may hold values from 0.4 to 1.6
- molecule: int32 [6144], P('space'), may hold values from 0 to 2047, as said below
Outputs:
- total_field: float32 [32, 3, 6144], P('bead', None, 'space')
- dipoles: float32 [4, 3, 6144], P(None, None, 'space')
Inputs may be any that keep to these rules, and one draw needn't show every extreme that they name: Each molecule has three atoms, all in one slab block of 384 atoms; no id appears in two blocks. `positions`: in slab block d every atom's first coordinate lies between 15.2 d and 15.2 (d + 1).
All inputs are finite; a program needn't handle non-finite values.
Results may differ from a plain program's by a relative error of at most 0.0003.
Values sent between devices are 32-bit elements; how exact they have to be, the bound alone decides.
No kernel may reach another device: no remote copies, remote signals or barrier semaphores. Data moves between devices by JAX's collectives and lax.ppermute only.
A program may use at most 64 MiB of HBM per device.

v0:
```python
import jax
import jax.numpy as jnp
from jax import lax
from jax.sharding import PartitionSpec as P

BEADS = 32
CONTR = 4
ITERS = 2


CUTOFF = 9.0


def padded(block, sides, width):
    for axis, dim in sides:
        count = lax.axis_size(axis)
        forward = [(i, i + 1) for i in range(count - 1)]
        backward = [(target, source) for source, target in forward]
        low = lax.ppermute(
            lax.slice_in_dim(block, block.shape[dim] - width, None, axis=dim), axis, forward
        )
        high = lax.ppermute(lax.slice_in_dim(block, 0, width, axis=dim), axis, backward)
        block = jnp.concatenate([low, block, high], axis=dim)
    return block


def pair_field(
    target,
    target_alpha,
    target_mol,
    source,
    source_charge,
    source_alpha,
    source_dip,
    source_mol,
    dipolar,
):
    width = source.shape[1] // 18
    count = source.shape[1] // width
    blocks = (
        source.reshape(3, count, width).transpose(1, 0, 2),
        source_charge.reshape(count, width),
        source_alpha.reshape(count, width),
        source_dip.reshape(3, count, width).transpose(1, 0, 2),
        source_mol.reshape(count, width),
    )

    def step(total, block):
        spot, charge, alpha, dip, mol = block
        diff = target[:, :, None] - spot[:, None, :]
        dist2 = jnp.sum(diff * diff, axis=0)
        keep = (
            (alpha[None, :] > 0.0)
            & (target_mol[:, None] != mol[None, :])
            & (dist2 < CUTOFF * CUTOFF)
        )
        safe2 = jnp.where(keep, dist2, 1.0)
        inverse = lax.rsqrt(safe2)
        inv3 = inverse * inverse * inverse
        both = jnp.where(keep, target_alpha[:, None] * alpha[None, :], 1.0)
        cube = 0.39 * safe2 * jnp.sqrt(safe2) * lax.rsqrt(both)
        decay = jnp.exp(-cube)
        damp3 = 1.0 - decay
        damp5 = 1.0 - (1.0 + cube) * decay
        ratio = 1.0 - dist2 / (CUTOFF * CUTOFF)
        taper = jnp.where(keep, ratio * ratio, 0.0)
        if dipolar:
            along = jnp.sum(diff * dip[:, None, :], axis=0)
            term = (3.0 * taper * damp5 * inv3 * inverse * inverse * along)[None] * diff - (
                taper * damp3 * inv3
            )[None] * dip[:, None, :]
        else:
            term = (taper * damp3 * inv3 * charge[None, :])[None] * diff
        return (total + jnp.sum(term, axis=2), None)

    start = jnp.zeros((3, target.shape[1]), jnp.float32)
    total, unused = lax.scan(step, start, blocks)
    return total


def body(positions, charges, polar, molecule):
    beads_here = positions.shape[0]
    atoms = positions.shape[2]
    rank = lax.axis_index("bead")
    local = (rank * beads_here + jnp.arange(beads_here, dtype=jnp.int32)).astype(jnp.float32)
    kidx = jnp.arange(CONTR, dtype=jnp.float32)[:, None] / CONTR
    theta = 2.0 * jnp.pi * (kidx - local[None, :] / BEADS)
    series = 1.0 + 2.0 * jnp.cos(theta) + jnp.cos(2.0 * theta)
    contract = series / BEADS
    spread_back = series.T / CONTR
    high = lax.Precision.HIGHEST
    packed = jnp.concatenate(
        [positions.reshape(beads_here * 3, atoms), charges[None], polar[None]], 0
    )
    rim = padded(packed, (("space", 1),), atoms)
    source_pos = rim[: beads_here * 3].reshape(beads_here, 3, 3 * atoms)
    source_charge = rim[beads_here * 3]
    source_alpha = rim[beads_here * 3 + 1]
    outside = jnp.full((atoms,), -1, jnp.int32)
    source_mol = jnp.concatenate([outside, molecule, outside])
    blank_dip = jnp.zeros((3, 3 * atoms), jnp.float32)
    blank_charge = jnp.zeros((3 * atoms,), jnp.float32)
    perm = lax.map(
        lambda pair: pair_field(
            pair[0],
            polar,
            molecule,
            pair[1],
            source_charge,
            source_alpha,
            blank_dip,
            source_mol,
            False,
        ),
        (positions, source_pos),
    )
    stacked = jnp.concatenate([positions, perm], 1)
    contracted = jnp.einsum("kb,bxa->kxa", contract, stacked, precision=high)
    whole = lax.psum(contracted, "bead")
    cpos = whole[:, :3]
    cfield = whole[:, 3:]
    source_cpos = padded(cpos.reshape(CONTR * 3, atoms), (("space", 1),), atoms).reshape(
        CONTR, 3, 3 * atoms
    )

    def induce(dip):
        source_dip = padded(dip.reshape(CONTR * 3, atoms), (("space", 1),), atoms).reshape(
            CONTR, 3, 3 * atoms
        )
        return lax.map(
            lambda item: pair_field(
                item[0],
                polar,
                molecule,
                item[1],
                blank_charge,
                source_alpha,
                item[2],
                source_mol,
                True,
            ),
            (cpos, source_cpos, source_dip),
        )

    moment = polar[None, None, :] * cfield
    for step in range(ITERS):
        moment = polar[None, None, :] * (cfield + induce(moment))
    induced = induce(moment)
    total = perm + jnp.einsum("bk,kxa->bxa", spread_back, induced, precision=high)
    return (total, moment)


def solution(mesh):
    in_specs = (P("bead", None, "space"), P("space"), P("space"), P("space"))
    out_specs = (P("bead", None, "space"), P(None, None, "space"))
    return jax.shard_map(body, mesh=mesh, in_specs=in_specs, out_specs=out_specs, check_vma=False)
```

profile of v0, /device:TPU:21, one launch (start us, length us, event | category | flops | bytes accessed | tf_op | source)
XLA Modules:
  0.0 350.9 jit_solution(2971484989202291845)
XLA Ops:
  2.9 3.7 %collective-permute-start = (f32[50,384]{1,0:T(8,128)S(1)}, f32[50,384]{1,0:T(8,128)S(1)}, u32[]{:S(2)}, u32[]{:S(2)}) collective-permute-start(f32[50,384]{1,0:T(8,128)S(1)} %pad_maximum_fusion.1), channel_id=1, source_target_pairs={{0,1},{1,2},{2,3},{3,4},{4,5},{5,6},{6,7},{7,8},{8,9},{9,10},{10,1... | collective-permute-start | bytes 230408 | tf_op jit(solution)/shard_map/ppermute | solution.py:19
  6.7 1.9 collective-permute-start.1
  9.3 4.0 %collective-permute-done.1 = f32[50,384]{1,0:T(8,128)S(1)} collective-permute-done((f32[50,384]{1,0:T(8,128)S(1)}, f32[50,384]{1,0:T(8,128)S(1)}, u32[]{:S(2)}, u32[]{:S(2)}) %collective-permute-start.1) | collective-permute-done | bytes 76832 | tf_op jit(solution)/shard_map/ppermute | solution.py:22
  13.5 159.5 %while.85 = (s32[]{:T(128)}, f32[16,3,384]{2,0,1:T(8,128)S(1)}, f32[16,3,1152]{2,1,0:T(4,128)S(1)}, f32[1,1152]{1,0:T(1,128)S(1)}, f32[1,1152]{1,0:T(1,128)S(1)}...) while((s32[]{:T(128)}, f32[16,3,384]{2,0,1:T(8,128)S(1)}, ...), condition=%wide.region_5.6_spmd, body=%wide.region_0.5_spmd.sunk | while | flops 935109 | bytes 560656 | solution.py:103
  13.9 9.5 %while.92 = (s32[]{:T(128)}, f32[3,384]{1,0:T(4,128)S(1)}, f32[18,64]{1,0:T(8,128)S(1)}, s32[384]{0:T(512)S(1)}, s32[18,64]{1,0:T(8,128)S(1)}, /*index=5*/f32[3,...) while((s32[]{:T(128)}, f32[3,384]{1,0:T(4,128)S(1)}, ...), condition=%wide.region_4.4_spmd.clone, body=%wide.region_1.3_spmd.clone.sunk | while | flops 935107 | bytes 431367 | solution.py:77
  23.9 9.5 %while.92 = (s32[]{:T(128)}, f32[3,384]{1,0:T(4,128)S(1)}, f32[18,64]{1,0:T(8,128)S(1)}, s32[384]{0:T(512)S(1)}, s32[18,64]{1,0:T(8,128)S(1)}, /*index=5*/f32[3,...) while((s32[]{:T(128)}, f32[3,384]{1,0:T(4,128)S(1)}, ...), condition=%wide.region_4.4_spmd.clone, body=%wide.region_1.3_spmd.clone.sunk | while | flops 935107 | bytes 431367 | solution.py:77
  33.9 9.5 %while.92 = (s32[]{:T(128)}, f32[3,384]{1,0:T(4,128)S(1)}, f32[18,64]{1,0:T(8,128)S(1)}, s32[384]{0:T(512)S(1)}, s32[18,64]{1,0:T(8,128)S(1)}, /*index=5*/f32[3,...) while((s32[]{:T(128)}, f32[3,384]{1,0:T(4,128)S(1)}, ...), condition=%wide.region_4.4_spmd.clone, body=%wide.region_1.3_spmd.clone.sunk | while | flops 935107 | bytes 431367 | solution.py:77
  43.8 9.5 %while.92 = (s32[]{:T(128)}, f32[3,384]{1,0:T(4,128)S(1)}, f32[18,64]{1,0:T(8,128)S(1)}, s32[384]{0:T(512)S(1)}, s32[18,64]{1,0:T(8,128)S(1)}, /*index=5*/f32[3,...) while((s32[]{:T(128)}, f32[3,384]{1,0:T(4,128)S(1)}, ...), condition=%wide.region_4.4_spmd.clone, body=%wide.region_1.3_spmd.clone.sunk | while | flops 935107 | bytes 431367 | solution.py:77
  53.8 9.5 %while.92 = (s32[]{:T(128)}, f32[3,384]{1,0:T(4,128)S(1)}, f32[18,64]{1,0:T(8,128)S(1)}, s32[384]{0:T(512)S(1)}, s32[18,64]{1,0:T(8,128)S(1)}, /*index=5*/f32[3,...) while((s32[]{:T(128)}, f32[3,384]{1,0:T(4,128)S(1)}, ...), condition=%wide.region_4.4_spmd.clone, body=%wide.region_1.3_spmd.clone.sunk | while | flops 935107 | bytes 431367 | solution.py:77
  63.8 9.5 %while.92 = (s32[]{:T(128)}, f32[3,384]{1,0:T(4,128)S(1)}, f32[18,64]{1,0:T(8,128)S(1)}, s32[384]{0:T(512)S(1)}, s32[18,64]{1,0:T(8,128)S(1)}, /*index=5*/f32[3,...) while((s32[]{:T(128)}, f32[3,384]{1,0:T(4,128)S(1)}, ...), condition=%wide.region_4.4_spmd.clone, body=%wide.region_1.3_spmd.clone.sunk | while | flops 935107 | bytes 431367 | solution.py:77
  73.7 9.5 %while.92 = (s32[]{:T(128)}, f32[3,384]{1,0:T(4,128)S(1)}, f32[18,64]{1,0:T(8,128)S(1)}, s32[384]{0:T(512)S(1)}, s32[18,64]{1,0:T(8,128)S(1)}, /*index=5*/f32[3,...) while((s32[]{:T(128)}, f32[3,384]{1,0:T(4,128)S(1)}, ...), condition=%wide.region_4.4_spmd.clone, body=%wide.region_1.3_spmd.clone.sunk | while | flops 935107 | bytes 431367 | solution.py:77
  83.7 9.5 %while.92 = (s32[]{:T(128)}, f32[3,384]{1,0:T(4,128)S(1)}, f32[18,64]{1,0:T(8,128)S(1)}, s32[384]{0:T(512)S(1)}, s32[18,64]{1,0:T(8,128)S(1)}, /*index=5*/f32[3,...) while((s32[]{:T(128)}, f32[3,384]{1,0:T(4,128)S(1)}, ...), condition=%wide.region_4.4_spmd.clone, body=%wide.region_1.3_spmd.clone.sunk | while | flops 935107 | bytes 431367 | solution.py:77
  93.7 9.5 %while.92 = (s32[]{:T(128)}, f32[3,384]{1,0:T(4,128)S(1)}, f32[18,64]{1,0:T(8,128)S(1)}, s32[384]{0:T(512)S(1)}, s32[18,64]{1,0:T(8,128)S(1)}, /*index=5*/f32[3,...) while((s32[]{:T(128)}, f32[3,384]{1,0:T(4,128)S(1)}, ...), condition=%wide.region_4.4_spmd.clone, body=%wide.region_1.3_spmd.clone.sunk | while | flops 935107 | bytes 431367 | solution.py:77
  103.6 9.5 %while.92 = (s32[]{:T(128)}, f32[3,384]{1,0:T(4,128)S(1)}, f32[18,64]{1,0:T(8,128)S(1)}, s32[384]{0:T(512)S(1)}, s32[18,64]{1,0:T(8,128)S(1)}, /*index=5*/f32[3,...) while((s32[]{:T(128)}, f32[3,384]{1,0:T(4,128)S(1)}, ...), condition=%wide.region_4.4_spmd.clone, body=%wide.region_1.3_spmd.clone.sunk | while | flops 935107 | bytes 431367 | solution.py:77
  113.6 9.5 %while.92 = (s32[]{:T(128)}, f32[3,384]{1,0:T(4,128)S(1)}, f32[18,64]{1,0:T(8,128)S(1)}, s32[384]{0:T(512)S(1)}, s32[18,64]{1,0:T(8,128)S(1)}, /*index=5*/f32[3,...) while((s32[]{:T(128)}, f32[3,384]{1,0:T(4,128)S(1)}, ...), condition=%wide.region_4.4_spmd.clone, body=%wide.region_1.3_spmd.clone.sunk | while | flops 935107 | bytes 431367 | solution.py:77
  123.6 9.5 %while.92 = (s32[]{:T(128)}, f32[3,384]{1,0:T(4,128)S(1)}, f32[18,64]{1,0:T(8,128)S(1)}, s32[384]{0:T(512)S(1)}, s32[18,64]{1,0:T(8,128)S(1)}, /*index=5*/f32[3,...) while((s32[]{:T(128)}, f32[3,384]{1,0:T(4,128)S(1)}, ...), condition=%wide.region_4.4_spmd.clone, body=%wide.region_1.3_spmd.clone.sunk | while | flops 935107 | bytes 431367 | solution.py:77
  133.5 9.5 %while.92 = (s32[]{:T(128)}, f32[3,384]{1,0:T(4,128)S(1)}, f32[18,64]{1,0:T(8,128)S(1)}, s32[384]{0:T(512)S(1)}, s32[18,64]{1,0:T(8,128)S(1)}, /*index=5*/f32[3,...) while((s32[]{:T(128)}, f32[3,384]{1,0:T(4,128)S(1)}, ...), condition=%wide.region_4.4_spmd.clone, body=%wide.region_1.3_spmd.clone.sunk | while | flops 935107 | bytes 431367 | solution.py:77
  143.5 9.5 %while.92 = (s32[]{:T(128)}, f32[3,384]{1,0:T(4,128)S(1)}, f32[18,64]{1,0:T(8,128)S(1)}, s32[384]{0:T(512)S(1)}, s32[18,64]{1,0:T(8,128)S(1)}, /*index=5*/f32[3,...) while((s32[]{:T(128)}, f32[3,384]{1,0:T(4,128)S(1)}, ...), condition=%wide.region_4.4_spmd.clone, body=%wide.region_1.3_spmd.clone.sunk | while | flops 935107 | bytes 431367 | solution.py:77
  153.5 9.5 %while.92 = (s32[]{:T(128)}, f32[3,384]{1,0:T(4,128)S(1)}, f32[18,64]{1,0:T(8,128)S(1)}, s32[384]{0:T(512)S(1)}, s32[18,64]{1,0:T(8,128)S(1)}, /*index=5*/f32[3,...) while((s32[]{:T(128)}, f32[3,384]{1,0:T(4,128)S(1)}, ...), condition=%wide.region_4.4_spmd.clone, body=%wide.region_1.3_spmd.clone.sunk | while | flops 935107 | bytes 431367 | solution.py:77
  163.5 9.5 %while.92 = (s32[]{:T(128)}, f32[3,384]{1,0:T(4,128)S(1)}, f32[18,64]{1,0:T(8,128)S(1)}, s32[384]{0:T(512)S(1)}, s32[18,64]{1,0:T(8,128)S(1)}, /*index=5*/f32[3,...) while((s32[]{:T(128)}, f32[3,384]{1,0:T(4,128)S(1)}, ...), condition=%wide.region_4.4_spmd.clone, body=%wide.region_1.3_spmd.clone.sunk | while | flops 935107 | bytes 431367 | solution.py:77
  173.4 6.4 %psum.7 = f32[4,6,384]{2,0,1:T(4,128)S(1)} all-reduce(f32[4,6,384]{2,0,1:T(4,128)S(1)} %fusion.28), channel_id=1, replica_groups=mesh['bead'=2,'space'=16] {'bead'}, use_global_device_ids=true, to_apply=%region_6.7 | all-reduce | flops 9216 | bytes 73728 | tf_op jit(solution)/shard_map/psum | solution.py:119
  179.9 3.9 %collective-permute-start.4 = (f32[12,384]{1,0:T(8,128)S(1)}, f32[12,384]{1,0:T(8,128)S(1)}, u32[]{:S(2)}, u32[]{:S(2)}) collective-permute-start(f32[12,384]{1,0:T(8,128)S(1)} %reshape.754), channel_id=1, source_target_pairs={{0,1},{1,2},{2,3},{3,4},{4,5},{5,6},{6,7},{7,8},{8,9},{9,10},{10,1... | collective-permute-start | bytes 55304 | tf_op jit(solution)/shard_map/ppermute | solution.py:19
  183.8 1.9 collective-permute-start.5
  185.8 4.5 %collective-permute-start.2 = (f32[12,384]{1,0:T(8,128)S(1)}, f32[12,384]{1,0:T(8,128)S(1)}, u32[]{:S(2)}, u32[]{:S(2)}) collective-permute-start(f32[12,384]{1,0:T(8,128)S(1)} %reshape.753), channel_id=1, source_target_pairs={{0,1},{1,2},{2,3},{3,4},{4,5},{5,6},{6,7},{7,8},{8,9},{9,10},{10,1... | collective-permute-start | bytes 55304 | tf_op jit(solution)/shard_map/ppermute | solution.py:19
  190.3 1.9 collective-permute-start.3
  192.4 4.0 %collective-permute-done.3 = f32[12,384]{1,0:T(8,128)S(1)} collective-permute-done((f32[12,384]{1,0:T(8,128)S(1)}, f32[12,384]{1,0:T(8,128)S(1)}, u32[]{:S(2)}, u32[]{:S(2)}) %collective-permute-start.3) | collective-permute-done | bytes 18464 | tf_op jit(solution)/shard_map/ppermute | solution.py:22
  196.5 45.7 %while.87 = (s32[]{:T(128)}, f32[4,3,384]{2,0,1:T(4,128)S(1)}, f32[4,3,1152]{2,1,0:T(4,128)S(1)}, f32[1,1152]{1,0:T(1,128)S(1)}, f32[4,3,1152]{2,0,1:T(4,128)S(1...) while((s32[]{:T(128)}, f32[4,3,384]{2,0,1:T(4,128)S(1)}, ...), condition=%wide.region_13.14_spmd, body=%wide.region_7.13_spmd.sunk | while | flops 1402053 | bytes 1022208 | solution.py:130
  196.9 10.9 %while.93 = (s32[]{:T(128)}, f32[3,384]{1,0:T(4,128)S(1)}, f32[18,64]{1,0:T(8,128)S(1)}, s32[384]{0:T(512)S(1)}, s32[18,64]{1,0:T(8,128)S(1)}, /*index=5*/f32[3,...) while((s32[]{:T(128)}, f32[3,384]{1,0:T(4,128)S(1)}, ...), condition=%wide.region_12.12_spmd.clone, body=%wide.region_8.11_spmd.clone.sunk | while | flops 1402051 | bytes 828423 | solution.py:77
  208.3 10.9 %while.93 = (s32[]{:T(128)}, f32[3,384]{1,0:T(4,128)S(1)}, f32[18,64]{1,0:T(8,128)S(1)}, s32[384]{0:T(512)S(1)}, s32[18,64]{1,0:T(8,128)S(1)}, /*index=5*/f32[3,...) while((s32[]{:T(128)}, f32[3,384]{1,0:T(4,128)S(1)}, ...), condition=%wide.region_12.12_spmd.clone, body=%wide.region_8.11_spmd.clone.sunk | while | flops 1402051 | bytes 828423 | solution.py:77
  219.7 10.9 %while.93 = (s32[]{:T(128)}, f32[3,384]{1,0:T(4,128)S(1)}, f32[18,64]{1,0:T(8,128)S(1)}, s32[384]{0:T(512)S(1)}, s32[18,64]{1,0:T(8,128)S(1)}, /*index=5*/f32[3,...) while((s32[]{:T(128)}, f32[3,384]{1,0:T(4,128)S(1)}, ...), condition=%wide.region_12.12_spmd.clone, body=%wide.region_8.11_spmd.clone.sunk | while | flops 1402051 | bytes 828423 | solution.py:77
  231.2 10.9 %while.93 = (s32[]{:T(128)}, f32[3,384]{1,0:T(4,128)S(1)}, f32[18,64]{1,0:T(8,128)S(1)}, s32[384]{0:T(512)S(1)}, s32[18,64]{1,0:T(8,128)S(1)}, /*index=5*/f32[3,...) while((s32[]{:T(128)}, f32[3,384]{1,0:T(4,128)S(1)}, ...), condition=%wide.region_12.12_spmd.clone, body=%wide.region_8.11_spmd.clone.sunk | while | flops 1402051 | bytes 828423 | solution.py:77
  242.3 1.9 collective-permute-start.6
  244.2 2.4 collective-permute-start.7
  246.6 3.6 %collective-permute-done.7 = f32[12,384]{1,0:T(8,128)S(1)} collective-permute-done((f32[12,384]{1,0:T(8,128)S(1)}, f32[12,384]{1,0:T(8,128)S(1)}, u32[]{:S(2)}, u32[]{:S(2)}) %collective-permute-start.7) | collective-permute-done | bytes 18464 | tf_op jit(solution)/shard_map/ppermute | solution.py:22
  250.3 45.7 %while.89 = (s32[]{:T(128)}, f32[4,3,384]{2,0,1:T(4,128)S(1)}, f32[4,3,1152]{2,1,0:T(4,128)S(1)}, f32[1,1152]{1,0:T(1,128)S(1)}, f32[4,3,1152]{2,0,1:T(4,128)S(1...) while((s32[]{:T(128)}, f32[4,3,384]{2,0,1:T(4,128)S(1)}, ...), condition=%wide.region_20.21_spmd, body=%wide.region_14.20_spmd.sunk | while | flops 1402053 | bytes 1022208 | solution.py:130
  250.7 10.9 %while.94 = (s32[]{:T(128)}, f32[3,384]{1,0:T(4,128)S(1)}, f32[18,64]{1,0:T(8,128)S(1)}, s32[384]{0:T(512)S(1)}, s32[18,64]{1,0:T(8,128)S(1)}, /*index=5*/f32[3,...) while((s32[]{:T(128)}, f32[3,384]{1,0:T(4,128)S(1)}, ...), condition=%wide.region_19.19_spmd.clone, body=%wide.region_15.18_spmd.clone.sunk | while | flops 1402051 | bytes 828423 | solution.py:77
  262.1 10.9 %while.94 = (s32[]{:T(128)}, f32[3,384]{1,0:T(4,128)S(1)}, f32[18,64]{1,0:T(8,128)S(1)}, s32[384]{0:T(512)S(1)}, s32[18,64]{1,0:T(8,128)S(1)}, /*index=5*/f32[3,...) while((s32[]{:T(128)}, f32[3,384]{1,0:T(4,128)S(1)}, ...), condition=%wide.region_19.19_spmd.clone, body=%wide.region_15.18_spmd.clone.sunk | while | flops 1402051 | bytes 828423 | solution.py:77
  273.5 10.9 %while.94 = (s32[]{:T(128)}, f32[3,384]{1,0:T(4,128)S(1)}, f32[18,64]{1,0:T(8,128)S(1)}, s32[384]{0:T(512)S(1)}, s32[18,64]{1,0:T(8,128)S(1)}, /*index=5*/f32[3,...) while((s32[]{:T(128)}, f32[3,384]{1,0:T(4,128)S(1)}, ...), condition=%wide.region_19.19_spmd.clone, body=%wide.region_15.18_spmd.clone.sunk | while | flops 1402051 | bytes 828423 | solution.py:77
  285.0 10.9 %while.94 = (s32[]{:T(128)}, f32[3,384]{1,0:T(4,128)S(1)}, f32[18,64]{1,0:T(8,128)S(1)}, s32[384]{0:T(512)S(1)}, s32[18,64]{1,0:T(8,128)S(1)}, /*index=5*/f32[3,...) while((s32[]{:T(128)}, f32[3,384]{1,0:T(4,128)S(1)}, ...), condition=%wide.region_19.19_spmd.clone, body=%wide.region_15.18_spmd.clone.sunk | while | flops 1402051 | bytes 828423 | solution.py:77
  296.1 1.9 collective-permute-start.8
  298.0 2.4 collective-permute-start.9
  300.5 3.6 %collective-permute-done.9 = f32[12,384]{1,0:T(8,128)S(1)} collective-permute-done((f32[12,384]{1,0:T(8,128)S(1)}, f32[12,384]{1,0:T(8,128)S(1)}, u32[]{:S(2)}, u32[]{:S(2)}) %collective-permute-start.9) | collective-permute-done | bytes 18464 | tf_op jit(solution)/shard_map/ppermute | solution.py:22
  304.1 45.7 %while.91 = (s32[]{:T(128)}, f32[4,3,384]{2,0,1:T(4,128)S(1)}, f32[4,3,1152]{2,1,0:T(4,128)S(1)}, f32[1,1152]{1,0:T(1,128)S(1)}, f32[4,3,1152]{2,0,1:T(4,128)S(1...) while((s32[]{:T(128)}, f32[4,3,384]{2,0,1:T(4,128)S(1)}, ...), condition=%wide.region_27.28_spmd, body=%wide.region_21.27_spmd.sunk | while | flops 1402053 | bytes 1022208 | solution.py:130
  304.5 10.9 %while.95 = (s32[]{:T(128)}, f32[3,384]{1,0:T(4,128)S(1)}, f32[18,64]{1,0:T(8,128)S(1)}, s32[384]{0:T(512)S(1)}, s32[18,64]{1,0:T(8,128)S(1)}, /*index=5*/f32[3,...) while((s32[]{:T(128)}, f32[3,384]{1,0:T(4,128)S(1)}, ...), condition=%wide.region_26.26_spmd.clone, body=%wide.region_22.25_spmd.clone.sunk | while | flops 1402051 | bytes 828423 | solution.py:77
  316.0 10.9 %while.95 = (s32[]{:T(128)}, f32[3,384]{1,0:T(4,128)S(1)}, f32[18,64]{1,0:T(8,128)S(1)}, s32[384]{0:T(512)S(1)}, s32[18,64]{1,0:T(8,128)S(1)}, /*index=5*/f32[3,...) while((s32[]{:T(128)}, f32[3,384]{1,0:T(4,128)S(1)}, ...), condition=%wide.region_26.26_spmd.clone, body=%wide.region_22.25_spmd.clone.sunk | while | flops 1402051 | bytes 828423 | solution.py:77
  327.4 10.9 %while.95 = (s32[]{:T(128)}, f32[3,384]{1,0:T(4,128)S(1)}, f32[18,64]{1,0:T(8,128)S(1)}, s32[384]{0:T(512)S(1)}, s32[18,64]{1,0:T(8,128)S(1)}, /*index=5*/f32[3,...) while((s32[]{:T(128)}, f32[3,384]{1,0:T(4,128)S(1)}, ...), condition=%wide.region_26.26_spmd.clone, body=%wide.region_22.25_spmd.clone.sunk | while | flops 1402051 | bytes 828423 | solution.py:77
  338.8 10.9 %while.95 = (s32[]{:T(128)}, f32[3,384]{1,0:T(4,128)S(1)}, f32[18,64]{1,0:T(8,128)S(1)}, s32[384]{0:T(512)S(1)}, s32[18,64]{1,0:T(8,128)S(1)}, /*index=5*/f32[3,...) while((s32[]{:T(128)}, f32[3,384]{1,0:T(4,128)S(1)}, ...), condition=%wide.region_26.26_spmd.clone, body=%wide.region_22.25_spmd.clone.sunk | while | flops 1402051 | bytes 828423 | solution.py:77
  349.9 1.0 convolution_add_fusion
  (5138 shorter events, 258.8 us)
Async XLA Ops:
  1.6 0.7 copy-start.4
  2.2 0.7 copy-start
  2.9 6.4 %collective-permute-start = (f32[50,384]{1,0:T(8,128)S(1)}, f32[50,384]{1,0:T(8,128)S(1)}, u32[]{:S(2)}, u32[]{:S(2)}) collective-permute-start(f32[50,384]{1,0:T(8,128)S(1)} %pad_maximum_fusion.1), channel_id=1, source_target_pairs={{0,1},{1,2},{2,3},{3,4},{4,5},{5,6},{6,7},{7,8},{8,9},{9,10},{10,1... | collective-permute-start | bytes 230408 | tf_op jit(solution)/shard_map/ppermute | solution.py:19
  6.7 6.7 %collective-permute-start.1 = (f32[50,384]{1,0:T(8,128)S(1)}, f32[50,384]{1,0:T(8,128)S(1)}, u32[]{:S(2)}, u32[]{:S(2)}) collective-permute-start(f32[50,384]{1,0:T(8,128)S(1)} %pad_maximum_fusion.1), channel_id=1, source_target_pairs={{1,0},{2,1},{3,2},{4,3},{5,4},{6,5},{7,6},{8,7},{9,8},{10,9},{11,1... | collective-permute-start | bytes 230408 | tf_op jit(solution)/shard_map/ppermute | solution.py:22
  8.6 0.7 copy-start.1
  13.5 159.5 %copy-start.2 = (f32[16,3,384]{2,0,1:T(8,128)S(1)}, f32[16,3,384]{2,0,1:T(8,128)}, u32[]{:S(2)}) copy-start(f32[16,3,384]{2,0,1:T(8,128)} %param.20) | copy-start | bytes 221188
  179.9 12.4 %collective-permute-start.4 = (f32[12,384]{1,0:T(8,128)S(1)}, f32[12,384]{1,0:T(8,128)S(1)}, u32[]{:S(2)}, u32[]{:S(2)}) collective-permute-start(f32[12,384]{1,0:T(8,128)S(1)} %reshape.754), channel_id=1, source_target_pairs={{0,1},{1,2},{2,3},{3,4},{4,5},{5,6},{6,7},{7,8},{8,9},{9,10},{10,1... | collective-permute-start | bytes 55304 | tf_op jit(solution)/shard_map/ppermute | solution.py:19
  183.8 8.5 %collective-permute-start.5 = (f32[12,384]{1,0:T(8,128)S(1)}, f32[12,384]{1,0:T(8,128)S(1)}, u32[]{:S(2)}, u32[]{:S(2)}) collective-permute-start(f32[12,384]{1,0:T(8,128)S(1)} %reshape.754), channel_id=1, source_target_pairs={{1,0},{2,1},{3,2},{4,3},{5,4},{6,5},{7,6},{8,7},{9,8},{10,9},{11,1... | collective-permute-start | bytes 55304 | tf_op jit(solution)/shard_map/ppermute | solution.py:22
  185.8 6.6 %collective-permute-start.2 = (f32[12,384]{1,0:T(8,128)S(1)}, f32[12,384]{1,0:T(8,128)S(1)}, u32[]{:S(2)}, u32[]{:S(2)}) collective-permute-start(f32[12,384]{1,0:T(8,128)S(1)} %reshape.753), channel_id=1, source_target_pairs={{0,1},{1,2},{2,3},{3,4},{4,5},{5,6},{6,7},{7,8},{8,9},{9,10},{10,1... | collective-permute-start | bytes 55304 | tf_op jit(solution)/shard_map/ppermute | solution.py:19
  190.3 6.0 %collective-permute-start.3 = (f32[12,384]{1,0:T(8,128)S(1)}, f32[12,384]{1,0:T(8,128)S(1)}, u32[]{:S(2)}, u32[]{:S(2)}) collective-permute-start(f32[12,384]{1,0:T(8,128)S(1)} %reshape.753), channel_id=1, source_target_pairs={{1,0},{2,1},{3,2},{4,3},{5,4},{6,5},{7,6},{8,7},{9,8},{10,9},{11,1... | collective-permute-start | bytes 55304 | tf_op jit(solution)/shard_map/ppermute | solution.py:22
  242.3 4.3 %collective-permute-start.6 = (f32[12,384]{1,0:T(8,128)S(1)}, f32[12,384]{1,0:T(8,128)S(1)}, u32[]{:S(2)}, u32[]{:S(2)}) collective-permute-start(f32[12,384]{1,0:T(8,128)S(1)} %reshape.755), channel_id=1, source_target_pairs={{0,1},{1,2},{2,3},{3,4},{4,5},{5,6},{6,7},{7,8},{8,9},{9,10},{10,1... | collective-permute-start | bytes 55304 | tf_op jit(solution)/shard_map/ppermute | solution.py:19
  244.2 6.0 %collective-permute-start.7 = (f32[12,384]{1,0:T(8,128)S(1)}, f32[12,384]{1,0:T(8,128)S(1)}, u32[]{:S(2)}, u32[]{:S(2)}) collective-permute-start(f32[12,384]{1,0:T(8,128)S(1)} %reshape.755), channel_id=1, source_target_pairs={{1,0},{2,1},{3,2},{4,3},{5,4},{6,5},{7,6},{8,7},{9,8},{10,9},{11,1... | collective-permute-start | bytes 55304 | tf_op jit(solution)/shard_map/ppermute | solution.py:22
  296.0 8.1 %copy-start.3 = (f32[4,3,384]{2,0,1:T(4,128)}, f32[4,3,384]{2,0,1:T(4,128)S(1)}, u32[]{:S(2)}) copy-start(f32[4,3,384]{2,0,1:T(4,128)S(1)} %add_multiply_fusion) | copy-start | bytes 55300
  296.1 4.3 %collective-permute-start.8 = (f32[12,384]{1,0:T(8,128)S(1)}, f32[12,384]{1,0:T(8,128)S(1)}, u32[]{:S(2)}, u32[]{:S(2)}) collective-permute-start(f32[12,384]{1,0:T(8,128)S(1)} %reshape.756), channel_id=1, source_target_pairs={{0,1},{1,2},{2,3},{3,4},{4,5},{5,6},{6,7},{7,8},{8,9},{9,10},{10,1... | collective-permute-start | bytes 55304 | tf_op jit(solution)/shard_map/ppermute | solution.py:19
  298.0 6.0 %collective-permute-start.9 = (f32[12,384]{1,0:T(8,128)S(1)}, f32[12,384]{1,0:T(8,128)S(1)}, u32[]{:S(2)}, u32[]{:S(2)}) collective-permute-start(f32[12,384]{1,0:T(8,128)S(1)} %reshape.756), channel_id=1, source_target_pairs={{1,0},{2,1},{3,2},{4,3},{5,4},{6,5},{7,6},{8,7},{9,8},{10,9},{11,1... | collective-permute-start | bytes 55304 | tf_op jit(solution)/shard_map/ppermute | solution.py:22
where the time goes:
time: 351 us
  other arithmetic  224 us (64%)
  loops' own time  41.7 us (12%)
  local copies, waits for them, and re-layouts  34.1 us (10%)
  starting transfers between devices  26.6 us (8%)
  waiting for transfers between devices  15.2 us (4%)
  blocking collectives  6.43 us (2%)
    reduce_sum x504, other arithmetic, step(): return (total + jnp.sum(term, axis=2), None)  62.9 us
    mul x288, other arithmetic, step(): term = (taper * damp3 * inv3 * charge[None, :])[None] * diff  50.3 us
    mul x216, other arithmetic, step(): 3.0 * taper * damp5 * inv3 * inverse * inverse * along  42.9 us
    another operation x28, loops' own time, pair_field(): total, unused = lax.scan(step, start, blocks)  40.1 us
    reduce_sum x288, other arithmetic, step(): dist2 = jnp.sum(diff * diff, axis=0)  27.6 us
    reduce_sum x216, other arithmetic, step(): along = jnp.sum(diff * dip[:, None, :], axis=0)  25.6 us
    dynamic_slice x2232, local copies, waits for them, and re-layouts, pair_field(): total, unused = lax.scan(step, start, blocks)  19.6 us
    ppermute x5, starting transfers between devices, padded(): lax.ppermute(lax.slice_in_dim(block, block.shape[dim] - width, None, axis...  16 us

commit v1 on v0

v1 whole, which is shorter than its diff:
```python
import functools
import math

import jax
import jax.numpy as jnp
import numpy as np
from jax import lax
from jax.experimental import pallas as pl
from jax.experimental.pallas import tpu as pltpu
from jax.sharding import PartitionSpec as P

BEADS = 32
CONTR = 4
ITERS = 2
CUTOFF = 9.0
CUT2 = CUTOFF * CUTOFF
THOLE = 0.39
LOG2E = 1.4426950408889634
LN2 = 0.6931471805599453
L = 128
KP = 8
F32 = jnp.float32
BF16 = jnp.bfloat16
VMEM_LIMIT = 40 * 1024 * 1024


def split3(x):
    h = x.astype(BF16).astype(F32)
    r = x - h
    m = r.astype(BF16).astype(F32)
    return h, m, r - m


def dot(a, b, ca=1, cb=0):
    return lax.dot_general(a, b, (((ca,), (cb,)), ((), ())), preferred_element_type=F32)


def dot3(x, mat, cb):
    rows = x.shape[0]
    out = dot(jnp.concatenate(split3(x), 0).astype(BF16), mat, 1, cb)
    return (out[:rows] + out[rows : 2 * rows]) + out[2 * rows :]


T_SLOTS, S_SLOTS = [], []
for _a in range(3):
    T_SLOTS += [(_a, 1)] * 3 + [(3 + _a, 1)] * 2 + [(6 + _a, 1)]
    S_SLOTS += [(_a, -2), (3 + _a, -2), (6 + _a, -2), (_a, -2), (3 + _a, -2), (_a, -2)]
T_SLOTS += [(9, 1), (10, 1), (11, 1), (12, 1), (12, 1), (12, 1)]
S_SLOTS += [(12, 1), (12, 1), (12, 1), (9, 1), (10, 1), (11, 1)]
TYPES = 13


def sel_pair(rows, count):
    groups = (count + 3) // 4
    sel_t = np.zeros((count * L, TYPES * rows), np.float32)
    sel_s = np.zeros((TYPES * rows, groups * L), np.float32)
    for b in range(count):
        for f in range(len(T_SLOTS)):
            kind, coef = T_SLOTS[f]
            sel_t[b * L + (b % 4) * 32 + f, kind * rows + b] = coef
            kind, coef = S_SLOTS[f]
            sel_s[kind * rows + b, (b // 4) * L + (b % 4) * 32 + f] = coef
    return jnp.asarray(sel_t, BF16), jnp.asarray(sel_s, BF16)


def sel_sum(rows, count):
    sel = np.zeros((count * 32, 12 * rows), np.float32)
    for b in range(count):
        for p in range(3):
            for f in range(4):
                sel[b * 32 + p * 8 + f, (p * 4 + f) * rows + b] = 1
    return jnp.asarray(sel, BF16)


def sel_induce():
    sel = np.zeros((CONTR * L, 48 * KP), np.float32)
    for k in range(CONTR):
        for p in range(3):
            for f in range(16):
                sel[k * L + p * 16 + f, (p * 16 + f) * KP + k] = 1
            for f in range(3):
                sel[k * L + 64 + p * 8 + f, (p * 16 + f) * KP + k] = 1
    return jnp.asarray(sel, BF16)


def perm_matrix(rank_row, w):
    rows = lax.broadcasted_iota(jnp.int32, (w, w), 0).astype(F32)
    return jnp.where(rows == rank_row, 1.0, 0.0).astype(BF16)


def pair_pieces(xs):
    hx, hy, hz = (split3(x) for x in xs)
    n = xs[0] * xs[0] + xs[1] * xs[1] + xs[2] * xs[2]
    parts = [hx[0], hy[0], hz[0], hx[1], hy[1], hz[1], hx[2], hy[2], hz[2]]
    parts += list(split3(n)) + [jnp.ones_like(n)]
    return jnp.concatenate(parts, 0).astype(BF16)


def center_of(xs, count):
    w = xs[0].shape[1]
    return [jnp.sum(x[:count], keepdims=True) * (1.0 / (count * w)) for x in xs]


def columns(misc):
    al = misc[1:2]
    good = al > 0.0
    inv = jnp.where(good, lax.rsqrt(jnp.where(good, al, 1.0)), 0.0)
    return jnp.concatenate([inv, misc[2:3], jnp.zeros_like(misc[:6])], 0)


def ranges(x, al, count, w):
    good = al > 0.0
    lo = jnp.where(good, x[:count], 1e30)
    hi = jnp.where(good, x[:count], -1e30)
    out = []
    for i in range(w // L):
        out.append((jnp.min(lo[:, i * L : (i + 1) * L]), jnp.max(hi[:, i * L : (i + 1) * L])))
    return out


def set_flags(flags, trange, sranges, nt):
    sj = 0
    for slab in sranges:
        for smin, smax in slab:
            for ti, (tmin, tmax) in enumerate(trange):
                near = (smin - tmax < CUTOFF) & (tmin - smax < CUTOFF)
                flags[sj * nt + ti] = near.astype(jnp.int32)
            sj += 1


def pair_basis(r2, q):
    safe = jnp.maximum(r2, 1e-4)
    inv = lax.rsqrt(safe)
    c = (safe * inv) * (safe * q)
    decay = jnp.exp2(c)
    v = jnp.maximum(CUT2 - r2, 0.0) * inv
    return c, decay, inv, v


def two(x):
    hi = x.astype(BF16)
    return hi, (x - hi.astype(F32)).astype(BF16)


def pack_kernel(nb, nbp, w, pos, charge, polar, mol, out, rank_out, scr):
    scr[...] = jnp.zeros_like(scr)
    for a in range(3):
        scr[a * nbp : a * nbp + nb, :] = pos[:, a, :]
    base = 3 * nbp
    scr[base : base + 1, :] = charge[...]
    scr[base + 1 : base + 2, :] = polar[...]
    scr[base + 2 : base + 3, :] = mol[...].astype(F32)
    x = scr[...]
    key = jnp.sum(x[:nbp], 0, keepdims=True)
    col = jnp.transpose(jnp.broadcast_to(key, (8, w)))[:, :1]
    jj = lax.broadcasted_iota(jnp.int32, (w, w), 0)
    ii = lax.broadcasted_iota(jnp.int32, (w, w), 1)
    before = (col < key) | ((col == key) & (jj < ii))
    rank = jnp.sum(jnp.where(before, 1.0, 0.0), 0, keepdims=True)
    rank_out[...] = jnp.broadcast_to(rank, (8, w))
    out[...] = dot3(x, perm_matrix(rank, w), 1)


def perm_kernel(nsrc, own, nb, nbp, w, *refs):
    tgt = refs[0]
    srcs = refs[1 : 1 + nsrc]
    refs = refs[1 + nsrc :]
    if own:
        sel_t, sel_s, sel_r, acc_out = refs[:4]
        refs = refs[4:]
    else:
        sel_t, sel_s, sel_r, acc_in, rank, contract, perm_out, msg_out = refs[:8]
        refs = refs[8:]
    ft, fs, rt, cols, acc, flags = refs
    nt = w // L
    base = 3 * nbp
    coords = [tgt[a * nbp : (a + 1) * nbp, :] for a in range(3)]
    center = center_of(coords, nb)
    xt = [x - c for x, c in zip(coords, center)]
    ft[...] = dot(sel_t[...], pair_pieces(xt)).astype(BF16)
    misc_t = columns(tgt[base : base + 8, :])
    trange = ranges(xt[0], tgt[base + 1 : base + 2, :], nb, w)
    sranges = []
    for s, src in enumerate(srcs):
        xs = [src[a * nbp : (a + 1) * nbp, :] - center[a] for a in range(3)]
        misc = src[base : base + 8, :]
        fs[s * w : (s + 1) * w, :] = dot(pair_pieces(xs), sel_s[...], 0, 0).astype(BF16)
        q = jnp.broadcast_to(misc[0:1] * (1.0 / (CUT2 * CUT2)), xs[0].shape)
        feats = [split3(v) for v in (xs[0] * q, xs[1] * q, xs[2] * q, q)]
        stack = jnp.concatenate([feats[f][p] for p in range(3) for f in range(4)], 0)
        rt[:, s * w : (s + 1) * w] = dot(sel_r[...], stack.astype(BF16)).astype(BF16)
        cols[s * w : (s + 1) * w, :] = jnp.transpose(columns(misc))
        sranges.append(ranges(xs[0], misc[1:2], nb, w))
    set_flags(flags, trange, sranges, nt)
    if own:
        acc[...] = jnp.zeros_like(acc)
    else:
        acc[...] = acc_in[...]
    qt_rows = misc_t * (-THOLE * LOG2E)
    mol_rows = misc_t[1:2]

    for ti in range(nt):
        t0 = ti * L
        qrow = qt_rows[0:1, t0 : t0 + L]
        mrow = mol_rows[:, t0 : t0 + L]

        def step(sj, carry):
            @pl.when(flags[sj * nt + ti] == 1)
            def _():
                s0 = pl.multiple_of(sj * L, L)
                cc = cols[pl.ds(s0, L), :]
                q = cc[:, 0:1] * qrow
                if own:
                    q = jnp.where(cc[:, 1:2] == mrow, 0.0, q)

                def group(g, c2):
                    g0 = pl.multiple_of(g * L, L)
                    lhs = fs[pl.ds(s0, L), pl.ds(g0, L)]
                    for i in range(4):
                        b = g * 4 + i
                        rhs = ft[pl.ds(pl.multiple_of(b * L, L), L), t0 : t0 + L]
                        c, decay, inv, v = pair_basis(dot(lhs, rhs), q)
                        f = (v * v) * (inv * (1.0 - decay))
                        pair = jnp.concatenate(two(f), 0)
                        r0 = pl.multiple_of(b * 32, 32)
                        r = rt[pl.ds(r0, 32), pl.ds(s0, L)]
                        acc[pl.ds(r0, 32), t0 : t0 + L] += dot(jnp.concatenate([r, r], 1), pair)
                    return c2

                lax.fori_loop(0, nb // 4, group, 0)

            return carry

        lax.fori_loop(0, nsrc * nt, step, 0)
    if own:
        acc_out[...] = acc[...]
        return
    for a in range(3):
        perm_out[a * nbp : (a + 1) * nbp, :] = jnp.zeros((nbp, w), F32)
    for b in range(nb):
        s = acc[b * 32 : b * 32 + 8, :] + acc[b * 32 + 8 : b * 32 + 16, :]
        s = s + acc[b * 32 + 16 : b * 32 + 24, :]
        for a in range(3):
            row = xt[a][b : b + 1] * s[3:4] - s[a : a + 1]
            perm_out[a * nbp + b : a * nbp + b + 1, :] = row
    wc = contract[lax.axis_index("bead")]
    parts = []
    for a in range(3):
        parts.append(
            jnp.dot(wc, perm_out[a * nbp : (a + 1) * nbp, :], precision=lax.Precision.HIGHEST, preferred_element_type=F32)
        )
    for a in range(3):
        parts.append(jnp.dot(wc, coords[a], precision=lax.Precision.HIGHEST, preferred_element_type=F32))
    msg_out[...] = dot3(jnp.concatenate(parts, 0), perm_matrix(rank[0:1, :], w), 0)


def start_kernel(nbp, w, msg, other, rank, pack, m0, cf):
    both = dot3(msg[...] + other[...], perm_matrix(rank[0:1, :], w), 1)
    n = 3 * KP
    cf[...] = both[:n]
    m0[:n, :] = both[:n] * pack[3 * nbp + 1 : 3 * nbp + 2, :]
    m0[n:, :] = both[n:]


def tensor_blocks(w, own, tgt_m, tgt_misc, srcs, sel_t, sel_s, tensors, flags, ft, fs, cols):
    nt = w // L
    n = 3 * KP
    coords = [tgt_m[n + a * KP : n + (a + 1) * KP, :] for a in range(3)]
    center = center_of(coords, CONTR)
    xt = [x - c for x, c in zip(coords, center)]
    ft[...] = dot(sel_t[...], pair_pieces(xt)).astype(BF16)
    misc_t = columns(tgt_misc)
    trange = ranges(xt[0], tgt_misc[1:2], CONTR, w)
    sranges = []
    for s, (sm, misc) in enumerate(srcs):
        xs = [sm[n + a * KP : n + (a + 1) * KP, :] - center[a] for a in range(3)]
        fs[s * w : (s + 1) * w, :] = dot(pair_pieces(xs), sel_s[...], 0, 0).astype(BF16)
        cols[s * w : (s + 1) * w, :] = jnp.transpose(columns(misc))
        sranges.append(ranges(xs[0], misc[1:2], CONTR, w))
    set_flags(flags, trange, sranges, nt)
    qt_rows = misc_t * (-THOLE * LOG2E)
    for ti in range(nt):
        t0 = ti * L
        qrow = qt_rows[0:1, t0 : t0 + L]
        mrow = misc_t[1:2, t0 : t0 + L]

        def step(sj, carry):
            blk = sj * nt + ti

            @pl.when(flags[blk] == 1)
            def _():
                s0 = pl.multiple_of(sj * L, L)
                cc = cols[pl.ds(s0, L), :]
                q = cc[:, 0:1] * qrow
                if own:
                    q = jnp.where(cc[:, 1:2] == mrow, 0.0, q)
                lhs = fs[pl.ds(s0, L), :]
                for k in range(CONTR):
                    c, decay, inv, v = pair_basis(dot(lhs, ft[k * L : (k + 1) * L, t0 : t0 + L]), q)
                    l3 = 1.0 - decay
                    l5 = l3 + (c * LN2) * decay
                    w3 = (v * v) * inv
                    w5 = w3 * (inv * inv)
                    a_hi, a_lo = two(w5 * l5)
                    b_hi, b_lo = two(w3 * l3)
                    tensors[k, blk, 0:L, :] = a_hi
                    tensors[k, blk, L : 2 * L, :] = a_lo
                    tensors[k, blk, 2 * L : 3 * L, :] = b_hi
                    tensors[k, blk, 3 * L : 4 * L, :] = b_lo

            return carry

        lax.fori_loop(0, len(srcs) * nt, step, 0)


def own_tensor_kernel(nbp, w, m0, pack, sel_t, sel_s, tensors, flags_out, ft, fs, cols):
    misc = pack[3 * nbp : 3 * nbp + 8, :]
    tensor_blocks(w, True, m0, misc, [(m0, misc)], sel_t, sel_s, tensors, flags_out, ft, fs, cols)


def induce_sums(w, mus, cps, sel_e, groups, le, acc_a, acc_b, ev):
    nt = w // L
    n = 3 * KP
    own = [cps[0][n + a * KP : n + (a + 1) * KP, :] for a in range(3)]
    center = center_of(own, CONTR)
    scale = 1.0 / (CUT2 * CUT2)
    for s, (mu, cp) in enumerate(zip(mus, cps)):
        m = [mu[a * KP : (a + 1) * KP, :] * scale for a in range(3)]
        x = [cp[n + a * KP : n + (a + 1) * KP, :] - center[a] for a in range(3)]
        dotted = x[0] * m[0] + x[1] * m[1] + x[2] * m[2]
        feats = m + [dotted] + [x[a] * m[b] for a in range(3) for b in range(3)]
        feats += [x[a] * dotted for a in range(3)]
        split = [split3(f) for f in feats]
        stack = jnp.concatenate([split[f][p] for p in range(3) for f in range(16)], 0)
        le[:, s * w : (s + 1) * w] = dot(sel_e[...], stack.astype(BF16)).astype(BF16)
    acc_a[...] = jnp.zeros_like(acc_a)
    acc_b[...] = jnp.zeros_like(acc_b)
    for first, nsrc, tensors, flags in groups:
        for ti in range(nt):
            t0 = ti * L

            def step(sj, carry):
                blk = sj * nt + ti

                @pl.when(flags[blk] == 1)
                def _():
                    s0 = pl.multiple_of((first * nt + sj) * L, L)
                    for k in range(CONTR):
                        fa = le[k * L : k * L + 48, pl.ds(s0, L)]
                        fb = le[k * L + 64 : k * L + 96, pl.ds(s0, L)]
                        acc_a[k * 48 : (k + 1) * 48, t0 : t0 + L] += dot(
                            jnp.concatenate([fa, fa], 1), tensors[k, blk, 0 : 2 * L, :]
                        )
                        acc_b[k * 32 : (k + 1) * 32, t0 : t0 + L] += dot(
                            jnp.concatenate([fb, fb], 1), tensors[k, blk, 2 * L : 4 * L, :]
                        )

                return carry

            lax.fori_loop(0, nsrc * nt, step, 0)
    ev[...] = jnp.zeros_like(ev)
    for k in range(CONTR):
        o = k * 48
        sa = acc_a[o : o + 16, :] + acc_a[o + 16 : o + 32, :] + acc_a[o + 32 : o + 48, :]
        o = k * 32
        sb = acc_b[o : o + 8, :] + acc_b[o + 8 : o + 16, :] + acc_b[o + 16 : o + 24, :]
        x = [own[a][k : k + 1] - center[a] for a in range(3)]
        mm = [sa[a : a + 1] for a in range(3)]
        along = x[0] * mm[0] + x[1] * mm[1] + x[2] * mm[2] - sa[3:4]
        for a in range(3):
            cross = sum(x[b] * sa[4 + 3 * a + b : 5 + 3 * a + b] for b in range(3))
            full = x[a] * along - cross + sa[13 + a : 14 + a]
            ev[a * KP + k : a * KP + k + 1, :] = 3.0 * full - sb[a : a + 1]


def update(pack, nbp, cf, ev):
    al = pack[3 * nbp + 1 : 3 * nbp + 2, :]
    return al * (cf[...] + ev[...])


def first_induce_kernel(
    nbp, w, m0, m0a, m0b, pack, packa, packb, cf, t_own, f_own, sel_t, sel_s, sel_e,
    mu_out, t_nbr, f_nbr, ft, fs, cols, le, acc_a, acc_b, ev,
):
    base = 3 * nbp
    tensor_blocks(
        w, False, m0, pack[base : base + 8, :],
        [(m0a, packa[base : base + 8, :]), (m0b, packb[base : base + 8, :])],
        sel_t, sel_s, t_nbr, f_nbr, ft, fs, cols,
    )
    m = [m0, m0a, m0b]
    induce_sums(w, m, m, sel_e, [(0, 1, t_own, f_own), (1, 2, t_nbr, f_nbr)], le, acc_a, acc_b, ev)
    mu_out[...] = update(pack, nbp, cf, ev)


def induce_kernel(
    nbp, w, mu, mua, mub, m0, m0a, m0b, pack, cf, t_own, f_own, t_nbr, f_nbr, sel_e,
    mu_out, le, acc_a, acc_b, ev,
):
    induce_sums(
        w, [mu, mua, mub], [m0, m0a, m0b], sel_e,
        [(0, 1, t_own, f_own), (1, 2, t_nbr, f_nbr)], le, acc_a, acc_b, ev,
    )
    mu_out[...] = update(pack, nbp, cf, ev)


def final_kernel(
    nb, nbp, w, mu, mua, mub, m0, m0a, m0b, perm, rank, t_own, f_own, t_nbr, f_nbr, sel_e, spread,
    total_out, dip_out, le, acc_a, acc_b, ev,
):
    induce_sums(
        w, [mu, mua, mub], [m0, m0a, m0b], sel_e,
        [(0, 1, t_own, f_own), (1, 2, t_nbr, f_nbr)], le, acc_a, acc_b, ev,
    )
    us = spread[lax.axis_index("bead")]
    parts = []
    for a in range(3):
        part = jnp.dot(us, ev[a * KP : (a + 1) * KP, :], precision=lax.Precision.HIGHEST, preferred_element_type=F32)
        parts.append(perm[a * nbp : (a + 1) * nbp, :] + part)
    parts.append(mu[...])
    out = dot3(jnp.concatenate(parts, 0), perm_matrix(rank[0:1, :], w), 0)
    for a in range(3):
        total_out[:, a, :] = out[a * nbp : a * nbp + nb]
        d0 = 3 * nbp + a * KP
        dip_out[:, a, :] = out[d0 : d0 + CONTR]


def swap_pairs(count, first):
    pairs = []
    for i in range(first, count - 1, 2):
        pairs += [(i, i + 1), (i + 1, i)]
    return pairs


def call(kernel, outs, name, scratch=(), smem_in=(), smem_out=(), nin=0):
    smem = pl.BlockSpec(memory_space=pltpu.SMEM)
    vmem = pl.BlockSpec(memory_space=pltpu.VMEM)
    return pl.pallas_call(
        kernel,
        out_shape=[jax.ShapeDtypeStruct(s, d) for s, d in outs],
        in_specs=[smem if i in smem_in else vmem for i in range(nin)],
        out_specs=[smem if i in smem_out else vmem for i in range(len(outs))],
        scratch_shapes=list(scratch),
        compiler_params=pltpu.CompilerParams(vmem_limit_bytes=VMEM_LIMIT),
        name=name,
    )


def body(positions, charges, polar, molecule):
    nb, _, w = positions.shape
    nbp = -(-nb // 16) * 16
    nt = w // L
    nbead = lax.axis_size("bead")
    nspace = lax.axis_size("space")
    rows = 3 * nbp + 8
    n = 3 * KP

    contract = np.zeros((nbead, KP, nbp), np.float32)
    spread = np.zeros((nbead, nbp, KP), np.float32)
    for r in range(nbead):
        for b in range(nb):
            for k in range(CONTR):
                theta = 2.0 * math.pi * (k / CONTR - (r * nb + b) / BEADS)
                series = 1.0 + 2.0 * math.cos(theta) + math.cos(2.0 * theta)
                contract[r, k, b] = series / BEADS
                spread[r, b, k] = series / CONTR
    contract = jnp.asarray(contract)
    spread = jnp.asarray(spread)
    sel_t, sel_s = sel_pair(nbp, nb)
    sel_r = sel_sum(nbp, nb)
    ksel_t, ksel_s = sel_pair(KP, CONTR)
    sel_e = sel_induce()

    def exchange(x):
        near = lax.ppermute(x, "space", swap_pairs(nspace, 0))
        far = lax.ppermute(x, "space", swap_pairs(nspace, 1))
        return near, far

    pack, rank = call(
        functools.partial(pack_kernel, nb, nbp, w), [((rows, w), F32), ((8, w), F32)], "pack",
        [pltpu.VMEM((rows, w), F32)], nin=4,
    )(positions, charges[None], polar[None], molecule[None])
    packa, packb = exchange(pack)

    groups = -(-nb // 4)

    def perm_scratch(nsrc):
        return [
            pltpu.VMEM((nb * L, w), BF16),
            pltpu.VMEM((nsrc * w, groups * L), BF16),
            pltpu.VMEM((nb * 32, nsrc * w), BF16),
            pltpu.VMEM((nsrc * w, 8), F32),
            pltpu.VMEM((nb * 32, w), F32),
            pltpu.SMEM((nsrc * nt * nt,), jnp.int32),
        ]

    (acc,) = call(
        functools.partial(perm_kernel, 1, True, nb, nbp, w), [((nb * 32, w), F32)], "perm_own",
        perm_scratch(1), nin=5,
    )(pack, pack, sel_t, sel_s, sel_r)
    perm, msg = call(
        functools.partial(perm_kernel, 2, False, nb, nbp, w), [((3 * nbp, w), F32), ((2 * n, w), F32)],
        "perm_near", perm_scratch(2), nin=9,
    )(pack, packa, packb, sel_t, sel_s, sel_r, acc, rank, contract)

    if nbead == 2:
        other = lax.ppermute(msg, "bead", [(0, 1), (1, 0)])
    else:
        other = lax.psum(msg, "bead") - msg
    m0, cf = call(
        functools.partial(start_kernel, nbp, w), [((2 * n, w), F32), ((n, w), F32)], "start", nin=4,
    )(msg, other, rank, pack)
    m0a, m0b = exchange(m0)

    def tensor_scratch(nsrc):
        return [
            pltpu.VMEM((CONTR * L, w), BF16),
            pltpu.VMEM((nsrc * w, L), BF16),
            pltpu.VMEM((nsrc * w, 8), F32),
        ]

    def tensor_shape(nsrc):
        return ((CONTR, nsrc * nt * nt, 4 * L, L), BF16)

    sum_scratch = [
        pltpu.VMEM((CONTR * L, 3 * w), BF16),
        pltpu.VMEM((CONTR * 48, w), F32),
        pltpu.VMEM((CONTR * 32, w), F32),
        pltpu.VMEM((n, w), F32),
    ]
    t_own, f_own = call(
        functools.partial(own_tensor_kernel, nbp, w), [tensor_shape(1), ((nt * nt,), jnp.int32)], "tensor_own",
        tensor_scratch(1), smem_out=(1,), nin=4,
    )(m0, pack, ksel_t, ksel_s)
    mu, t_nbr, f_nbr = call(
        functools.partial(first_induce_kernel, nbp, w),
        [((n, w), F32), tensor_shape(2), ((2 * nt * nt,), jnp.int32)], "induce_first",
        tensor_scratch(2) + sum_scratch, smem_in=(8,), smem_out=(2,), nin=12,
    )(m0, m0a, m0b, pack, packa, packb, cf, t_own, f_own, ksel_t, ksel_s, sel_e)
    for step in range(ITERS - 1):
        mua, mub = exchange(mu)
        (mu,) = call(
            functools.partial(induce_kernel, nbp, w), [((n, w), F32)], f"induce_{step + 1}",
            sum_scratch, smem_in=(9, 11), nin=13,
        )(mu, mua, mub, m0, m0a, m0b, pack, cf, t_own, f_own, t_nbr, f_nbr, sel_e)
    mua, mub = exchange(mu)
    total, dipoles = call(
        functools.partial(final_kernel, nb, nbp, w), [((nb, 3, w), F32), ((CONTR, 3, w), F32)], "final",
        sum_scratch, smem_in=(9, 11), nin=14,
    )(mu, mua, mub, m0, m0a, m0b, perm, rank, t_own, f_own, t_nbr, f_nbr, sel_e, spread)
    return (total, dipoles)


def solution(mesh):
    in_specs = (P("bead", None, "space"), P("space"), P("space"), P("space"))
    out_specs = (P("bead", None, "space"), P(None, None, "space"))
    return jax.shard_map(body, mesh=mesh, in_specs=in_specs, out_specs=out_specs, check_vma=False)
```

time: 351 us -> 104 us (0.30)
  other arithmetic: 224 us -> 0 us
  Pallas kernels: 0 us -> 63.1 us
  loops' own time: 41.7 us -> 0 us
  local copies, waits for them, and re-layouts: 34.1 us -> 14.7 us
  starting transfers between devices: 26.6 us -> 14.5 us
  blocking collectives: 6.43 us -> 0 us
  waiting for transfers between devices: 15.2 us -> 9.67 us
    reduce_sum x1008 -> x0, other arithmetic: 116 us -> none  [the longest x504 62.9 us: step(): return (total + jnp.sum(term, axis=2), None)]
    mul x507 -> x0, other arithmetic: 93.2 us -> none  [the longest x288 50.3 us: step(): term = (taper * damp3 * inv3 * charge[None, :])[None] * diff]
    pallas_call x0 -> x8, Pallas kernels: none -> 63.1 us  [the longest x1 16.9 us: body(): call(functools.partial(perm_kernel, 1, True, nb, nbp, w), [((nb * 32, w),...]
    another operation x32 -> x0, loops' own time: 41.7 us -> none  [the longest x28 40.1 us: pair_field(): total, unused = lax.scan(step, start, blocks)]
    dynamic_slice x2284 -> x0, local copies, waits for them, and re-layouts: 20.1 us -> none  [the longest x2232 19.6 us: pair_field(): total, unused = lax.scan(step, start, blocks)]
    ppermute x10 -> x9, starting transfers between devices: 26.6 us -> 14.5 us  [the longest x4 12.3 us: exchange(): far = lax.ppermute(x, 'space', swap_pairs(nspace, 1))]
    unnamed x11 -> x27, local copies, waits for them, and re-layouts: 2.91 us -> 11.4 us
    gt x504 -> x0, other arithmetic: 7.69 us -> none  [step(): alpha[None, :] > 0.0]
where the time goes in v1:
time: 104 us; the launch traced here: 103 us
  Pallas kernels  63.1 us (61%)
  local copies, waits for them, and re-layouts  14.7 us (14%)
  starting transfers between devices  14.5 us (14%)
  waiting for transfers between devices  9.67 us (9%)
    pallas_call x1, Pallas kernels, body(): call(functools.partial(perm_kernel, 1, True, nb, nbp, w), [((nb * 32, w),...  16.9 us
    pallas_call x1, Pallas kernels, body(): call(functools.partial(perm_kernel, 2, False, nb, nbp, w), [((3 * nbp, w)...  12.5 us
    ppermute x4, starting transfers between devices, exchange(): far = lax.ppermute(x, 'space', swap_pairs(nspace, 1))  12.3 us
    pallas_call x1, Pallas kernels, body(): call(functools.partial(first_induce_kernel, nbp, w), [((n, w), F32), tens...  11.5 us
    unnamed x27, local copies, waits for them, and re-layouts  11.4 us
    pallas_call x1, Pallas kernels, body(): call(functools.partial(final_kernel, nb, nbp, w), [((nb, 3, w), F32), ((C...  8.75 us
    pallas_call x1, Pallas kernels, body(): call(functools.partial(induce_kernel, nbp, w), [((n, w), F32)], f'induce_...  8.33 us
    ppermute x4, waiting for transfers between devices, exchange(): far = lax.ppermute(x, 'space', swap_pairs(nspace, 1))  7.66 us
  transfers between devices with their start and end apart: 9, of which 3 were waited for; matrix products, arithmetic and copies ran while one was open for 0% of the time, Pallas kernels for 21%

profile of v1, /device:TPU:21, one launch (start us, length us, event | category | flops | bytes accessed | tf_op | source)
XLA Modules:
  0.0 102.8 jit_solution(6473627543471895110)
XLA Ops:
  0.6 0.7 broadcast_in_dim.9.charge
  1.3 0.7 broadcast_in_dim.10.polar
  2.0 0.7 broadcast_in_dim.11.mol
  2.7 0.9 copy.14.pos
  3.6 0.6 pack.1
  4.2 3.7 %collective-permute-start.1 = (f32[56,384]{1,0:T(8,128)S(1)}, f32[56,384]{1,0:T(8,128)S(1)}, u32[]{:S(2)}, u32[]{:S(2)}) collective-permute-start(f32[56,384]{1,0:T(8,128)S(1)} %get-tuple-element.13.refs_0_.refs_1_.pack), channel_id=1, source_target_pairs={{1,2},{2,1},{3,4},{4,3},{5,6},{6,5},{7,8},{8,7},{9,10},{10,9},{11,... | collective-permute-start | bytes 258056 | tf_op jit(solution)/shard_map/ppermute | solution.py:476
  7.9 0.1 collective-permute-start
  8.0 0.0 copy-start
  8.0 1.2 %copy-done = bf16[2048,208]{1,0:T(8,128)(2,1)S(1)} copy-done((bf16[2048,208]{1,0:T(8,128)(2,1)S(1)}, bf16[2048,208]{1,0:T(8,128)(2,1)}, u32[]{:S(2)}) %copy-start) | copy-done | bytes 851992
  9.2 0.9 copy-done.4
  10.2 0.9 copy-done.6
  11.1 16.9 %perm_own.1.refs_6_ = f32[512,384]{1,0:T(8,128)S(1)} custom-call(f32[56,384]{1,0:T(8,128)S(1)} %get-tuple-element.13.refs_0_.refs_1_.pack, f32[56,384]{1,0:T(8,128)S(1)} %get-tuple-element.13.refs_0_.refs_1_.pack, bf16[2048,208]{1,0:T(8,128)(2,1)S(1)} %copy-done, bf16[208,512]{1,0:T(8,128)(2,1)S(1)} %copy-done.6, bf16[512,192]{1,0:T(8,128)(2,1)S(1)} %copy-done.4), custom_call_target="tpu_custom_call" | custom-call | tf_op jit(solution)/shard_map/perm_own/pallas_call | solution.py:497
  28.0 0.0 collective-permute-done.1.refs_2_.packb
  28.0 0.0 collective-permute-done.refs_1_.packa
  28.1 0.0 copy-start.1
  28.1 1.2 %copy-done.1 = bf16[2048,208]{1,0:T(8,128)(2,1)S(1)} copy-done((bf16[2048,208]{1,0:T(8,128)(2,1)S(1)}, bf16[2048,208]{1,0:T(8,128)(2,1)}, u32[]{:S(2)}) %copy-start.1) | copy-done | bytes 851992
  29.3 0.9 copy-done.5
  30.2 0.9 copy-done.7
  31.2 0.7 copy-done.12
  31.9 12.5 %perm_near.1 = (f32[48,384]{1,0:T(8,128)S(1)}, f32[48,384]{1,0:T(8,128)S(1)}) custom-call(f32[56,384]{1,0:T(8,128)S(1)} %get-tuple-element.13.refs_0_.refs_1_.pack, f32[56,384]{1,0:T(8,128)S(1)} %collective-permute-done.refs_1_.packa, f32[56,384]{1,0:T(8,128)S(1)} %collective-permute-done.1.refs_2_.packb, bf16[2048,208]{1,0:T(8,128)(2,1)S(1)} %copy-done.1, ...), custom_call_target="tpu_custom_call" | custom-call | tf_op jit(solution)/shard_map/perm_near/pallas_call | solution.py:501
  44.3 1.3 %collective-permute-start.2 = (f32[48,384]{1,0:T(8,128)S(1)}, f32[48,384]{1,0:T(8,128)S(1)}, u32[]{:S(2)}, u32[]{:S(2)}) collective-permute-start(f32[48,384]{1,0:T(8,128)S(1)} %get-tuple-element.15.msg), channel_id=1, source_target_pairs={{0,16},{16,0},{1,17},{17,1},{2,18},{18,2},{3,19},{19,3},{4,20},{20... | collective-permute-start | bytes 221192 | tf_op jit(solution)/shard_map/ppermute | solution.py:507
  45.6 2.0 %collective-permute-done.2.other = f32[48,384]{1,0:T(8,128)S(1)} collective-permute-done((f32[48,384]{1,0:T(8,128)S(1)}, f32[48,384]{1,0:T(8,128)S(1)}, u32[]{:S(2)}, u32[]{:S(2)}) %collective-permute-start.2) | collective-permute-done | bytes 73760 | tf_op jit(solution)/shard_map/ppermute | solution.py:507
  47.6 0.2 start.1
  47.9 4.7 %collective-permute-start.4 = (f32[48,384]{1,0:T(8,128)S(1)}, f32[48,384]{1,0:T(8,128)S(1)}, u32[]{:S(2)}, u32[]{:S(2)}) collective-permute-start(f32[48,384]{1,0:T(8,128)S(1)} %get-tuple-element.16.m0), channel_id=1, source_target_pairs={{1,2},{2,1},{3,4},{4,3},{5,6},{6,5},{7,8},{8,7},{9,10},{10,9},{11,... | collective-permute-start | bytes 221192 | tf_op jit(solution)/shard_map/ppermute | solution.py:476
  52.6 0.1 collective-permute-start.3
  52.6 0.0 copy-start.8
  52.6 0.9 copy-done.8
  53.5 0.7 copy-done.10
  54.3 4.3 %tensor_own.1 = (bf16[4,9,512,128]{3,2,1,0:T(8,128)(2,1)S(1)}, s32[9]{0:T(128)S(1)}) custom-call(f32[48,384]{1,0:T(8,128)S(1)} %get-tuple-element.16.m0, f32[56,384]{1,0:T(8,128)S(1)} %get-tuple-element.13.refs_0_.refs_1_.pack, bf16[512,104]{1,0:T(8,128)(2,1)S(1)} %copy-done.8, bf16[104,128]{1,0:T(8,128)(2,1)S(1)} %copy-done.10), custom_call_target="tpu_custom_call" | custom-call | tf_op jit(solution)/shard_map/tensor_own/pallas_call | solution.py:531
  58.6 0.0 collective-permute-done.4.m0b
  58.6 0.0 collective-permute-done.3.m0a
  58.6 0.0 copy-start.2
  58.6 1.0 copy-done.2
  59.6 0.9 copy-done.9
  60.5 11.5 %induce_first.1 = (f32[24,384]{1,0:T(8,128)S(1)}, bf16[4,18,512,128]{3,2,1,0:T(8,128)(2,1)}, s32[18]{0:T(128)S(1)}) custom-call(f32[48,384]{1,0:T(8,128)S(1)} %get-tuple-element.16.m0, f32[48,384]{1,0:T(8,128)S(1)} %collective-permute-done.3.m0a, f32[48,384]{1,0:T(8,128)S(1)} %collective-permute-done.4.m0b, ...), custom_call_target="tpu_custom_call" | custom-call | tf_op jit(solution)/shard_map/induce_first/pallas_call | solution.py:535
  72.1 1.9 %collective-permute-start.6 = (f32[24,384]{1,0:T(8,128)S(1)}, f32[24,384]{1,0:T(8,128)S(1)}, u32[]{:S(2)}, u32[]{:S(2)}) collective-permute-start(f32[24,384]{1,0:T(8,128)S(1)} %get-tuple-element.20.mu), channel_id=1, source_target_pairs={{1,2},{2,1},{3,4},{4,3},{5,6},{6,5},{7,8},{8,7},{9,10},{10,9},{11,... | collective-permute-start | bytes 110600 | tf_op jit(solution)/shard_map/ppermute | solution.py:476
  74.0 0.7 collective-permute-start.5
  74.7 3.6 %collective-permute-done.6.mub = f32[24,384]{1,0:T(8,128)S(1)} collective-permute-done((f32[24,384]{1,0:T(8,128)S(1)}, f32[24,384]{1,0:T(8,128)S(1)}, u32[]{:S(2)}, u32[]{:S(2)}) %collective-permute-start.6) | collective-permute-done | bytes 36896 | tf_op jit(solution)/shard_map/ppermute | solution.py:476
  78.3 0.0 collective-permute-done.5.mua
  78.3 0.0 copy-done.3
  78.3 8.3 %induce_1.1.mu = f32[24,384]{1,0:T(8,128)S(1)} custom-call(f32[24,384]{1,0:T(8,128)S(1)} %get-tuple-element.20.mu, f32[24,384]{1,0:T(8,128)S(1)} %collective-permute-done.5.mua, f32[24,384]{1,0:T(8,128)S(1)} %collective-permute-done.6.mub, f32[48,384]{1,0:T(8,128)S(1)} %get-tuple-element.16.m0, f32[48,384]{1,0:T(8,128)S(1)} %collective-permute-done.3.m0a, ...), custom_call_target="tpu_custom_call" | custom-call | tf_op jit(solution)/shard_map/induce_1/pallas_call | solution.py:542
  86.6 2.0 %collective-permute-start.8 = (f32[24,384]{1,0:T(8,128)S(1)}, f32[24,384]{1,0:T(8,128)S(1)}, u32[]{:S(2)}, u32[]{:S(2)}) collective-permute-start(f32[24,384]{1,0:T(8,128)S(1)} %induce_1.1.mu), channel_id=1, source_target_pairs={{1,2},{2,1},{3,4},{4,3},{5,6},{6,5},{7,8},{8,7},{9,10},{10,9},{11,... | collective-permute-start | bytes 110600 | tf_op jit(solution)/shard_map/ppermute | solution.py:476
  88.6 0.1 collective-permute-start.7
  88.7 4.1 %collective-permute-done.8.mub = f32[24,384]{1,0:T(8,128)S(1)} collective-permute-done((f32[24,384]{1,0:T(8,128)S(1)}, f32[24,384]{1,0:T(8,128)S(1)}, u32[]{:S(2)}, u32[]{:S(2)}) %collective-permute-start.8) | collective-permute-done | bytes 36896 | tf_op jit(solution)/shard_map/ppermute | solution.py:476
  92.8 0.0 collective-permute-done.7.mua
  92.8 8.7 %final.1 = (f32[16,3,384]{2,1,0:T(4,128)S(1)}, f32[4,3,384]{2,1,0:T(4,128)S(1)}) custom-call(f32[24,384]{1,0:T(8,128)S(1)} %induce_1.1.mu, f32[24,384]{1,0:T(8,128)S(1)} %collective-permute-done.7.mua, f32[24,384]{1,0:T(8,128)S(1)} %collective-permute-done.8.mub, f32[48,384]{1,0:T(8,128)S(1)} %get-tuple-element.16.m0, ...), custom_call_target="tpu_custom_call" | custom-call | tf_op jit(solution)/shard_map/final/pallas_call | solution.py:547
  101.5 0.6 copy.15
  102.2 0.6 copy.16
  (10 shorter events, 0.0 us)
Async XLA Ops:
  4.2 23.9 %collective-permute-start.1 = (f32[56,384]{1,0:T(8,128)S(1)}, f32[56,384]{1,0:T(8,128)S(1)}, u32[]{:S(2)}, u32[]{:S(2)}) collective-permute-start(f32[56,384]{1,0:T(8,128)S(1)} %get-tuple-element.13.refs_0_.refs_1_.pack), channel_id=1, source_target_pairs={{1,2},{2,1},{3,4},{4,3},{5,6},{6,5},{7,8},{8,7},{9,10},{10,9},{11,... | collective-permute-start | bytes 258056 | tf_op jit(solution)/shard_map/ppermute | solution.py:476
  7.9 20.1 %collective-permute-start = (f32[56,384]{1,0:T(8,128)S(1)}, f32[56,384]{1,0:T(8,128)S(1)}, u32[]{:S(2)}, u32[]{:S(2)}) collective-permute-start(f32[56,384]{1,0:T(8,128)S(1)} %get-tuple-element.13.refs_0_.refs_1_.pack), channel_id=1, source_target_pairs={{0,1},{1,0},{2,3},{3,2},{4,5},{5,4},{6,7},{7,6},{8,9},{9,8},{10,11... | collective-permute-start | bytes 258056 | tf_op jit(solution)/shard_map/ppermute | solution.py:475
  8.0 1.2 %copy-start = (bf16[2048,208]{1,0:T(8,128)(2,1)S(1)}, bf16[2048,208]{1,0:T(8,128)(2,1)}, u32[]{:S(2)}) copy-start(bf16[2048,208]{1,0:T(8,128)(2,1)} %constant.18.clone.refs_2_.refs_3_) | copy-start | bytes 2555908
  9.2 0.9 copy-start.4
  10.2 0.9 copy-start.6
  11.1 67.2 %copy-start.3 = (bf16[512,384]{1,0:T(8,128)(2,1)S(1)}, bf16[512,384]{1,0:T(8,128)(2,1)}, u32[]{:S(2)}) copy-start(bf16[512,384]{1,0:T(8,128)(2,1)} %constant.23.clone.sel_e) | copy-start | bytes 1179652
  28.1 1.2 %copy-start.1 = (bf16[2048,208]{1,0:T(8,128)(2,1)S(1)}, bf16[2048,208]{1,0:T(8,128)(2,1)}, u32[]{:S(2)}) copy-start(bf16[2048,208]{1,0:T(8,128)(2,1)} %constant.18.clone.refs_2_.refs_3_) | copy-start | bytes 2555908
  29.3 0.9 copy-start.5
  30.2 0.9 copy-start.7
  31.2 0.7 copy-start.12
  44.3 3.3 %collective-permute-start.2 = (f32[48,384]{1,0:T(8,128)S(1)}, f32[48,384]{1,0:T(8,128)S(1)}, u32[]{:S(2)}, u32[]{:S(2)}) collective-permute-start(f32[48,384]{1,0:T(8,128)S(1)} %get-tuple-element.15.msg), channel_id=1, source_target_pairs={{0,16},{16,0},{1,17},{17,1},{2,18},{18,2},{3,19},{19,3},{4,20},{20... | collective-permute-start | bytes 221192 | tf_op jit(solution)/shard_map/ppermute | solution.py:507
  47.9 10.7 %collective-permute-start.4 = (f32[48,384]{1,0:T(8,128)S(1)}, f32[48,384]{1,0:T(8,128)S(1)}, u32[]{:S(2)}, u32[]{:S(2)}) collective-permute-start(f32[48,384]{1,0:T(8,128)S(1)} %get-tuple-element.16.m0), channel_id=1, source_target_pairs={{1,2},{2,1},{3,4},{4,3},{5,6},{6,5},{7,8},{8,7},{9,10},{10,9},{11,... | collective-permute-start | bytes 221192 | tf_op jit(solution)/shard_map/ppermute | solution.py:476
  52.6 6.0 %collective-permute-start.3 = (f32[48,384]{1,0:T(8,128)S(1)}, f32[48,384]{1,0:T(8,128)S(1)}, u32[]{:S(2)}, u32[]{:S(2)}) collective-permute-start(f32[48,384]{1,0:T(8,128)S(1)} %get-tuple-element.16.m0), channel_id=1, source_target_pairs={{0,1},{1,0},{2,3},{3,2},{4,5},{5,4},{6,7},{7,6},{8,9},{9,8},{10,11... | collective-permute-start | bytes 221192 | tf_op jit(solution)/shard_map/ppermute | solution.py:475
  52.6 0.9 copy-start.8
  53.5 0.7 copy-start.10
  58.6 1.0 copy-start.2
  59.6 0.9 copy-start.9
  60.5 32.3 %copy-start.11 = (f32[2,16,8]{2,1,0:T(8,128)S(1)}, f32[2,16,8]{2,1,0:T(8,128)}, u32[]{:S(2)}) copy-start(f32[2,16,8]{2,1,0:T(8,128)} %constant.17.clone.spread) | copy-start | bytes 3076
  72.1 6.2 %collective-permute-start.6 = (f32[24,384]{1,0:T(8,128)S(1)}, f32[24,384]{1,0:T(8,128)S(1)}, u32[]{:S(2)}, u32[]{:S(2)}) collective-permute-start(f32[24,384]{1,0:T(8,128)S(1)} %get-tuple-element.20.mu), channel_id=1, source_target_pairs={{1,2},{2,1},{3,4},{4,3},{5,6},{6,5},{7,8},{8,7},{9,10},{10,9},{11,... | collective-permute-start | bytes 110600 | tf_op jit(solution)/shard_map/ppermute | solution.py:476
  74.0 4.3 %collective-permute-start.5 = (f32[24,384]{1,0:T(8,128)S(1)}, f32[24,384]{1,0:T(8,128)S(1)}, u32[]{:S(2)}, u32[]{:S(2)}) collective-permute-start(f32[24,384]{1,0:T(8,128)S(1)} %get-tuple-element.20.mu), channel_id=1, source_target_pairs={{0,1},{1,0},{2,3},{3,2},{4,5},{5,4},{6,7},{7,6},{8,9},{9,8},{10,11... | collective-permute-start | bytes 110600 | tf_op jit(solution)/shard_map/ppermute | solution.py:475
  86.6 6.2 %collective-permute-start.8 = (f32[24,384]{1,0:T(8,128)S(1)}, f32[24,384]{1,0:T(8,128)S(1)}, u32[]{:S(2)}, u32[]{:S(2)}) collective-permute-start(f32[24,384]{1,0:T(8,128)S(1)} %induce_1.1.mu), channel_id=1, source_target_pairs={{1,2},{2,1},{3,4},{4,3},{5,6},{6,5},{7,8},{8,7},{9,10},{10,9},{11,... | collective-permute-start | bytes 110600 | tf_op jit(solution)/shard_map/ppermute | solution.py:476
  88.6 4.2 %collective-permute-start.7 = (f32[24,384]{1,0:T(8,128)S(1)}, f32[24,384]{1,0:T(8,128)S(1)}, u32[]{:S(2)}, u32[]{:S(2)}) collective-permute-start(f32[24,384]{1,0:T(8,128)S(1)} %induce_1.1.mu), channel_id=1, source_target_pairs={{0,1},{1,0},{2,3},{3,2},{4,5},{5,4},{6,7},{7,6},{8,9},{9,8},{10,11... | collective-permute-start | bytes 110600 | tf_op jit(solution)/shard_map/ppermute | solution.py:475

commit v2 on v0

v2 whole, which is shorter than its diff:
```python
import functools
import math

import jax
import jax.numpy as jnp
from jax import lax
from jax.experimental import pallas as pl
from jax.experimental.pallas import tpu as pltpu
from jax.sharding import PartitionSpec as P

BEADS = 32
CONTR = 4
ITERS = 2
CUTOFF = 9.0
CUT2 = CUTOFF * CUTOFF
THOLE = 0.39
LOG2E = 1.4426950408889634
LN2 = 0.6931471805599453
L = 128
KP = 8
F32 = jnp.float32
BF16 = jnp.bfloat16
VMEM_LIMIT = 20 * 1024 * 1024


def split3(x):
    h = x.astype(BF16).astype(F32)
    r = x - h
    m = r.astype(BF16).astype(F32)
    return h, m, r - m


def dot(a, b, ca=1, cb=0):
    return lax.dot_general(a, b, (((ca,), (cb,)), ((), ())), preferred_element_type=F32)


def dot3(x, mat, cb):
    rows = x.shape[0]
    out = dot(jnp.concatenate(split3(x), 0).astype(BF16), mat, 1, cb)
    return (out[:rows] + out[rows : 2 * rows]) + out[2 * rows :]


TYPES = 13


def lanes(n):
    return lax.broadcasted_iota(jnp.int32, (1, n), 1)


def select(kind, coef, stride, slot, depth):
    rows = lax.broadcasted_iota(jnp.int32, (depth, kind.shape[1]), 0)
    want = jnp.where(kind < 0, -1, kind * stride + slot)
    return jnp.where(rows == want, coef, 0.0).astype(BF16)


def pair_selects(rows, count):
    lane = lanes(max(count * 32, L))
    b, f = lane // 32, lane % 32
    a, j = f // 6, f % 6
    t_kind = jnp.where(j < 3, a, jnp.where(j < 5, 3 + a, 6 + a))
    s_level = jnp.where(j < 3, j, jnp.where(j == 4, 1, 0))
    s_kind = 3 * s_level + a
    t_kind = jnp.where(f < 18, t_kind, jnp.where(f < 21, f - 9, 12))
    s_kind = jnp.where(f < 18, s_kind, jnp.where(f < 21, 12, f - 12))
    none = (f >= 24) | (b >= count)
    t_kind = jnp.where(none, -1, t_kind)
    s_kind = jnp.where(none, -1, s_kind)
    s_coef = jnp.where(f < 18, -2.0, 1.0)
    depth = TYPES * rows
    return select(t_kind, jnp.ones_like(s_coef), rows, b, depth), select(s_kind, s_coef, rows, b, depth)


def sum_select(rows, count):
    lane = lanes(max(count * 32, L))
    b, r = lane // 32, lane % 32
    p, f = r // 8, r % 8
    kind = jnp.where((f < 4) & (p < 3) & (b < count), p * 4 + f, -1)
    return select(kind, 1.0, rows, b, 12 * rows)


def induce_select():
    lane = lanes(CONTR * L)
    k, r = lane // L, lane % L
    p, f = (r - 64) // 8, (r - 64) % 8
    second = jnp.where((r >= 64) & (r < 88) & (f < 3), p * 16 + f, -1)
    kind = jnp.where(r < 48, r, second)
    return select(kind, 1.0, KP, k, 48 * KP)


def perm_matrix(rank_row, w):
    rows = lax.broadcasted_iota(jnp.int32, (w, w), 0).astype(F32)
    return jnp.where(rows == rank_row, 1.0, 0.0).astype(BF16)


def pair_pieces(xs):
    hx, hy, hz = (split3(x) for x in xs)
    n = xs[0] * xs[0] + xs[1] * xs[1] + xs[2] * xs[2]
    parts = [hx[0], hy[0], hz[0], hx[1], hy[1], hz[1], hx[2], hy[2], hz[2]]
    parts += list(split3(n)) + [jnp.ones_like(n)]
    return jnp.concatenate(parts, 0).astype(BF16)


def center_of(xs, count):
    w = xs[0].shape[1]
    return [jnp.sum(x[:count], keepdims=True) * (1.0 / (count * w)) for x in xs]


def columns(misc):
    al = misc[1:2]
    good = al > 0.0
    inv = jnp.where(good, lax.rsqrt(jnp.where(good, al, 1.0)), 0.0)
    return jnp.concatenate([inv, misc[2:3], jnp.zeros_like(misc[:6])], 0)


def ranges(x, al, count, w):
    good = al > 0.0
    lo = jnp.where(good, x[:count], 1e30)
    hi = jnp.where(good, x[:count], -1e30)
    out = []
    for i in range(w // L):
        out.append((jnp.min(lo[:, i * L : (i + 1) * L]), jnp.max(hi[:, i * L : (i + 1) * L])))
    return out


def near_list(lst, size, trange, sranges):
    lst[1] = 0
    lst[1 + size] = 0
    count = jnp.int32(0)
    sj = 0
    for slab in sranges:
        for smin, smax in slab:
            for ti, (tmin, tmax) in enumerate(trange):
                near = (smin - tmax < CUTOFF) & (tmin - smax < CUTOFF)
                lst[1 + count] = sj * L
                lst[1 + size + count] = ti * L
                count = count + near.astype(jnp.int32)
            sj += 1
    lst[0] = count


def own_blocks(nt):
    return [(i, i) for i in range(nt)], [(i, j) for i in range(nt) for j in range(i + 1, nt)]


def pair_basis(r2, q):
    safe = jnp.maximum(r2, 1e-4)
    inv = lax.rsqrt(safe)
    c = (safe * inv) * (safe * q)
    decay = jnp.exp2(c)
    v = jnp.maximum(CUT2 - r2, 0.0) * inv
    return c, decay, inv, v


def two(x):
    hi = x.astype(BF16)
    return hi, (x - hi.astype(F32)).astype(BF16)


def weights(nb, shape, rank, bead_dim):
    b = lax.broadcasted_iota(jnp.int32, shape, bead_dim)
    k = lax.broadcasted_iota(jnp.int32, shape, 1 - bead_dim)
    turn = k * (BEADS // CONTR) - (rank * nb + b) + 2 * BEADS
    turn = (turn + BEADS // 2) % BEADS - BEADS // 2
    cos = jnp.cos(turn.astype(F32) * (2.0 * math.pi / BEADS))
    return jnp.where((k < CONTR) & (b < nb), 2.0 * cos * (1.0 + cos), 0.0)


def hdot(a, b):
    return jnp.dot(a, b, precision=lax.Precision.HIGHEST, preferred_element_type=F32)


def pack_kernel(nb, nbp, w, pos, charge, polar, mol, out, rank_out, scr):
    scr[...] = jnp.zeros_like(scr)
    for a in range(3):
        scr[a * nbp : a * nbp + nb, :] = pos[a]
    base = 3 * nbp
    scr[base : base + 1, :] = charge[...].reshape(1, w)
    scr[base + 1 : base + 2, :] = polar[...].reshape(1, w)
    scr[base + 2 : base + 3, :] = mol[...].reshape(1, w).astype(F32)
    x = scr[...]
    key = jnp.sum(x[:nbp], 0, keepdims=True)
    col = jnp.transpose(jnp.broadcast_to(key, (8, w)))[:, :1]
    jj = lax.broadcasted_iota(jnp.int32, (w, w), 0)
    ii = lax.broadcasted_iota(jnp.int32, (w, w), 1)
    before = (col < key) | ((col == key) & (jj < ii))
    rank = jnp.sum(jnp.where(before, 1.0, 0.0), 0, keepdims=True)
    rank_out[...] = jnp.broadcast_to(rank, (8, w))
    out[...] = dot3(x, perm_matrix(rank, w), 1)


def perm_sources(nbp, w, src, center, s, sel_s, sel_r, fs, rt, cols):
    base = 3 * nbp
    xs = [src[a * nbp : (a + 1) * nbp, :] - center[a] for a in range(3)]
    misc = src[base : base + 8, :]
    fs[s * w : (s + 1) * w, :] = dot(pair_pieces(xs), sel_s, 0, 0).astype(BF16)
    q = jnp.broadcast_to(misc[0:1] * (1.0 / (CUT2 * CUT2)), xs[0].shape)
    feats = [split3(v) for v in (xs[0] * q, xs[1] * q, xs[2] * q, q)]
    stack = jnp.concatenate([feats[f][p] for p in range(3) for f in range(4)], 0)
    rt[:, s * w : (s + 1) * w] = dot(sel_r, stack.astype(BF16), 0, 0).astype(BF16)
    cols[s * w : (s + 1) * w, :] = jnp.transpose(columns(misc))
    return xs[0], misc[1:2]


def perm_pairs(n, first, lst, size, sym, groups, fs, ft, rt, qbuf, acc, r2buf, fbuf):
    r2buf[...] = jnp.full_like(r2buf, 2.0 * CUT2)
    fbuf[...] = jnp.zeros_like(fbuf)
    total = n * groups

    def where_is(i):
        i = jnp.maximum(jnp.minimum(i, total - 1), 0)
        e = first + i // groups
        s0 = pl.multiple_of(lst[1 + e], L)
        t0 = pl.multiple_of(lst[1 + size + e], L)
        return e, s0, t0, i % groups

    def step(i, carry):
        e, s0, t0, g = where_is(i - 2)
        for j in range(4):
            r0 = pl.multiple_of((g * 4 + j) * 32, 32)
            r = rt[pl.ds(r0, 32), pl.ds(s0, L)]
            pair = fbuf[j]
            acc[pl.ds(r0, 32), pl.ds(t0, L)] += dot(jnp.concatenate([r, r], 1), pair)
            if sym:
                back = dot(rt[pl.ds(r0, 32), pl.ds(t0, L)], pair, 1, 1)
                acc[pl.ds(r0, 32), pl.ds(s0, L)] += back[:, :L] + back[:, L:]
        e, s0, t0, g = where_is(i - 1)
        for j in range(4):
            c, decay, inv, v = pair_basis(r2buf[j], qbuf[e])
            hi, lo = two((v * v) * (inv * (1.0 - decay)))
            fbuf[j, :L, :] = hi
            fbuf[j, L:, :] = lo
        e, s0, t0, g = where_is(i)
        lhs = fs[pl.ds(s0, L), pl.ds(pl.multiple_of(g * L, L), L)]
        for j in range(4):
            b0 = pl.multiple_of((g * 4 + j) * L, L)
            r2buf[j] = dot(lhs, ft[pl.ds(b0, L), pl.ds(t0, L)])
        return carry

    lax.fori_loop(0, total + 2, step, 0)


def block_q(n, first, lst, size, own, cols, qrow, qbuf):
    def one(i, carry):
        e = first + i
        s0 = pl.multiple_of(lst[1 + e], L)
        t0 = pl.multiple_of(lst[1 + size + e], L)
        cc = cols[pl.ds(s0, L), :]
        row = qrow[:, pl.ds(t0, L)]
        q = cc[:, 0:1] * row[0:1]
        if own:
            q = jnp.where(cc[:, 1:2] == row[1:2], 0.0, q)
        qbuf[e] = q
        return carry

    lax.fori_loop(0, n, one, 0)


def q_rows(misc, qrow):
    c = columns(misc)
    qrow[...] = c
    qrow[0:1, :] = c[0:1] * (-THOLE * LOG2E)


def fixed_list(lst, size, blocks):
    lst[0] = len(blocks)
    for e, (s, t) in enumerate(blocks):
        lst[1 + e] = s * L
        lst[1 + size + e] = t * L


def perm_own_kernel(nb, nbp, w, tgt, acc, ft, fs, rt, cols, qrow, qbuf, r2buf, fbuf, lst):
    nt = w // L
    base = 3 * nbp
    sel_t, sel_s = pair_selects(nbp, nb)
    coords = [tgt[a * nbp : (a + 1) * nbp, :] for a in range(3)]
    center = center_of(coords, nb)
    compact = dot(sel_t, pair_pieces([x - c for x, c in zip(coords, center)]), 0, 0).astype(BF16)
    ft[...] = jnp.zeros_like(ft)
    for b in range(nb):
        r0 = b * L + (b % 4) * 32
        ft[r0 : r0 + 32, :] = compact[b * 32 : (b + 1) * 32]
    perm_sources(nbp, w, tgt, center, 0, sel_s, sum_select(nbp, nb), fs, rt, cols)
    q_rows(tgt[base : base + 8, :], qrow)
    acc[...] = jnp.zeros_like(acc)
    diag, off = own_blocks(nt)
    size = len(diag) + len(off)
    fixed_list(lst, size, diag + off)
    block_q(size, 0, lst, size, True, cols, qrow, qbuf)
    groups = nb // 4
    perm_pairs(len(diag), 0, lst, size, False, groups, fs, ft, rt, qbuf, acc, r2buf, fbuf)
    perm_pairs(len(off), len(diag), lst, size, True, groups, fs, ft, rt, qbuf, acc, r2buf, fbuf)


def perm_near_kernel(
    nb, nbp, w, tgt, srca, srcb, ft, acc_in, rank, perm_out, msg_out,
    fs, rt, cols, qrow, qbuf, r2buf, fbuf, acc, lst,
):
    nt = w // L
    base = 3 * nbp
    _, sel_s = pair_selects(nbp, nb)
    sel_r = sum_select(nbp, nb)
    coords = [tgt[a * nbp : (a + 1) * nbp, :] for a in range(3)]
    center = center_of(coords, nb)
    xt = [x - c for x, c in zip(coords, center)]
    sranges = []
    for s, src in enumerate((srca, srcb)):
        x, al = perm_sources(nbp, w, src, center, s, sel_s, sel_r, fs, rt, cols)
        sranges.append(ranges(x, al, nb, w))
    size = 2 * nt * nt
    near_list(lst, size, ranges(xt[0], tgt[base + 1 : base + 2, :], nb, w), sranges)
    q_rows(tgt[base : base + 8, :], qrow)
    n = lst[0]
    block_q(n, 0, lst, size, False, cols, qrow, qbuf)
    acc[...] = acc_in[...]
    perm_pairs(n, 0, lst, size, False, nb // 4, fs, ft, rt, qbuf, acc, r2buf, fbuf)
    if nb < nbp:
        perm_out[...] = jnp.zeros_like(perm_out)
    for b in range(nb):
        s = acc[b * 32 : b * 32 + 8, :] + acc[b * 32 + 8 : b * 32 + 16, :]
        s = s + acc[b * 32 + 16 : b * 32 + 24, :]
        for a in range(3):
            row = xt[a][b : b + 1] * s[3:4] - s[a : a + 1]
            perm_out[a * nbp + b : a * nbp + b + 1, :] = row
    wc = weights(nb, (KP, nbp), lax.axis_index("bead"), 1) * (1.0 / BEADS)
    parts = [hdot(wc, perm_out[a * nbp : (a + 1) * nbp, :]) for a in range(3)]
    parts += [hdot(wc, coords[a]) for a in range(3)]
    msg_out[...] = dot3(jnp.concatenate(parts, 0), perm_matrix(rank[0:1, :], w), 0)


def start_kernel(nbp, w, msg, other, rank, pack, m0, cf):
    both = dot3(msg[...] + other[...], perm_matrix(rank[0:1, :], w), 1)
    n = 3 * KP
    cf[...] = both[:n]
    m0[:n, :] = both[:n] * pack[3 * nbp + 1 : 3 * nbp + 2, :]
    m0[n:, :] = both[n:]


def centered(m, center):
    n = 3 * KP
    return [m[n + a * KP : n + (a + 1) * KP, :] - center[a] for a in range(3)]


def own_center(m):
    n = 3 * KP
    return center_of([m[n + a * KP : n + (a + 1) * KP, :] for a in range(3)], CONTR)


def tensor_targets(xt, sel_t, ft):
    compact = dot(sel_t, pair_pieces(xt), 0, 0).astype(BF16)
    ft[...] = jnp.zeros_like(ft)
    for k in range(CONTR):
        r0 = k * L + k * 32
        ft[r0 : r0 + 32, :] = compact[k * 32 : (k + 1) * 32]


def tensor_pairs(n, lst, size, fs, ft, qbuf, r2buf, tensors):
    def where_is(i):
        e = jnp.maximum(jnp.minimum(i, n - 1), 0)
        return e, pl.multiple_of(lst[1 + e], L), pl.multiple_of(lst[1 + size + e], L)

    def step(i, carry):
        e, s0, t0 = where_is(i - 1)
        for k in range(CONTR):
            c, decay, inv, v = pair_basis(r2buf[k], qbuf[e])
            l3 = 1.0 - decay
            l5 = l3 + (c * LN2) * decay
            w3 = (v * v) * inv
            w5 = w3 * (inv * inv)
            a_hi, a_lo = two(w5 * l5)
            b_hi, b_lo = two(w3 * l3)
            tensors[k, e, 0:L, :] = a_hi
            tensors[k, e, L : 2 * L, :] = a_lo
            tensors[k, e, 2 * L : 3 * L, :] = b_hi
            tensors[k, e, 3 * L : 4 * L, :] = b_lo
        e, s0, t0 = where_is(i)
        lhs = fs[pl.ds(s0, L), :]
        for k in range(CONTR):
            r2buf[k] = dot(lhs, ft[k * L : (k + 1) * L, pl.ds(t0, L)])
        return carry

    r2buf[...] = jnp.full_like(r2buf, 2.0 * CUT2)
    lax.fori_loop(0, n + 1, step, 0)


def induce_features(mu, x, sel_e):
    scale = 1.0 / (CUT2 * CUT2)
    m = [mu[a * KP : (a + 1) * KP, :] * scale for a in range(3)]
    dotted = x[0] * m[0] + x[1] * m[1] + x[2] * m[2]
    feats = m + [dotted] + [x[a] * m[b] for a in range(3) for b in range(3)]
    feats += [x[a] * dotted for a in range(3)]
    split = [split3(f) for f in feats]
    stack = jnp.concatenate([split[f][p] for p in range(3) for f in range(16)], 0)
    return dot(sel_e, stack.astype(BF16), 0, 0).astype(BF16)


def twice(x):
    return jnp.concatenate([x, x], 1)


def own_sums(w, mu, m0, tensors, acc_a, acc_b, le):
    nt = w // L
    le[...] = induce_features(mu, centered(m0, own_center(m0)), induce_select())
    acc_a[...] = jnp.zeros_like(acc_a)
    acc_b[...] = jnp.zeros_like(acc_b)
    diag, off = own_blocks(nt)
    for e, (s, t) in enumerate(diag + off):
        s0, t0 = s * L, t * L
        for k in range(CONTR):
            ra, rb = k * L, k * L + 64
            pa, pb = tensors[k, e, 0 : 2 * L, :], tensors[k, e, 2 * L : 4 * L, :]
            a0, b0 = k * 48, k * 32
            acc_a[a0 : a0 + 48, t0 : t0 + L] += dot(twice(le[ra : ra + 48, s0 : s0 + L]), pa)
            acc_b[b0 : b0 + 32, t0 : t0 + L] += dot(twice(le[rb : rb + 32, s0 : s0 + L]), pb)
            if s != t:
                back = dot(le[ra : ra + 48, t0 : t0 + L], pa, 1, 1)
                acc_a[a0 : a0 + 48, s0 : s0 + L] += back[:, :L] + back[:, L:]
                back = dot(le[rb : rb + 32, t0 : t0 + L], pb, 1, 1)
                acc_b[b0 : b0 + 32, s0 : s0 + L] += back[:, :L] + back[:, L:]


def near_sums(w, mus, cps, m0, tensors, lst, acc_a_in, acc_b_in, acc_a, acc_b, le, ev):
    nt = w // L
    center = own_center(m0)
    sel_e = induce_select()
    for s, (mu, cp) in enumerate(zip(mus, cps)):
        le[:, s * w : (s + 1) * w] = induce_features(mu, centered(cp, center), sel_e)
    acc_a[...] = acc_a_in[...]
    acc_b[...] = acc_b_in[...]
    size = 2 * nt * nt

    def step(e, carry):
        s0 = pl.multiple_of(lst[1 + e], L)
        t0 = pl.multiple_of(lst[1 + size + e], L)
        for k in range(CONTR):
            ra, rb = k * L, k * L + 64
            a0, b0 = k * 48, k * 32
            fa, fb = twice(le[ra : ra + 48, pl.ds(s0, L)]), twice(le[rb : rb + 32, pl.ds(s0, L)])
            acc_a[a0 : a0 + 48, pl.ds(t0, L)] += dot(fa, tensors[k, e, 0 : 2 * L, :])
            acc_b[b0 : b0 + 32, pl.ds(t0, L)] += dot(fb, tensors[k, e, 2 * L : 4 * L, :])
        return carry

    lax.fori_loop(0, lst[0], step, 0)
    ev[...] = jnp.zeros_like(ev)
    xt = centered(m0, center)
    for k in range(CONTR):
        o = k * 48
        sa = acc_a[o : o + 16, :] + acc_a[o + 16 : o + 32, :] + acc_a[o + 32 : o + 48, :]
        o = k * 32
        sb = acc_b[o : o + 8, :] + acc_b[o + 8 : o + 16, :] + acc_b[o + 16 : o + 24, :]
        x = [v[k : k + 1] for v in xt]
        along = x[0] * sa[0:1] + x[1] * sa[1:2] + x[2] * sa[2:3] - sa[3:4]
        for a in range(3):
            cross = sum(x[b] * sa[4 + 3 * a + b : 5 + 3 * a + b] for b in range(3))
            full = x[a] * along - cross + sa[13 + a : 14 + a]
            ev[a * KP + k : a * KP + k + 1, :] = 3.0 * full - sb[a : a + 1]


def own_first_kernel(nbp, w, m0, pack, tensors, acc_a, acc_b, le, fs, ft, cols, qrow, qbuf, r2buf, lst):
    misc = pack[3 * nbp : 3 * nbp + 8, :]
    sel_t, sel_s = pair_selects(KP, CONTR)
    xt = centered(m0, own_center(m0))
    tensor_targets(xt, sel_t, ft)
    fs[...] = dot(pair_pieces(xt), sel_s, 0, 0).astype(BF16)
    cols[...] = jnp.transpose(columns(misc))
    q_rows(misc, qrow)
    diag, off = own_blocks(w // L)
    size = len(diag) + len(off)
    fixed_list(lst, size, diag + off)
    block_q(size, 0, lst, size, True, cols, qrow, qbuf)
    tensor_pairs(size, lst, size, fs, ft, qbuf, r2buf, tensors)
    own_sums(w, m0, m0, tensors, acc_a, acc_b, le)


def own_kernel(w, mu, m0, tensors, acc_a, acc_b, le):
    own_sums(w, mu, m0, tensors, acc_a, acc_b, le)


def update(pack, nbp, cf, ev):
    return pack[3 * nbp + 1 : 3 * nbp + 2, :] * (cf[...] + ev[...])


def near_first_kernel(
    nbp, w, m0, m0a, m0b, pack, packa, packb, cf, acc_a_in, acc_b_in,
    mu_out, tensors, lst, fs, ft, cols, qrow, qbuf, r2buf, acc_a, acc_b, le, ev,
):
    nt = w // L
    base = 3 * nbp
    sel_t, sel_s = pair_selects(KP, CONTR)
    center = own_center(m0)
    xt = centered(m0, center)
    tensor_targets(xt, sel_t, ft)
    sranges = []
    for s, (m, pk) in enumerate(((m0a, packa), (m0b, packb))):
        misc = pk[base : base + 8, :]
        xs = centered(m, center)
        fs[s * w : (s + 1) * w, :] = dot(pair_pieces(xs), sel_s, 0, 0).astype(BF16)
        cols[s * w : (s + 1) * w, :] = jnp.transpose(columns(misc))
        sranges.append(ranges(xs[0], misc[1:2], CONTR, w))
    misc = pack[base : base + 8, :]
    size = 2 * nt * nt
    near_list(lst, size, ranges(xt[0], misc[1:2], CONTR, w), sranges)
    q_rows(misc, qrow)
    n = lst[0]
    block_q(n, 0, lst, size, False, cols, qrow, qbuf)
    tensor_pairs(n, lst, size, fs, ft, qbuf, r2buf, tensors)
    near_sums(w, [m0a, m0b], [m0a, m0b], m0, tensors, lst, acc_a_in, acc_b_in, acc_a, acc_b, le, ev)
    mu_out[...] = update(pack, nbp, cf, ev)


def near_kernel(
    nbp, w, mua, mub, m0, m0a, m0b, pack, cf, acc_a_in, acc_b_in, tensors, lst, mu_out, acc_a, acc_b, le, ev,
):
    near_sums(w, [mua, mub], [m0a, m0b], m0, tensors, lst, acc_a_in, acc_b_in, acc_a, acc_b, le, ev)
    mu_out[...] = update(pack, nbp, cf, ev)


def final_kernel(
    nb, nbp, w, mua, mub, m0, m0a, m0b, mu, perm, rank, acc_a_in, acc_b_in, tensors, lst,
    total_out, dip_out, acc_a, acc_b, le, ev,
):
    near_sums(w, [mua, mub], [m0a, m0b], m0, tensors, lst, acc_a_in, acc_b_in, acc_a, acc_b, le, ev)
    us = weights(nb, (nbp, KP), lax.axis_index("bead"), 0) * (1.0 / CONTR)
    parts = [perm[a * nbp : (a + 1) * nbp, :] + hdot(us, ev[a * KP : (a + 1) * KP, :]) for a in range(3)]
    parts.append(mu[...])
    out = dot3(jnp.concatenate(parts, 0), perm_matrix(rank[0:1, :], w), 0)
    for a in range(3):
        total_out[a] = out[a * nbp : a * nbp + nb]
        d0 = 3 * nbp + a * KP
        dip_out[a] = out[d0 : d0 + CONTR]


def swap_pairs(count, first):
    pairs = []
    for i in range(first, count - 1, 2):
        pairs += [(i, i + 1), (i + 1, i)]
    return pairs


def call(kernel, outs, name, scratch, args, smem_in=(), smem_out=()):
    smem = pl.BlockSpec(memory_space=pltpu.SMEM)
    vmem = pl.BlockSpec(memory_space=pltpu.VMEM)
    return pl.pallas_call(
        kernel,
        out_shape=[jax.ShapeDtypeStruct(s, d) for s, d in outs],
        in_specs=[smem if i in smem_in else vmem for i in range(len(args))],
        out_specs=[smem if i in smem_out else vmem for i in range(len(outs))],
        scratch_shapes=list(scratch),
        compiler_params=pltpu.CompilerParams(vmem_limit_bytes=VMEM_LIMIT),
        name=name,
    )(*args)


def body(positions, charges, polar, molecule):
    nb, _, w = positions.shape
    nbp = -(-nb // 16) * 16
    nt = w // L
    nbead = lax.axis_size("bead")
    nspace = lax.axis_size("space")
    rows = 3 * nbp + 8
    n = 3 * KP
    own_size = nt * (nt + 1) // 2
    near_size = 2 * nt * nt
    part = functools.partial

    def exchange(x):
        near = lax.ppermute(x, "space", swap_pairs(nspace, 0))
        far = lax.ppermute(x, "space", swap_pairs(nspace, 1))
        return near, far

    pack, rank = call(
        part(pack_kernel, nb, nbp, w), [((rows, w), F32), ((8, w), F32)], "pack",
        [pltpu.VMEM((rows, w), F32)],
        (jnp.transpose(positions, (1, 0, 2)), charges, polar, molecule),
    )
    packa, packb = exchange(pack)

    def perm_scratch(nsrc, blocks):
        return [
            pltpu.VMEM((nsrc * w, nb * 32), BF16),
            pltpu.VMEM((nb * 32, nsrc * w), BF16),
            pltpu.VMEM((nsrc * w, 8), F32),
            pltpu.VMEM((8, w), F32),
            pltpu.VMEM((blocks, L, L), F32),
            pltpu.VMEM((4, L, L), F32),
            pltpu.VMEM((4, 2 * L, L), BF16),
        ]

    acc, ft = call(
        part(perm_own_kernel, nb, nbp, w), [((nb * 32, w), F32), ((nb * L, w), BF16)], "perm_own",
        perm_scratch(1, own_size) + [pltpu.SMEM((1 + 2 * own_size,), jnp.int32)], (pack,),
    )
    perm, msg = call(
        part(perm_near_kernel, nb, nbp, w), [((3 * nbp, w), F32), ((2 * n, w), F32)], "perm_near",
        perm_scratch(2, near_size)
        + [pltpu.VMEM((nb * 32, w), F32), pltpu.SMEM((1 + 2 * near_size,), jnp.int32)],
        (pack, packa, packb, ft, acc, rank),
    )

    if nbead == 2:
        other = lax.ppermute(msg, "bead", [(0, 1), (1, 0)])
    else:
        other = lax.psum(msg, "bead") - msg
    m0, cf = call(
        part(start_kernel, nbp, w), [((2 * n, w), F32), ((n, w), F32)], "start", [], (msg, other, rank, pack),
    )
    m0a, m0b = exchange(m0)

    def tensor_scratch(nsrc, blocks):
        return [
            pltpu.VMEM((nsrc * w, L), BF16),
            pltpu.VMEM((CONTR * L, w), BF16),
            pltpu.VMEM((nsrc * w, 8), F32),
            pltpu.VMEM((8, w), F32),
            pltpu.VMEM((blocks, L, L), F32),
            pltpu.VMEM((CONTR, L, L), F32),
        ]

    accs = [((CONTR * 48, w), F32), ((CONTR * 32, w), F32)]
    near_scratch = [pltpu.VMEM(s, d) for s, d in accs]
    near_scratch += [pltpu.VMEM((CONTR * L, 2 * w), BF16), pltpu.VMEM((n, w), F32)]
    own_scratch = [pltpu.VMEM((CONTR * L, w), BF16)]
    t_own, acc_a, acc_b = call(
        part(own_first_kernel, nbp, w), [((CONTR, own_size, 4 * L, L), BF16)] + accs, "own_0",
        own_scratch + tensor_scratch(1, own_size) + [pltpu.SMEM((1 + 2 * own_size,), jnp.int32)],
        (m0, pack),
    )
    mu, t_nbr, lst = call(
        part(near_first_kernel, nbp, w),
        [((n, w), F32), ((CONTR, near_size, 4 * L, L), BF16), ((1 + 2 * near_size,), jnp.int32)], "near_0",
        tensor_scratch(2, near_size) + near_scratch,
        (m0, m0a, m0b, pack, packa, packb, cf, acc_a, acc_b), smem_out=(2,),
    )
    for step in range(1, ITERS + 1):
        mua, mub = exchange(mu)
        acc_a, acc_b = call(part(own_kernel, w), accs, f"own_{step}", own_scratch, (mu, m0, t_own))
        if step < ITERS:
            (mu,) = call(
                part(near_kernel, nbp, w), [((n, w), F32)], f"near_{step}", near_scratch,
                (mua, mub, m0, m0a, m0b, pack, cf, acc_a, acc_b, t_nbr, lst), smem_in=(10,),
            )
    total, dipoles = call(
        part(final_kernel, nb, nbp, w), [((3, nb, w), F32), ((3, CONTR, w), F32)], "final", near_scratch,
        (mua, mub, m0, m0a, m0b, mu, perm, rank, acc_a, acc_b, t_nbr, lst), smem_in=(11,),
    )
    return (jnp.transpose(total, (1, 0, 2)), jnp.transpose(dipoles, (1, 0, 2)))


def solution(mesh):
    in_specs = (P("bead", None, "space"), P("space"), P("space"), P("space"))
    out_specs = (P("bead", None, "space"), P(None, None, "space"))
    return jax.shard_map(body, mesh=mesh, in_specs=in_specs, out_specs=out_specs, check_vma=False)
```

time: 351 us -> 65 us (0.19)
  other arithmetic: 224 us -> 0 us
  loops' own time: 41.7 us -> 0 us
  Pallas kernels: 0 us -> 39.9 us
  local copies, waits for them, and re-layouts: 34.1 us -> 2.92 us
  starting transfers between devices: 26.6 us -> 14.6 us
  waiting for transfers between devices: 15.2 us -> 6.57 us
  blocking collectives: 6.43 us -> 0 us
    reduce_sum x1008 -> x0, other arithmetic: 116 us -> none  [the longest x504 62.9 us: step(): return (total + jnp.sum(term, axis=2), None)]
    mul x507 -> x0, other arithmetic: 93.2 us -> none  [the longest x288 50.3 us: step(): term = (taper * damp3 * inv3 * charge[None, :])[None] * diff]
    another operation x32 -> x0, loops' own time: 41.7 us -> none  [the longest x28 40.1 us: pair_field(): total, unused = lax.scan(step, start, blocks)]
    pallas_call x0 -> x10, Pallas kernels: none -> 39.9 us  [call(): pl.pallas_call(kernel, out_shape=[jax.ShapeDtypeStruct(s, d) for s, d in...]
    dynamic_slice x2284 -> x0, local copies, waits for them, and re-layouts: 20.1 us -> none  [the longest x2232 19.6 us: pair_field(): total, unused = lax.scan(step, start, blocks)]
    ppermute x10 -> x9, starting transfers between devices: 26.6 us -> 14.6 us  [the longest x4 12.4 us: exchange(): far = lax.ppermute(x, 'space', swap_pairs(nspace, 1))]
    ppermute x10 -> x9, waiting for transfers between devices: 15.2 us -> 6.57 us  [the longest x4 4.58 us: exchange(): far = lax.ppermute(x, 'space', swap_pairs(nspace, 1))]
    gt x504 -> x0, other arithmetic: 7.69 us -> none  [step(): alpha[None, :] > 0.0]
where the time goes in v2:
time: 65 us; the launch traced here: 64.7 us
  Pallas kernels  39.9 us (61%)
  starting transfers between devices  14.6 us (22%)
  waiting for transfers between devices  6.57 us (10%)
  local copies, waits for them, and re-layouts  2.92 us (4%)
  between operations  0.79 us (1%)
    pallas_call x10, Pallas kernels, call(): pl.pallas_call(kernel, out_shape=[jax.ShapeDtypeStruct(s, d) for s, d in...  39.9 us
    ppermute x4, starting transfers between devices, exchange(): far = lax.ppermute(x, 'space', swap_pairs(nspace, 1))  12.4 us
    ppermute x4, waiting for transfers between devices, exchange(): far = lax.ppermute(x, 'space', swap_pairs(nspace, 1))  4.58 us
    unnamed x8, local copies, waits for them, and re-layouts  2.92 us
    ppermute x1, waiting for transfers between devices, body(): other = lax.ppermute(msg, 'bead', [(0, 1), (1, 0)])  1.98 us
  transfers between devices with their start and end apart: 9, of which 3 were waited for; matrix products, arithmetic and copies ran while one was open for 0% of the time, Pallas kernels for 27%

profile of v2, /device:TPU:21, one launch (start us, length us, event | category | flops | bytes accessed | tf_op | source)
XLA Modules:
  0.0 64.7 jit_solution(1912093762898592968)
XLA Ops:
  0.6 0.0 copy-start
  0.6 0.9 %copy-done = f32[16,3,384]{2,0,1:T(8,128)S(1)} copy-done((f32[16,3,384]{2,0,1:T(8,128)S(1)}, f32[16,3,384]{2,0,1:T(8,128)}, u32[]{:S(2)}) %copy-start) | copy-done | bytes 73752
  1.5 0.0 copy-start.1
  1.5 0.7 %copy-done.1 = f32[384]{0:T(512)S(1)} copy-done((f32[384]{0:T(512)S(1)}, f32[384]{0:T(512)}, u32[]{:S(2)}) %copy-start.1) | copy-done | bytes 1560
  2.2 0.0 copy-start.2
  2.2 0.7 %copy-done.2 = f32[384]{0:T(512)S(1)} copy-done((f32[384]{0:T(512)S(1)}, f32[384]{0:T(512)}, u32[]{:S(2)}) %copy-start.2) | copy-done | bytes 1560
  2.9 0.0 copy-start.3
  2.9 0.7 %copy-done.3 = s32[384]{0:T(512)S(1)} copy-done((s32[384]{0:T(512)S(1)}, s32[384]{0:T(512)}, u32[]{:S(2)}) %copy-start.3) | copy-done | bytes 1560
  3.6 0.6 pack.1
  4.1 3.7 %collective-permute-start.1 = (f32[56,384]{1,0:T(8,128)S(1)}, f32[56,384]{1,0:T(8,128)S(1)}, u32[]{:S(2)}, u32[]{:S(2)}) collective-permute-start(f32[56,384]{1,0:T(8,128)S(1)} %get-tuple-element.22.tgt.pack), channel_id=1, source_target_pairs={{1,2},{2,1},{3,4},{4,3},{5,6},{6,5},{7,8},{8,7},{9,10},{10,9},{11,... | collective-permute-start | bytes 258056 | tf_op jit(solution)/shard_map/ppermute | solution.py:567
  7.8 0.1 collective-permute-start
  7.9 9.6 %perm_own.1 = (f32[512,384]{1,0:T(8,128)S(1)}, bf16[2048,384]{1,0:T(8,128)(2,1)S(1)}) custom-call(f32[56,384]{1,0:T(8,128)S(1)} %get-tuple-element.22.tgt.pack), custom_call_target="tpu_custom_call" | custom-call | tf_op jit(solution)/shard_map/perm_own/pallas_call | solution.py:542
  17.5 0.0 collective-permute-done.1.srcb.packb
  17.6 0.0 collective-permute-done.srca.packa
  17.6 9.5 %perm_near.1 = (f32[48,384]{1,0:T(8,128)S(1)}, f32[48,384]{1,0:T(8,128)S(1)}) custom-call(f32[56,384]{1,0:T(8,128)S(1)} %get-tuple-element.22.tgt.pack, f32[56,384]{1,0:T(8,128)S(1)} %collective-permute-done.srca.packa, f32[56,384]{1,0:T(8,128)S(1)} %collective-permute-done.1.srcb.packb, bf16[2048,384]{1,0:T(8,128)(2,1)S(1)} %get-tuple-element.23.ft, ...), custom_call_target="tpu_custom_call" | custom-call | tf_op jit(solution)/shard_map/perm_near/pallas_call | solution.py:542
  27.1 1.3 %collective-permute-start.2 = (f32[48,384]{1,0:T(8,128)S(1)}, f32[48,384]{1,0:T(8,128)S(1)}, u32[]{:S(2)}, u32[]{:S(2)}) collective-permute-start(f32[48,384]{1,0:T(8,128)S(1)} %get-tuple-element.26.msg), channel_id=1, source_target_pairs={{0,16},{16,0},{1,17},{17,1},{2,18},{18,2},{3,19},{19,3},{4,20},{20... | collective-permute-start | bytes 221192 | tf_op jit(solution)/shard_map/ppermute | solution.py:600
  28.4 2.0 %collective-permute-done.2.other = f32[48,384]{1,0:T(8,128)S(1)} collective-permute-done((f32[48,384]{1,0:T(8,128)S(1)}, f32[48,384]{1,0:T(8,128)S(1)}, u32[]{:S(2)}, u32[]{:S(2)}) %collective-permute-start.2) | collective-permute-done | bytes 73760 | tf_op jit(solution)/shard_map/ppermute | solution.py:600
  30.3 0.2 start.1
  30.6 4.7 %collective-permute-start.4 = (f32[48,384]{1,0:T(8,128)S(1)}, f32[48,384]{1,0:T(8,128)S(1)}, u32[]{:S(2)}, u32[]{:S(2)}) collective-permute-start(f32[48,384]{1,0:T(8,128)S(1)} %get-tuple-element.27.m0), channel_id=1, source_target_pairs={{1,2},{2,1},{3,4},{4,3},{5,6},{6,5},{7,8},{8,7},{9,10},{10,9},{11,... | collective-permute-start | bytes 221192 | tf_op jit(solution)/shard_map/ppermute | solution.py:567
  35.3 0.1 collective-permute-start.3
  35.4 4.6 %own_0.1 = (bf16[4,6,512,128]{3,2,1,0:T(8,128)(2,1)S(1)}, f32[192,384]{1,0:T(8,128)S(1)}, f32[128,384]{1,0:T(8,128)S(1)}) custom-call(f32[48,384]{1,0:T(8,128)S(1)} %get-tuple-element.27.m0, f32[56,384]{1,0:T(8,128)S(1)} %get-tuple-element.22.tgt.pack), custom_call_target="tpu_custom_call" | custom-call | tf_op jit(solution)/shard_map/own_0/pallas_call | solution.py:542
  40.0 0.0 collective-permute-done.4.m0b
  40.0 0.0 collective-permute-done.3.m0a
  40.0 5.8 %near_0.1 = (f32[24,384]{1,0:T(8,128)S(1)}, bf16[4,18,512,128]{3,2,1,0:T(8,128)(2,1)S(1)}, s32[37]{0:T(128)S(1)}) custom-call(f32[48,384]{1,0:T(8,128)S(1)} %get-tuple-element.27.m0, f32[48,384]{1,0:T(8,128)S(1)} %collective-permute-done.3.m0a, f32[48,384]{1,0:T(8,128)S(1)} %collective-permute-done.4.m0b, f32[56,384]{1,0:T(8,128)S(1)} %get-tuple-element.22.tgt.pack, ...), custom_call_target="tpu_custom_call" | custom-call | tf_op jit(solution)/shard_map/near_0/pallas_call | solution.py:542
  45.8 1.9 %collective-permute-start.6 = (f32[24,384]{1,0:T(8,128)S(1)}, f32[24,384]{1,0:T(8,128)S(1)}, u32[]{:S(2)}, u32[]{:S(2)}) collective-permute-start(f32[24,384]{1,0:T(8,128)S(1)} %get-tuple-element.31.mu), channel_id=1, source_target_pairs={{1,2},{2,1},{3,4},{4,3},{5,6},{6,5},{7,8},{8,7},{9,10},{10,9},{11,... | collective-permute-start | bytes 110600 | tf_op jit(solution)/shard_map/ppermute | solution.py:567
  47.7 0.7 %collective-permute-start.5 = (f32[24,384]{1,0:T(8,128)S(1)}, f32[24,384]{1,0:T(8,128)S(1)}, u32[]{:S(2)}, u32[]{:S(2)}) collective-permute-start(f32[24,384]{1,0:T(8,128)S(1)} %get-tuple-element.31.mu), channel_id=1, source_target_pairs={{0,1},{1,0},{2,3},{3,2},{4,5},{5,4},{6,7},{7,6},{8,9},{9,8},{10,11... | collective-permute-start | bytes 110600 | tf_op jit(solution)/shard_map/ppermute | solution.py:566
  48.4 1.5 %own_1.1 = (f32[192,384]{1,0:T(8,128)S(1)}, f32[128,384]{1,0:T(8,128)S(1)}) custom-call(f32[24,384]{1,0:T(8,128)S(1)} %get-tuple-element.31.mu, f32[48,384]{1,0:T(8,128)S(1)} %get-tuple-element.27.m0, bf16[4,6,512,128]{3,2,1,0:T(8,128)(2,1)S(1)} %get-tuple-element.32.tensors), custom_call_target="tpu_custom_call" | custom-call | tf_op jit(solution)/shard_map/own_1/pallas_call | solution.py:542
  49.9 2.1 %collective-permute-done.6.mub = f32[24,384]{1,0:T(8,128)S(1)} collective-permute-done((f32[24,384]{1,0:T(8,128)S(1)}, f32[24,384]{1,0:T(8,128)S(1)}, u32[]{:S(2)}, u32[]{:S(2)}) %collective-permute-start.6) | collective-permute-done | bytes 36896 | tf_op jit(solution)/shard_map/ppermute | solution.py:567
  51.9 0.0 collective-permute-done.5.mua
  51.9 2.7 %near_1.1.mu = f32[24,384]{1,0:T(8,128)S(1)} custom-call(f32[24,384]{1,0:T(8,128)S(1)} %collective-permute-done.5.mua, f32[24,384]{1,0:T(8,128)S(1)} %collective-permute-done.6.mub, f32[48,384]{1,0:T(8,128)S(1)} %get-tuple-element.27.m0, f32[48,384]{1,0:T(8,128)S(1)} %collective-permute-done.3.m0a, f32[48,384]{1,0:T(8,128)S(1)} %collective-permute-done.4.m0b, ...), custom_call_target="tpu_custom_call" | custom-call | tf_op jit(solution)/shard_map/near_1/pallas_call | solution.py:542
  54.7 2.0 %collective-permute-start.8 = (f32[24,384]{1,0:T(8,128)S(1)}, f32[24,384]{1,0:T(8,128)S(1)}, u32[]{:S(2)}, u32[]{:S(2)}) collective-permute-start(f32[24,384]{1,0:T(8,128)S(1)} %near_1.1.mu), channel_id=1, source_target_pairs={{1,2},{2,1},{3,4},{4,3},{5,6},{6,5},{7,8},{8,7},{9,10},{10,9},{11,... | collective-permute-start | bytes 110600 | tf_op jit(solution)/shard_map/ppermute | solution.py:567
  56.7 0.1 collective-permute-start.7
  56.8 1.5 %own_2.1 = (f32[192,384]{1,0:T(8,128)S(1)}, f32[128,384]{1,0:T(8,128)S(1)}) custom-call(f32[24,384]{1,0:T(8,128)S(1)} %near_1.1.mu, f32[48,384]{1,0:T(8,128)S(1)} %get-tuple-element.27.m0, bf16[4,6,512,128]{3,2,1,0:T(8,128)(2,1)S(1)} %get-tuple-element.32.tensors), custom_call_target="tpu_custom_call" | custom-call | tf_op jit(solution)/shard_map/own_2/pallas_call | solution.py:542
  58.3 2.5 %collective-permute-done.8.mub = f32[24,384]{1,0:T(8,128)S(1)} collective-permute-done((f32[24,384]{1,0:T(8,128)S(1)}, f32[24,384]{1,0:T(8,128)S(1)}, u32[]{:S(2)}, u32[]{:S(2)}) %collective-permute-start.8) | collective-permute-done | bytes 36896 | tf_op jit(solution)/shard_map/ppermute | solution.py:567
  60.8 0.0 collective-permute-done.7.mua
  60.9 3.9 %final.1 = (f32[3,16,384]{2,1,0:T(8,128)}, f32[3,4,384]{2,1,0:T(4,128)}) custom-call(f32[24,384]{1,0:T(8,128)S(1)} %collective-permute-done.7.mua, f32[24,384]{1,0:T(8,128)S(1)} %collective-permute-done.8.mub, f32[48,384]{1,0:T(8,128)S(1)} %get-tuple-element.27.m0, f32[48,384]{1,0:T(8,128)S(1)} %collective-permute-done.3.m0a, ...), custom_call_target="tpu_custom_call" | custom-call | tf_op jit(solution)/shard_map/final/pallas_call | solution.py:542
Async XLA Ops:
  0.6 0.9 %copy-start = (f32[16,3,384]{2,0,1:T(8,128)S(1)}, f32[16,3,384]{2,0,1:T(8,128)}, u32[]{:S(2)}) copy-start(f32[16,3,384]{2,0,1:T(8,128)} %param.4) | copy-start | bytes 221188
  1.5 0.7 %copy-start.1 = (f32[384]{0:T(512)S(1)}, f32[384]{0:T(512)}, u32[]{:S(2)}) copy-start(f32[384]{0:T(512)} %charge.1) | copy-start | bytes 4612
  2.2 0.7 %copy-start.2 = (f32[384]{0:T(512)S(1)}, f32[384]{0:T(512)}, u32[]{:S(2)}) copy-start(f32[384]{0:T(512)} %polar.1) | copy-start | bytes 4612
  2.9 0.7 %copy-start.3 = (s32[384]{0:T(512)S(1)}, s32[384]{0:T(512)}, u32[]{:S(2)}) copy-start(s32[384]{0:T(512)} %mol.1) | copy-start | bytes 4612
  4.1 13.4 %collective-permute-start.1 = (f32[56,384]{1,0:T(8,128)S(1)}, f32[56,384]{1,0:T(8,128)S(1)}, u32[]{:S(2)}, u32[]{:S(2)}) collective-permute-start(f32[56,384]{1,0:T(8,128)S(1)} %get-tuple-element.22.tgt.pack), channel_id=1, source_target_pairs={{1,2},{2,1},{3,4},{4,3},{5,6},{6,5},{7,8},{8,7},{9,10},{10,9},{11,... | collective-permute-start | bytes 258056 | tf_op jit(solution)/shard_map/ppermute | solution.py:567
  7.8 9.7 %collective-permute-start = (f32[56,384]{1,0:T(8,128)S(1)}, f32[56,384]{1,0:T(8,128)S(1)}, u32[]{:S(2)}, u32[]{:S(2)}) collective-permute-start(f32[56,384]{1,0:T(8,128)S(1)} %get-tuple-element.22.tgt.pack), channel_id=1, source_target_pairs={{0,1},{1,0},{2,3},{3,2},{4,5},{5,4},{6,7},{7,6},{8,9},{9,8},{10,11... | collective-permute-start | bytes 258056 | tf_op jit(solution)/shard_map/ppermute | solution.py:566
  27.1 3.3 %collective-permute-start.2 = (f32[48,384]{1,0:T(8,128)S(1)}, f32[48,384]{1,0:T(8,128)S(1)}, u32[]{:S(2)}, u32[]{:S(2)}) collective-permute-start(f32[48,384]{1,0:T(8,128)S(1)} %get-tuple-element.26.msg), channel_id=1, source_target_pairs={{0,16},{16,0},{1,17},{17,1},{2,18},{18,2},{3,19},{19,3},{4,20},{20... | collective-permute-start | bytes 221192 | tf_op jit(solution)/shard_map/ppermute | solution.py:600
  30.6 9.4 %collective-permute-start.4 = (f32[48,384]{1,0:T(8,128)S(1)}, f32[48,384]{1,0:T(8,128)S(1)}, u32[]{:S(2)}, u32[]{:S(2)}) collective-permute-start(f32[48,384]{1,0:T(8,128)S(1)} %get-tuple-element.27.m0), channel_id=1, source_target_pairs={{1,2},{2,1},{3,4},{4,3},{5,6},{6,5},{7,8},{8,7},{9,10},{10,9},{11,... | collective-permute-start | bytes 221192 | tf_op jit(solution)/shard_map/ppermute | solution.py:567
  35.3 4.7 %collective-permute-start.3 = (f32[48,384]{1,0:T(8,128)S(1)}, f32[48,384]{1,0:T(8,128)S(1)}, u32[]{:S(2)}, u32[]{:S(2)}) collective-permute-start(f32[48,384]{1,0:T(8,128)S(1)} %get-tuple-element.27.m0), channel_id=1, source_target_pairs={{0,1},{1,0},{2,3},{3,2},{4,5},{5,4},{6,7},{7,6},{8,9},{9,8},{10,11... | collective-permute-start | bytes 221192 | tf_op jit(solution)/shard_map/ppermute | solution.py:566
  45.8 6.2 %collective-permute-start.6 = (f32[24,384]{1,0:T(8,128)S(1)}, f32[24,384]{1,0:T(8,128)S(1)}, u32[]{:S(2)}, u32[]{:S(2)}) collective-permute-start(f32[24,384]{1,0:T(8,128)S(1)} %get-tuple-element.31.mu), channel_id=1, source_target_pairs={{1,2},{2,1},{3,4},{4,3},{5,6},{6,5},{7,8},{8,7},{9,10},{10,9},{11,... | collective-permute-start | bytes 110600 | tf_op jit(solution)/shard_map/ppermute | solution.py:567
  47.7 4.2 %collective-permute-start.5 = (f32[24,384]{1,0:T(8,128)S(1)}, f32[24,384]{1,0:T(8,128)S(1)}, u32[]{:S(2)}, u32[]{:S(2)}) collective-permute-start(f32[24,384]{1,0:T(8,128)S(1)} %get-tuple-element.31.mu), channel_id=1, source_target_pairs={{0,1},{1,0},{2,3},{3,2},{4,5},{5,4},{6,7},{7,6},{8,9},{9,8},{10,11... | collective-permute-start | bytes 110600 | tf_op jit(solution)/shard_map/ppermute | solution.py:566
  54.7 6.2 %collective-permute-start.8 = (f32[24,384]{1,0:T(8,128)S(1)}, f32[24,384]{1,0:T(8,128)S(1)}, u32[]{:S(2)}, u32[]{:S(2)}) collective-permute-start(f32[24,384]{1,0:T(8,128)S(1)} %near_1.1.mu), channel_id=1, source_target_pairs={{1,2},{2,1},{3,4},{4,3},{5,6},{6,5},{7,8},{8,7},{9,10},{10,9},{11,... | collective-permute-start | bytes 110600 | tf_op jit(solution)/shard_map/ppermute | solution.py:567
  56.7 4.1 %collective-permute-start.7 = (f32[24,384]{1,0:T(8,128)S(1)}, f32[24,384]{1,0:T(8,128)S(1)}, u32[]{:S(2)}, u32[]{:S(2)}) collective-permute-start(f32[24,384]{1,0:T(8,128)S(1)} %near_1.1.mu), channel_id=1, source_target_pairs={{0,1},{1,0},{2,3},{3,2},{4,5},{5,4},{6,7},{7,6},{8,9},{9,8},{10,11... | collective-permute-start | bytes 110600 | tf_op jit(solution)/shard_map/ppermute | solution.py:566

commit v3 on v2

v3 whole, which is shorter than its diff:
```python
import functools
import math

import jax
import jax.numpy as jnp
from jax import lax
from jax.experimental import pallas as pl
from jax.experimental.pallas import tpu as pltpu
from jax.sharding import PartitionSpec as P

BEADS = 32
CONTR = 4
ITERS = 2
CUTOFF = 9.0
CUT2 = CUTOFF * CUTOFF
THOLE = 0.39
LOG2E = 1.4426950408889634
LN2 = 0.6931471805599453
L = 128
KP = 8
F32 = jnp.float32
BF16 = jnp.bfloat16
VMEM_LIMIT = 20 * 1024 * 1024


def split3(x):
    h = x.astype(BF16).astype(F32)
    r = x - h
    m = r.astype(BF16).astype(F32)
    return h, m, r - m


def dot(a, b, ca=1, cb=0):
    return lax.dot_general(a, b, (((ca,), (cb,)), ((), ())), preferred_element_type=F32)


def dot3(x, mat, cb):
    rows = x.shape[0]
    out = dot(jnp.concatenate(split3(x), 0).astype(BF16), mat, 1, cb)
    return (out[:rows] + out[rows : 2 * rows]) + out[2 * rows :]


T_SLOTS, S_SLOTS = [], []
for _a in range(3):
    T_SLOTS += [(_a, 1)] * 3 + [(3 + _a, 1)] * 2 + [(6 + _a, 1)]
    S_SLOTS += [(_a, -2), (3 + _a, -2), (6 + _a, -2), (_a, -2), (3 + _a, -2), (_a, -2)]
T_SLOTS += [(9, 1), (10, 1), (11, 1), (12, 1), (12, 1), (12, 1)]
S_SLOTS += [(12, 1), (12, 1), (12, 1), (9, 1), (10, 1), (11, 1)]
SLOT = 32
DEEP = 4 * len(T_SLOTS)
TYPES = 13


def perm_matrix(rank_row, w):
    rows = lax.broadcasted_iota(jnp.int32, (w, w), 0).astype(F32)
    return jnp.where(rows == rank_row, 1.0, 0.0).astype(BF16)


def pair_pieces(xs):
    hx, hy, hz = (split3(x) for x in xs)
    n = xs[0] * xs[0] + xs[1] * xs[1] + xs[2] * xs[2]
    parts = [hx[0], hy[0], hz[0], hx[1], hy[1], hz[1], hx[2], hy[2], hz[2]]
    return parts + list(split3(n)) + [jnp.ones_like(n)]


def store_rows(ref, tile, row, stride, value):
    for i in range(value.shape[1] // L):
        ref[tile + i, pl.ds(row, value.shape[0], stride=stride), :] = value[:, i * L : (i + 1) * L]


def slot_stack(pieces, slots, g):
    lo = g // 2 * 8
    top = lax.broadcasted_iota(jnp.int32, (8, pieces[0].shape[1]), 0) < 4
    here, there = {}, {}
    for kind, coef in slots:
        if (kind, coef) not in here:
            x = pieces[kind][lo : lo + 8]
            here[kind, coef] = x if coef == 1 else x * float(coef)
            there[kind, coef] = here[kind, coef] if kind == TYPES - 1 else pltpu.roll(here[kind, coef], 4, 0)
    first, second = (here, there) if g % 2 == 0 else (there, here)
    return jnp.concatenate(
        [jnp.where(top, first[slots[f]], second[slots[f + 1]]) for f in range(0, len(slots), 2)], 0
    )


def target_features(pieces, ft, count):
    for g in range(-(-count // 4)):
        stack = slot_stack(pieces, T_SLOTS, g)
        row = lax.broadcasted_iota(jnp.int32, stack.shape, 0) % 4
        for i in range(min(4, count - g * 4)):
            ft[g * 4 + i] = jnp.where(row == i, stack, 0.0).astype(BF16)


def source_features(pieces, fs, s, w, count):
    for g in range(-(-count // 4)):
        fs[g, s * w : (s + 1) * w, :] = jnp.transpose(slot_stack(pieces, S_SLOTS, g)).astype(BF16)


def sum_select(rows, count):
    lane = lax.broadcasted_iota(jnp.int32, (1, max(count * SLOT, L)), 1)
    b, r = lane // SLOT, lane % SLOT
    p, f = r // 8, r % 8
    want = jnp.where((f < 4) & (p < 3) & (b < count), (p * 4 + f) * rows + b, -1)
    row = lax.broadcasted_iota(jnp.int32, (12 * rows, lane.shape[1]), 0)
    return jnp.where(row == want, 1.0, 0.0).astype(BF16)


def center_of(xs, count):
    w = xs[0].shape[1]
    return [jnp.sum(x[:count], keepdims=True) * (1.0 / (count * w)) for x in xs]


def columns(misc):
    al = misc[1:2]
    good = al > 0.0
    inv = jnp.where(good, lax.rsqrt(jnp.where(good, al, 1.0)), 0.0)
    return jnp.concatenate([inv, misc[2:3], jnp.zeros_like(misc[:6])], 0)


def ranges(x, al, count, w):
    good = al > 0.0
    lo = jnp.where(good, x[:count], 1e30)
    hi = jnp.where(good, x[:count], -1e30)
    out = []
    for i in range(w // L):
        out.append((jnp.min(lo[:, i * L : (i + 1) * L]), jnp.max(hi[:, i * L : (i + 1) * L])))
    return out


def near_list(lst, size, trange, sranges):
    lst[1] = 0
    lst[1 + size] = 0
    count = jnp.int32(0)
    sj = 0
    for slab in sranges:
        for smin, smax in slab:
            for ti, (tmin, tmax) in enumerate(trange):
                near = (smin - tmax < CUTOFF) & (tmin - smax < CUTOFF)
                lst[1 + count] = sj * L
                lst[1 + size + count] = ti * L
                count = count + near.astype(jnp.int32)
            sj += 1
    lst[0] = count


def own_blocks(nt):
    return [(i, i) for i in range(nt)], [(i, j) for i in range(nt) for j in range(i + 1, nt)]


def pair_basis(r2, q):
    safe = jnp.maximum(r2, 1e-4)
    inv = lax.rsqrt(safe)
    c = (safe * inv) * (safe * q)
    decay = jnp.exp2(c)
    v = jnp.maximum(CUT2 - r2, 0.0) * inv
    return c, decay, inv, v


def comps(ref, first, count=3):
    out = []
    for c in range(first, first + count):
        block = ref[c // 2 * 8 : c // 2 * 8 + 8]
        out.append(block if c % 2 == 0 else pltpu.roll(block, 4, 0))
    return out


def stack_comps(parts):
    top = lax.broadcasted_iota(jnp.int32, parts[0].shape, 0) < 4
    return jnp.concatenate(
        [jnp.where(top, parts[i], pltpu.roll(parts[i + 1], 4, 0)) for i in range(0, len(parts), 2)], 0
    )


def two(x):
    hi = x.astype(BF16)
    return hi, (x - hi.astype(F32)).astype(BF16)


def weights(nb, shape, rank, bead_dim):
    b = lax.broadcasted_iota(jnp.int32, shape, bead_dim)
    k = lax.broadcasted_iota(jnp.int32, shape, 1 - bead_dim)
    turn = k * (BEADS // CONTR) - (rank * nb + b) + 2 * BEADS
    turn = (turn + BEADS // 2) % BEADS - BEADS // 2
    cos = jnp.cos(turn.astype(F32) * (2.0 * math.pi / BEADS))
    return jnp.where((k < CONTR) & (b < nb), 2.0 * cos * (1.0 + cos), 0.0)


def hdot(a, b):
    return jnp.dot(a, b, precision=lax.Precision.HIGHEST, preferred_element_type=F32)


def pack_kernel(nb, nbp, w, pos, charge, polar, mol, out, scr, posv, chargev, polarv, molv, sem):
    copies = [
        pltpu.make_async_copy(src, dst, sem.at[i])
        for i, (src, dst) in enumerate(((pos, posv), (charge, chargev), (polar, polarv), (mol, molv)))
    ]
    for c in copies:
        c.start()
    scr[...] = jnp.zeros_like(scr)
    for c in copies:
        c.wait()
    for a in range(3):
        scr[a * nbp : a * nbp + nb, :] = posv[a]
    base = 3 * nbp
    scr[base : base + 1, :] = chargev[...].reshape(1, w)
    scr[base + 1 : base + 2, :] = polarv[...].reshape(1, w)
    scr[base + 2 : base + 3, :] = molv[...].reshape(1, w).astype(F32)
    x = scr[...]
    key = jnp.sum(x[:nbp], 0, keepdims=True)
    col = jnp.transpose(jnp.broadcast_to(key, (8, w)))[:, :1]
    jj = lax.broadcasted_iota(jnp.int32, (w, w), 0)
    ii = lax.broadcasted_iota(jnp.int32, (w, w), 1)
    before = (col < key) | ((col == key) & (jj < ii))
    rank = jnp.sum(jnp.where(before, 1.0, 0.0), 0, keepdims=True)
    out[...] = dot3(x, perm_matrix(rank, w), 1)
    out[base + 3 : base + 4, :] = rank


def perm_sources(nb, nbp, w, src, pieces, xs, s, sel_r, fs, rt, cols):
    base = 3 * nbp
    misc = src[base : base + 8, :]
    source_features(pieces, fs, s, w, nb)
    q = jnp.broadcast_to(misc[0:1] * (1.0 / (CUT2 * CUT2)), xs[0].shape)
    feats = [split3(v) for v in (xs[0] * q, xs[1] * q, xs[2] * q, q)]
    stack = jnp.concatenate([feats[f][p] for p in range(3) for f in range(4)], 0)
    rt[:, s * w : (s + 1) * w] = dot(sel_r, stack.astype(BF16), 0, 0).astype(BF16)
    cols[s * w : (s + 1) * w, :] = jnp.transpose(columns(misc))
    return misc[1:2]


class Item:
    def __init__(self, e, s0, t0, g=0, sym=False):
        self.e, self.s0, self.t0, self.g, self.sym = e, s0, t0, g, sym

    def at(self, g):
        return Item(self.e, self.s0, self.t0, g, self.sym)


def perm_run(items, head, tail, nb, fs, ft, rt, qbuf, acc, r2s, fbs):
    def sums(it, f):
        for j in range(4):
            r0 = (it.g * 4 + j) * SLOT
            r = rt[r0 : r0 + SLOT, pl.ds(it.s0, L)]
            pair = f[j]
            acc[r0 : r0 + SLOT, pl.ds(it.t0, L)] += dot(jnp.concatenate([r, r], 1), pair)
            if it.sym:
                back = dot(rt[r0 : r0 + SLOT, pl.ds(it.t0, L)], pair, 1, 1)
                acc[r0 : r0 + SLOT, pl.ds(it.s0, L)] += back[:, :L] + back[:, L:]

    def functions(it, r2, f):
        for j in range(4):
            c, decay, inv, v = pair_basis(r2[j], qbuf[it.e])
            hi, lo = two((v * v) * (inv * (1.0 - decay)))
            f[j, :L, :] = hi
            f[j, L:, :] = lo

    def distances(it, r2):
        lhs = fs[it.g, pl.ds(it.s0, L), :]
        for j in range(4):
            r2[j] = dot(lhs, ft[it.g * 4 + j, :, pl.ds(it.t0, L)])

    if not items:
        if tail is not None:
            distances(tail, r2s[0])
        if head is not None:
            sums(head, fbs[1])
        return
    for i, it in enumerate(items):
        functions(it, r2s[i % 2], fbs[i % 2])
        after = items[i + 1] if i + 1 < len(items) else tail
        if after is not None:
            distances(after, r2s[(i + 1) % 2])
        before = items[i - 1] if i > 0 else head
        if before is not None:
            sums(before, fbs[(i - 1) % 2])


def perm_own_pairs(blocks, nb, *rest):
    items = [
        Item(e, s * L, t * L, g, s != t) for e, (s, t) in enumerate(blocks) for g in range(nb // 4)
    ]
    args = rest
    perm_run([], None, items[0], nb, *args)
    odd = len(items) % 2
    perm_run(items[: len(items) - odd], None, items[-1] if odd else None, nb, *args)
    if odd:
        perm_run([items[-1]], items[-2] if len(items) > 1 else None, None, nb, *args)
        fbs = args[-1]
        fbs[1][...] = fbs[0][...]
    perm_run([], items[-1], None, nb, *args)


def perm_near_pairs(n, lst, size, nb, *rest):
    fbs = rest[-1]
    fbs[1][...] = jnp.zeros_like(fbs[1])
    groups = nb // 4

    def entry(i):
        good = i < n
        e = jnp.where(good, i, 0)
        return jnp.where(good, e, size), lst[1 + e], lst[1 + size + e]

    def item(it):
        return Item(it[0], pl.multiple_of(it[1], L), pl.multiple_of(it[2], L))

    def step(i, carry):
        before, first, second, after = carry
        later = (entry(2 * i + 3), entry(2 * i + 4))
        items = [item(it).at(g) for it in (first, second) for g in range(groups)]
        perm_run(items, item(before).at(groups - 1), item(after).at(0), nb, *rest)
        return (second, after) + later

    start = entry(0)
    perm_run([], None, item(start).at(0), nb, *rest)
    last = lax.fori_loop(0, (n + 1) // 2, step, (start, start, entry(1), entry(2)))[0]
    perm_run([], item(last).at(groups - 1), None, nb, *rest)


def block_q(n, first, lst, size, own, cols, qrow, qbuf):
    def one(i, carry):
        e = first + i
        s0 = pl.multiple_of(lst[1 + e], L)
        t0 = pl.multiple_of(lst[1 + size + e], L)
        cc = cols[pl.ds(s0, L), :]
        row = qrow[:, pl.ds(t0, L)]
        q = cc[:, 0:1] * row[0:1]
        if own:
            q = jnp.where(cc[:, 1:2] == row[1:2], 0.0, q)
        qbuf[e] = q
        return carry

    lax.fori_loop(0, n, one, 0)
    qbuf[size] = jnp.zeros_like(qbuf[size])


def q_rows(misc, qrow):
    c = columns(misc)
    qrow[...] = c
    qrow[0:1, :] = c[0:1] * (-THOLE * LOG2E)


def fixed_list(lst, size, blocks):
    lst[0] = len(blocks)
    for e, (s, t) in enumerate(blocks):
        lst[1 + e] = s * L
        lst[1 + size + e] = t * L


def perm_own_kernel(nb, nbp, w, tgt, acc, ft, order, keep, fs, rt, cols, qrow, qbuf, r2a, r2b, fa, fb, lst):
    nt = w // L
    base = 3 * nbp
    sel_r = sum_select(nbp, nb)
    acc[...] = jnp.zeros_like(acc)
    order[...] = perm_matrix(tgt[base + 3 : base + 4, :], w)
    keep[...] = tgt[...]
    coords = [tgt[a * nbp : (a + 1) * nbp, :] for a in range(3)]
    xt = [x - c for x, c in zip(coords, center_of(coords, nb))]
    pieces = pair_pieces(xt)
    target_features(pieces, ft, nb)
    perm_sources(nb, nbp, w, tgt, pieces, xt, 0, sel_r, fs, rt, cols)
    q_rows(tgt[base : base + 8, :], qrow)
    diag, off = own_blocks(nt)
    size = len(diag) + len(off)
    fixed_list(lst, size, diag + off)
    block_q(size, 0, lst, size, True, cols, qrow, qbuf)
    perm_own_pairs(diag + off, nb, fs, ft, rt, qbuf, acc, (r2a, r2b), (fa, fb))


def perm_near_kernel(
    nb, nbp, w, tgt, srca, srcb, ft, acc_in, order, perm_out, msg_out, acc,
    fs, rt, cols, qrow, qbuf, r2a, r2b, fa, fb, lst,
):
    nt = w // L
    base = 3 * nbp
    coords = [tgt[a * nbp : (a + 1) * nbp, :] for a in range(3)]
    center = center_of(coords, nb)
    xt = [x - c for x, c in zip(coords, center)]
    sel_r = sum_select(nbp, nb)
    sranges = []
    for s, src in enumerate((srca, srcb)):
        xs = [src[a * nbp : (a + 1) * nbp, :] - center[a] for a in range(3)]
        al = perm_sources(nb, nbp, w, src, pair_pieces(xs), xs, s, sel_r, fs, rt, cols)
        sranges.append(ranges(xs[0], al, nb, w))
    size = 2 * nt * nt
    near_list(lst, size, ranges(xt[0], tgt[base + 1 : base + 2, :], nb, w), sranges)
    q_rows(tgt[base : base + 8, :], qrow)
    n = lst[0]
    block_q(n, 0, lst, size, False, cols, qrow, qbuf)
    perm_near_pairs(n, lst, size, nb, fs, ft, rt, qbuf, acc, (r2a, r2b), (fa, fb))
    if nb < nbp:
        perm_out[...] = jnp.zeros_like(perm_out)
    for b in range(nb):
        s = acc[b * 32 : b * 32 + 8, :] + acc[b * 32 + 8 : b * 32 + 16, :]
        s = s + acc[b * 32 + 16 : b * 32 + 24, :]
        for a in range(3):
            row = xt[a][b : b + 1] * s[3:4] - s[a : a + 1]
            perm_out[a * nbp + b : a * nbp + b + 1, :] = row
    wc = weights(nb, (KP, nbp), lax.axis_index("bead"), 1) * (1.0 / BEADS)
    parts = [hdot(wc, perm_out[a * nbp : (a + 1) * nbp, :]) for a in range(3)]
    parts += [hdot(wc, coords[a]) for a in range(3)]
    msg_out[...] = dot3(stack_comps(parts), order[...], 0)


def start_kernel(nbp, w, msg, other, order, pack, m0, cf):
    both = dot3(msg[...] + other[...], order[...], 1)
    cf[...] = both[: 2 * KP]
    row = lax.broadcasted_iota(jnp.int32, both.shape, 0)
    m0[...] = jnp.where(row < 3 * CONTR, both * pack[3 * nbp + 1 : 3 * nbp + 2, :], both)


def centered(m, center):
    return [x - c for x, c in zip(comps(m, 3), center)]


def own_center(m):
    return center_of(comps(m, 3), CONTR)


def tensor_pairs(n, lst, size, fs, ft, qbuf, r2a, r2b, tensors):
    def where_is(i):
        e = jnp.maximum(jnp.minimum(i, n - 1), 0)
        return e, pl.multiple_of(lst[1 + e], L), pl.multiple_of(lst[1 + size + e], L)

    def tensor(i, r2):
        e, _, _ = where_is(i)
        for k in range(CONTR):
            c, decay, inv, v = pair_basis(r2[k], qbuf[e])
            l3 = 1.0 - decay
            l5 = l3 + (c * LN2) * decay
            w3 = (v * v) * inv
            w5 = w3 * (inv * inv)
            a_hi, a_lo = two(w5 * l5)
            b_hi, b_lo = two(w3 * l3)
            tensors[k, e, 0:L, :] = a_hi
            tensors[k, e, L : 2 * L, :] = a_lo
            tensors[k, e, 2 * L : 3 * L, :] = b_hi
            tensors[k, e, 3 * L : 4 * L, :] = b_lo

    def distances(i, r2):
        _, s0, t0 = where_is(i)
        lhs = fs[0, pl.ds(s0, L), :]
        for k in range(CONTR):
            r2[k] = dot(lhs, ft[k, :, pl.ds(t0, L)])

    def step(p, carry):
        distances(2 * p + 1, r2b)
        tensor(2 * p, r2a)
        distances(2 * p + 2, r2a)
        tensor(2 * p + 1, r2b)
        return carry

    distances(0, r2a)
    lax.fori_loop(0, (n + 1) // 2, step, 0)


def induce_features(mu, x, le, s, w):
    scale = 1.0 / (CUT2 * CUT2)
    m = [v * scale for v in comps(mu, 0)]
    dotted = x[0] * m[0] + x[1] * m[1] + x[2] * m[2]
    feats = m + [dotted] + [x[a] * m[b] for a in range(3) for b in range(3)]
    feats += [x[a] * dotted for a in range(3)]
    tile = s * (w // L)
    for f, v in enumerate(feats):
        for p, piece in enumerate(split3(v)):
            store_rows(le, tile, p * 16 + f, L, piece[:CONTR])
            if f < 3:
                store_rows(le, tile, 64 + p * 8 + f, L, piece[:CONTR])


def twice(x):
    x = x.astype(BF16)
    return jnp.concatenate([x, x], 1)


def own_sums(w, mu, m0, tensors, acc_a, acc_b, le):
    nt = w // L
    induce_features(mu, centered(m0, own_center(m0)), le, 0, w)
    acc_a[...] = jnp.zeros_like(acc_a)
    acc_b[...] = jnp.zeros_like(acc_b)
    diag, off = own_blocks(nt)
    for e, (s, t) in enumerate(diag + off):
        s0, t0 = s * L, t * L
        for k in range(CONTR):
            ra, rb = k * L, k * L + 64
            pa, pb = tensors[k, e, 0 : 2 * L, :], tensors[k, e, 2 * L : 4 * L, :]
            a0, b0 = k * 48, k * 32
            acc_a[a0 : a0 + 48, t0 : t0 + L] += dot(twice(le[s, ra : ra + 48, :]), pa)
            acc_b[b0 : b0 + 32, t0 : t0 + L] += dot(twice(le[s, rb : rb + 32, :]), pb)
            if s != t:
                back = dot(le[t, ra : ra + 48, :].astype(BF16), pa, 1, 1)
                acc_a[a0 : a0 + 48, s0 : s0 + L] += back[:, :L] + back[:, L:]
                back = dot(le[t, rb : rb + 32, :].astype(BF16), pb, 1, 1)
                acc_b[b0 : b0 + 32, s0 : s0 + L] += back[:, :L] + back[:, L:]


def near_sums(w, mus, cps, m0, tensors, lst, acc_a, acc_b, le, ev, bring=None):
    nt = w // L
    center = own_center(m0)
    for s, (mu, cp) in enumerate(zip(mus, cps)):
        induce_features(mu, centered(cp, center), le, s, w)
    size = 2 * nt * nt
    if bring is not None:
        bring.wait()

    def step(e, carry):
        tile = lst[1 + e] // L
        t0 = pl.multiple_of(lst[1 + size + e], L)
        for k in range(CONTR):
            ra, rb = k * L, k * L + 64
            a0, b0 = k * 48, k * 32
            fa, fb = twice(le[tile, ra : ra + 48, :]), twice(le[tile, rb : rb + 32, :])
            acc_a[a0 : a0 + 48, pl.ds(t0, L)] += dot(fa, tensors[k, e, 0 : 2 * L, :])
            acc_b[b0 : b0 + 32, pl.ds(t0, L)] += dot(fb, tensors[k, e, 2 * L : 4 * L, :])
        return carry

    lax.fori_loop(0, lst[0], step, 0)
    ev[...] = jnp.zeros_like(ev)
    xt = centered(m0, center)
    for k in range(CONTR):
        o = k * 48
        sa = acc_a[o : o + 16, :] + acc_a[o + 16 : o + 32, :] + acc_a[o + 32 : o + 48, :]
        o = k * 32
        sb = acc_b[o : o + 8, :] + acc_b[o + 8 : o + 16, :] + acc_b[o + 16 : o + 24, :]
        x = [v[k : k + 1] for v in xt]
        along = x[0] * sa[0:1] + x[1] * sa[1:2] + x[2] * sa[2:3] - sa[3:4]
        for a in range(3):
            cross = sum(x[b] * sa[4 + 3 * a + b : 5 + 3 * a + b] for b in range(3))
            full = x[a] * along - cross + sa[13 + a : 14 + a]
            ev[a * CONTR + k : a * CONTR + k + 1, :] = 3.0 * full - sb[a : a + 1]


def own_first_kernel(nbp, w, m0, pack, tensors, acc_a, acc_b, le, fs, ft, cols, qrow, qbuf, r2a, r2b, lst):
    misc = pack[3 * nbp : 3 * nbp + 8, :]
    pieces = pair_pieces(centered(m0, own_center(m0)))
    target_features(pieces, ft, CONTR)
    source_features(pieces, fs, 0, w, CONTR)
    cols[...] = jnp.transpose(columns(misc))
    q_rows(misc, qrow)
    diag, off = own_blocks(w // L)
    size = len(diag) + len(off)
    fixed_list(lst, size, diag + off)
    block_q(size, 0, lst, size, True, cols, qrow, qbuf)
    tensor_pairs(size, lst, size, fs, ft, qbuf, r2a, r2b, tensors)
    own_sums(w, m0, m0, tensors, acc_a, acc_b, le)


def own_kernel(w, mu, m0, tensors, acc_a, acc_b, le):
    own_sums(w, mu, m0, tensors, acc_a, acc_b, le)


def update(pack, nbp, cf, ev):
    return pack[3 * nbp + 1 : 3 * nbp + 2, :] * (cf[...] + ev[...])


def near_first_kernel(
    nbp, w, m0, m0a, m0b, pack, packa, packb, cf, acc_a_in, acc_b_in,
    mu_out, tensors, lst, acc_a, acc_b, fs, ft, cols, qrow, qbuf, r2a, r2b, le, ev,
):
    nt = w // L
    base = 3 * nbp
    center = own_center(m0)
    xt = centered(m0, center)
    target_features(pair_pieces(xt), ft, CONTR)
    sranges = []
    for s, (m, pk) in enumerate(((m0a, packa), (m0b, packb))):
        misc = pk[base : base + 8, :]
        xs = centered(m, center)
        source_features(pair_pieces(xs), fs, s, w, CONTR)
        cols[s * w : (s + 1) * w, :] = jnp.transpose(columns(misc))
        sranges.append(ranges(xs[0], misc[1:2], CONTR, w))
    misc = pack[base : base + 8, :]
    size = 2 * nt * nt
    near_list(lst, size, ranges(xt[0], misc[1:2], CONTR, w), sranges)
    q_rows(misc, qrow)
    n = lst[0]
    block_q(n, 0, lst, size, False, cols, qrow, qbuf)
    tensor_pairs(n, lst, size, fs, ft, qbuf, r2a, r2b, tensors)
    near_sums(w, [m0a, m0b], [m0a, m0b], m0, tensors, lst, acc_a, acc_b, le, ev)
    mu_out[...] = update(pack, nbp, cf, ev)


def near_kernel(
    nbp, w, mua, mub, m0, m0a, m0b, pack, cf, acc_a_in, acc_b_in, tensors, lst_hbm, mu_out, acc_a, acc_b, le, ev, lst, sem,
):
    bring = pltpu.make_async_copy(lst_hbm, lst, sem)
    bring.start()
    near_sums(w, [mua, mub], [m0a, m0b], m0, tensors, lst, acc_a, acc_b, le, ev, bring)
    mu_out[...] = update(pack, nbp, cf, ev)


def last_own_kernel(w, mu, m0, tensors, perm, order, acc_a, acc_b, perm_out, le):
    own_sums(w, mu, m0, tensors, acc_a, acc_b, le)
    perm_out[...] = dot3(perm[...], order[...], 0)


def final_kernel(
    nb, nbp, w, mua, mub, m0, m0a, m0b, mu, perm, order, acc_a_in, acc_b_in, tensors, lst_hbm,
    total_out, dip_out, acc_a, acc_b, le, ev, lst, sem,
):
    bring = pltpu.make_async_copy(lst_hbm, lst, sem)
    bring.start()
    near_sums(w, [mua, mub], [m0a, m0b], m0, tensors, lst, acc_a, acc_b, le, ev, bring)
    out = dot3(jnp.concatenate([ev[...], mu[...]], 0), order[...], 0)
    us = weights(nb, (nbp, KP), lax.axis_index("bead"), 0) * (1.0 / CONTR)
    for a, v in enumerate(comps(out, 0)):
        total_out[a] = (perm[a * nbp : (a + 1) * nbp, :] + hdot(us, v))[:nb]
        d0 = 2 * KP + a * CONTR
        dip_out[a] = out[d0 : d0 + CONTR]


def swap_pairs(count, first):
    pairs = []
    for i in range(first, count - 1, 2):
        pairs += [(i, i + 1), (i + 1, i)]
    return pairs


def call(kernel, outs, name, scratch, args, any_in=(), smem_out=(), hbm_in=(), alias=None):
    smem = pl.BlockSpec(memory_space=pltpu.SMEM)
    vmem = pl.BlockSpec(memory_space=pltpu.VMEM)
    hbm = pl.BlockSpec(memory_space=pltpu.HBM)
    return pl.pallas_call(
        kernel,
        out_shape=[jax.ShapeDtypeStruct(s, d) for s, d in outs],
        in_specs=[pl.BlockSpec(memory_space=pl.ANY) if i in any_in else hbm if i in hbm_in else vmem for i in range(len(args))],
        out_specs=[smem if i in smem_out else vmem for i in range(len(outs))],
        scratch_shapes=list(scratch),
        input_output_aliases=alias or {},
        compiler_params=pltpu.CompilerParams(vmem_limit_bytes=VMEM_LIMIT),
        name=name,
    )(*args)


def body(positions, charges, polar, molecule):
    nb, _, w = positions.shape
    nbp = -(-nb // 16) * 16
    nt = w // L
    nbead = lax.axis_size("bead")
    nspace = lax.axis_size("space")
    rows = 3 * nbp + 8
    own_size = nt * (nt + 1) // 2
    near_size = 2 * nt * nt
    part = functools.partial

    def exchange(x):
        near = lax.ppermute(x, "space", swap_pairs(nspace, 0))
        far = lax.ppermute(x, "space", swap_pairs(nspace, 1))
        return near, far

    raw = (jnp.transpose(positions, (1, 0, 2)), charges, polar, molecule)
    (pack,) = call(
        part(pack_kernel, nb, nbp, w), [((rows, w), F32)], "pack",
        [
            pltpu.VMEM((rows, w), F32),
            pltpu.VMEM((3, nb, w), F32),
            pltpu.VMEM((w,), F32),
            pltpu.VMEM((w,), F32),
            pltpu.VMEM((w,), jnp.int32),
            pltpu.SemaphoreType.DMA((4,)),
        ],
        tuple(pltpu.with_memory_space_constraint(v, pltpu.HBM) for v in raw), hbm_in=(0, 1, 2, 3),
    )
    packa, packb = exchange(pack)

    def pair_scratch(nsrc, blocks):
        return [
            pltpu.VMEM((nsrc * w, 8), F32),
            pltpu.VMEM((8, w), F32),
            pltpu.VMEM((blocks + 1, L, L), F32),
            pltpu.VMEM((4, L, L), F32),
            pltpu.VMEM((4, L, L), F32),
        ]

    def perm_scratch(nsrc, blocks):
        return [
            pltpu.VMEM((-(-nb // 4), nsrc * w, DEEP), BF16),
            pltpu.VMEM((nb * SLOT, nsrc * w), BF16),
            *pair_scratch(nsrc, blocks),
            pltpu.VMEM((4, 2 * L, L), BF16),
            pltpu.VMEM((4, 2 * L, L), BF16),
            pltpu.SMEM((2 + 2 * blocks,), jnp.int32),
        ]

    acc, ft, order, pack = call(
        part(perm_own_kernel, nb, nbp, w),
        [((nb * SLOT, w), F32), ((nb, DEEP, w), BF16), ((w, w), BF16), ((rows, w), F32)], "perm_own",
        perm_scratch(1, own_size), (pack,),
    )
    perm, msg, _ = call(
        part(perm_near_kernel, nb, nbp, w), [((3 * nbp, w), F32), ((6 * CONTR, w), F32), ((nb * SLOT, w), F32)],
        "perm_near", perm_scratch(2, near_size), (pack, packa, packb, ft, acc, order), alias={4: 2},
    )

    if nbead == 2:
        other = lax.ppermute(msg, "bead", [(0, 1), (1, 0)])
    else:
        other = lax.psum(msg, "bead") - msg
    m0, cf = call(
        part(start_kernel, nbp, w), [((6 * CONTR, w), F32), ((2 * KP, w), F32)], "start", [], (msg, other, order, pack),
    )
    m0a, m0b = exchange(m0)

    def tensor_scratch(nsrc, blocks):
        return [
            pltpu.VMEM((1, nsrc * w, DEEP), BF16),
            pltpu.VMEM((CONTR, DEEP, w), BF16),
            *pair_scratch(nsrc, blocks),
        ]

    accs = [((CONTR * 48, w), F32), ((CONTR * 32, w), F32)]
    near_scratch = [pltpu.VMEM((2 * nt, CONTR * L, L), F32), pltpu.VMEM((2 * KP, w), F32)]
    list_scratch = [pltpu.SMEM((2 + 2 * near_size,), jnp.int32), pltpu.SemaphoreType.DMA]
    own_scratch = [pltpu.VMEM((nt, CONTR * L, L), F32)]
    t_own, acc_a, acc_b = call(
        part(own_first_kernel, nbp, w), [((CONTR, own_size, 4 * L, L), BF16)] + accs, "own_0",
        own_scratch + tensor_scratch(1, own_size) + [pltpu.SMEM((2 + 2 * own_size,), jnp.int32)],
        (m0, pack),
    )
    mu, t_nbr, lst, _, _ = call(
        part(near_first_kernel, nbp, w),
        [((2 * KP, w), F32), ((CONTR, near_size, 4 * L, L), BF16), ((2 + 2 * near_size,), jnp.int32)] + accs, "near_0",
        tensor_scratch(2, near_size) + near_scratch,
        (m0, m0a, m0b, pack, packa, packb, cf, acc_a, acc_b), smem_out=(2,), alias={7: 3, 8: 4},
    )
    for step in range(1, ITERS):
        mua, mub = exchange(mu)
        acc_a, acc_b = call(part(own_kernel, w), accs, f"own_{step}", own_scratch, (mu, m0, t_own))
        mu, _, _ = call(
            part(near_kernel, nbp, w), [((2 * KP, w), F32)] + accs, f"near_{step}", near_scratch + list_scratch,
            (mua, mub, m0, m0a, m0b, pack, cf, acc_a, acc_b, t_nbr, lst), any_in=(10,), alias={7: 1, 8: 2},
        )
    mua, mub = exchange(mu)
    acc_a, acc_b, perm = call(
        part(last_own_kernel, w), accs + [((3 * nbp, w), F32)], "own_last", own_scratch,
        (mu, m0, t_own, perm, order),
    )
    total, dipoles, _, _ = call(
        part(final_kernel, nb, nbp, w), [((3, nb, w), F32), ((3, CONTR, w), F32)] + accs, "final",
        near_scratch + list_scratch,
        (mua, mub, m0, m0a, m0b, mu, perm, order, acc_a, acc_b, t_nbr, lst), any_in=(11,), alias={8: 2, 9: 3},
    )
    return (jnp.transpose(total, (1, 0, 2)), jnp.transpose(dipoles, (1, 0, 2)))


def solution(mesh):
    in_specs = (P("bead", None, "space"), P("space"), P("space"), P("space"))
    out_specs = (P("bead", None, "space"), P(None, None, "space"))
    return jax.shard_map(body, mesh=mesh, in_specs=in_specs, out_specs=out_specs, check_vma=False)
```

time: 65 us -> 53.5 us (0.82)
  Pallas kernels: 39.9 us -> 31.6 us
  local copies, waits for them, and re-layouts: 2.92 us -> 0 us
    pallas_call x10, Pallas kernels: 39.9 us -> 31.6 us  [call(): pl.pallas_call(kernel, out_shape=[jax.ShapeDtypeStruct(s, d) for s, d in...]
    unnamed x8 -> x0, local copies, waits for them, and re-layouts: 2.92 us -> none
  transfers between devices with their start and end apart: 9 -> 9, of which waited for: 3 -> 3; matrix products, arithmetic and copies ran while one was open for 0% -> 0% of each run, Pallas kernels for 27% -> 24%
where the time goes in v3:
time: 53.5 us; the launch traced here: 53.3 us
  Pallas kernels  31.6 us (59%)
  starting transfers between devices  14.7 us (27%)
  waiting for transfers between devices  6.09 us (11%)
  between operations  0.94 us (2%)
    pallas_call x10, Pallas kernels, call(): pl.pallas_call(kernel, out_shape=[jax.ShapeDtypeStruct(s, d) for s, d in...  31.6 us
    ppermute x4, starting transfers between devices, exchange(): far = lax.ppermute(x, 'space', swap_pairs(nspace, 1))  12.5 us
    ppermute x4, waiting for transfers between devices, exchange(): far = lax.ppermute(x, 'space', swap_pairs(nspace, 1))  4.49 us
    ppermute x1, waiting for transfers between devices, body(): other = lax.ppermute(msg, 'bead', [(0, 1), (1, 0)])  1.59 us
    ppermute x1, starting transfers between devices, body(): other = lax.ppermute(msg, 'bead', [(0, 1), (1, 0)])  1.28 us
  transfers between devices with their start and end apart: 9, of which 3 were waited for; matrix products, arithmetic and copies ran while one was open for 0% of the time, Pallas kernels for 24%

profile of v3, /device:TPU:21, one launch (start us, length us, event | category | flops | bytes accessed | tf_op | source)
XLA Modules:
  0.0 53.3 jit_solution(17063422494601271819)
XLA Ops:
  0.6 1.5 %pack.1.tgt = f32[56,384]{1,0:T(8,128)S(1)} custom-call(f32[3,16,384]{2,1,0:T(8,128)} %bitcast.3, f32[384]{0:T(512)} %charge.1, f32[384]{0:T(512)} %polar.1, s32[384]{0:T(512)} %mol.1), custom_call_target="tpu_custom_call" | custom-call | tf_op jit(solution)/shard_map/pack/pallas_call | solution.py:622
  2.1 3.7 %collective-permute-start.1 = (f32[56,384]{1,0:T(8,128)S(1)}, f32[56,384]{1,0:T(8,128)S(1)}, u32[]{:S(2)}, u32[]{:S(2)}) collective-permute-start(f32[56,384]{1,0:T(8,128)S(1)} %pack.1.tgt), channel_id=1, source_target_pairs={{1,2},{2,1},{3,4},{4,3},{5,6},{6,5},{7,8},{8,7},{9,10},{10,9},{11,... | collective-permute-start | bytes 258056 | tf_op jit(solution)/shard_map/ppermute | solution.py:647
  5.8 0.1 collective-permute-start
  5.9 5.6 %perm_own.1 = (f32[512,384]{1,0:T(8,128)S(1)}, bf16[16,96,384]{2,1,0:T(8,128)(2,1)S(1)}, bf16[384,384]{1,0:T(8,128)(2,1)S(1)}, f32[56,384]{1,0:T(8,128)S(1)}) custom-call(f32[56,384]{1,0:T(8,128)S(1)} %pack.1.tgt), custom_call_target="tpu_custom_call" | custom-call | tf_op jit(solution)/shard_map/perm_own/pallas_call | solution.py:622
  11.5 0.0 collective-permute-done.1.srcb.packb
  11.5 0.0 collective-permute-done.srca.packa
  11.5 7.0 %perm_near.1 = (f32[48,384]{1,0:T(8,128)S(1)}, f32[24,384]{1,0:T(8,128)S(1)}, f32[512,384]{1,0:T(8,128)S(1)}) custom-call(f32[56,384]{1,0:T(8,128)S(1)} %get-tuple-element.24.tgt.pack, f32[56,384]{1,0:T(8,128)S(1)} %collective-permute-done.srca.packa, f32[56,384]{1,0:T(8,128)S(1)} %collective-permute-done.1.srcb.packb, ...), custom_call_target="tpu_custom_call", output_to_operand_aliasing={{2}: (4, {})} | custom-call | tf_op jit(solution)/shard_map/perm_near/pallas_call | solution.py:622
  18.5 1.3 %collective-permute-start.2 = (f32[24,384]{1,0:T(8,128)S(1)}, f32[24,384]{1,0:T(8,128)S(1)}, u32[]{:S(2)}, u32[]{:S(2)}) collective-permute-start(f32[24,384]{1,0:T(8,128)S(1)} %get-tuple-element.28.msg), channel_id=1, source_target_pairs={{0,16},{16,0},{1,17},{17,1},{2,18},{18,2},{3,19},{19,3},{4,20},{20... | collective-permute-start | bytes 110600 | tf_op jit(solution)/shard_map/ppermute | solution.py:695
  19.8 1.6 %collective-permute-done.2.other = f32[24,384]{1,0:T(8,128)S(1)} collective-permute-done((f32[24,384]{1,0:T(8,128)S(1)}, f32[24,384]{1,0:T(8,128)S(1)}, u32[]{:S(2)}, u32[]{:S(2)}) %collective-permute-start.2) | collective-permute-done | bytes 36896 | tf_op jit(solution)/shard_map/ppermute | solution.py:695
  21.4 0.2 start.1
  21.7 4.7 %collective-permute-start.4 = (f32[24,384]{1,0:T(8,128)S(1)}, f32[24,384]{1,0:T(8,128)S(1)}, u32[]{:S(2)}, u32[]{:S(2)}) collective-permute-start(f32[24,384]{1,0:T(8,128)S(1)} %get-tuple-element.29.m0), channel_id=1, source_target_pairs={{1,2},{2,1},{3,4},{4,3},{5,6},{6,5},{7,8},{8,7},{9,10},{10,9},{11,... | collective-permute-start | bytes 110600 | tf_op jit(solution)/shard_map/ppermute | solution.py:647
  26.3 0.1 collective-permute-start.3
  26.4 4.2 %own_0.1 = (bf16[4,6,512,128]{3,2,1,0:T(8,128)(2,1)S(1)}, f32[192,384]{1,0:T(8,128)S(1)}, f32[128,384]{1,0:T(8,128)S(1)}) custom-call(f32[24,384]{1,0:T(8,128)S(1)} %get-tuple-element.29.m0, f32[56,384]{1,0:T(8,128)S(1)} %get-tuple-element.24.tgt.pack), custom_call_target="tpu_custom_call" | custom-call | tf_op jit(solution)/shard_map/own_0/pallas_call | solution.py:622
  30.6 0.0 collective-permute-done.4.m0b
  30.6 0.0 collective-permute-done.3.m0a
  30.7 5.4 %near_0.1 = (f32[16,384]{1,0:T(8,128)S(1)}, bf16[4,18,512,128]{3,2,1,0:T(8,128)(2,1)S(1)}, s32[38]{0:T(128)S(1)}, f32[192,384]{1,0:T(8,128)S(1)}, f32[128,384]{1,0:T(8,128)S(1)}) custom-call(f32[24,384]{1,0:T(8,128)S(1)} %get-tuple-element.29.m0, f32[24,384]{1,0:T(8,128)S(1)} %collective-permute-done.3.m0a, ...), custom_call_target="tpu_custom_call", output_to_operand_aliasing={{3}: (7, {}), {4}: (8, {})} | custom-call | tf_op jit(solution)/shard_map/near_0/pallas_call | solution.py:622
  36.0 2.1 %collective-permute-start.6 = (f32[16,384]{1,0:T(8,128)S(1)}, f32[16,384]{1,0:T(8,128)S(1)}, u32[]{:S(2)}, u32[]{:S(2)}) collective-permute-start(f32[16,384]{1,0:T(8,128)S(1)} %get-tuple-element.33.mu), channel_id=1, source_target_pairs={{1,2},{2,1},{3,4},{4,3},{5,6},{6,5},{7,8},{8,7},{9,10},{10,9},{11,... | collective-permute-start | bytes 73736 | tf_op jit(solution)/shard_map/ppermute | solution.py:647
  38.1 0.7 %collective-permute-start.5 = (f32[16,384]{1,0:T(8,128)S(1)}, f32[16,384]{1,0:T(8,128)S(1)}, u32[]{:S(2)}, u32[]{:S(2)}) collective-permute-start(f32[16,384]{1,0:T(8,128)S(1)} %get-tuple-element.33.mu), channel_id=1, source_target_pairs={{0,1},{1,0},{2,3},{3,2},{4,5},{5,4},{6,7},{7,6},{8,9},{9,8},{10,11... | collective-permute-start | bytes 73736 | tf_op jit(solution)/shard_map/ppermute | solution.py:646
  38.8 1.3 %own_1.1 = (f32[192,384]{1,0:T(8,128)S(1)}, f32[128,384]{1,0:T(8,128)S(1)}) custom-call(f32[16,384]{1,0:T(8,128)S(1)} %get-tuple-element.33.mu, f32[24,384]{1,0:T(8,128)S(1)} %get-tuple-element.29.m0, bf16[4,6,512,128]{3,2,1,0:T(8,128)(2,1)S(1)} %get-tuple-element.34.tensors), custom_call_target="tpu_custom_call" | custom-call | tf_op jit(solution)/shard_map/own_1/pallas_call | solution.py:622
  40.1 2.0 %collective-permute-done.6.mub = f32[16,384]{1,0:T(8,128)S(1)} collective-permute-done((f32[16,384]{1,0:T(8,128)S(1)}, f32[16,384]{1,0:T(8,128)S(1)}, u32[]{:S(2)}, u32[]{:S(2)}) %collective-permute-start.6) | collective-permute-done | bytes 24608 | tf_op jit(solution)/shard_map/ppermute | solution.py:647
  42.1 0.0 collective-permute-done.5.mua
  42.1 1.9 %near_1.1 = (f32[16,384]{1,0:T(8,128)S(1)}, f32[192,384]{1,0:T(8,128)S(1)}, f32[128,384]{1,0:T(8,128)S(1)}) custom-call(f32[16,384]{1,0:T(8,128)S(1)} %collective-permute-done.5.mua, f32[16,384]{1,0:T(8,128)S(1)} %collective-permute-done.6.mub, f32[24,384]{1,0:T(8,128)S(1)} %get-tuple-element.29.m0, ...), custom_call_target="tpu_custom_call", output_to_operand_aliasing={{1}: (7, {}), {2}: (8, {})} | custom-call | tf_op jit(solution)/shard_map/near_1/pallas_call | solution.py:622
  44.0 2.0 %collective-permute-start.8 = (f32[16,384]{1,0:T(8,128)S(1)}, f32[16,384]{1,0:T(8,128)S(1)}, u32[]{:S(2)}, u32[]{:S(2)}) collective-permute-start(f32[16,384]{1,0:T(8,128)S(1)} %get-tuple-element.39.mu), channel_id=1, source_target_pairs={{1,2},{2,1},{3,4},{4,3},{5,6},{6,5},{7,8},{8,7},{9,10},{10,9},{11,... | collective-permute-start | bytes 73736 | tf_op jit(solution)/shard_map/ppermute | solution.py:647
  46.0 0.1 collective-permute-start.7
  46.1 1.4 %own_last.1 = (f32[192,384]{1,0:T(8,128)S(1)}, f32[128,384]{1,0:T(8,128)S(1)}, f32[48,384]{1,0:T(8,128)S(1)}) custom-call(f32[16,384]{1,0:T(8,128)S(1)} %get-tuple-element.39.mu, f32[24,384]{1,0:T(8,128)S(1)} %get-tuple-element.29.m0, bf16[4,6,512,128]{3,2,1,0:T(8,128)(2,1)S(1)} %get-tuple-element.34.tensors, f32[48,384]{1,0:T(8,128)S(1)} %get-tuple-element.40.perm, ...), custom_call_target="tpu_custom_call" | custom-call | tf_op jit(solution)/shard_map/own_last/pallas_call | solution.py:622
  47.5 2.5 %collective-permute-done.8.mub = f32[16,384]{1,0:T(8,128)S(1)} collective-permute-done((f32[16,384]{1,0:T(8,128)S(1)}, f32[16,384]{1,0:T(8,128)S(1)}, u32[]{:S(2)}, u32[]{:S(2)}) %collective-permute-start.8) | collective-permute-done | bytes 24608 | tf_op jit(solution)/shard_map/ppermute | solution.py:647
  50.1 0.0 collective-permute-done.7.mua
  50.1 3.0 %final.1 = (f32[3,16,384]{2,1,0:T(8,128)}, f32[3,4,384]{2,1,0:T(4,128)}, f32[192,384]{1,0:T(8,128)S(1)}, f32[128,384]{1,0:T(8,128)S(1)}) custom-call(f32[16,384]{1,0:T(8,128)S(1)} %collective-permute-done.7.mua, f32[16,384]{1,0:T(8,128)S(1)} %collective-permute-done.8.mub, ...), custom_call_target="tpu_custom_call", output_to_operand_aliasing={{2}: (8, {}), {3}: (9, {})} | custom-call | tf_op jit(solution)/shard_map/final/pallas_call | solution.py:622
Async XLA Ops:
  2.1 9.4 %collective-permute-start.1 = (f32[56,384]{1,0:T(8,128)S(1)}, f32[56,384]{1,0:T(8,128)S(1)}, u32[]{:S(2)}, u32[]{:S(2)}) collective-permute-start(f32[56,384]{1,0:T(8,128)S(1)} %pack.1.tgt), channel_id=1, source_target_pairs={{1,2},{2,1},{3,4},{4,3},{5,6},{6,5},{7,8},{8,7},{9,10},{10,9},{11,... | collective-permute-start | bytes 258056 | tf_op jit(solution)/shard_map/ppermute | solution.py:647
  5.8 5.7 %collective-permute-start = (f32[56,384]{1,0:T(8,128)S(1)}, f32[56,384]{1,0:T(8,128)S(1)}, u32[]{:S(2)}, u32[]{:S(2)}) collective-permute-start(f32[56,384]{1,0:T(8,128)S(1)} %pack.1.tgt), channel_id=1, source_target_pairs={{0,1},{1,0},{2,3},{3,2},{4,5},{5,4},{6,7},{7,6},{8,9},{9,8},{10,11... | collective-permute-start | bytes 258056 | tf_op jit(solution)/shard_map/ppermute | solution.py:646
  18.5 2.9 %collective-permute-start.2 = (f32[24,384]{1,0:T(8,128)S(1)}, f32[24,384]{1,0:T(8,128)S(1)}, u32[]{:S(2)}, u32[]{:S(2)}) collective-permute-start(f32[24,384]{1,0:T(8,128)S(1)} %get-tuple-element.28.msg), channel_id=1, source_target_pairs={{0,16},{16,0},{1,17},{17,1},{2,18},{18,2},{3,19},{19,3},{4,20},{20... | collective-permute-start | bytes 110600 | tf_op jit(solution)/shard_map/ppermute | solution.py:695
  21.7 9.0 %collective-permute-start.4 = (f32[24,384]{1,0:T(8,128)S(1)}, f32[24,384]{1,0:T(8,128)S(1)}, u32[]{:S(2)}, u32[]{:S(2)}) collective-permute-start(f32[24,384]{1,0:T(8,128)S(1)} %get-tuple-element.29.m0), channel_id=1, source_target_pairs={{1,2},{2,1},{3,4},{4,3},{5,6},{6,5},{7,8},{8,7},{9,10},{10,9},{11,... | collective-permute-start | bytes 110600 | tf_op jit(solution)/shard_map/ppermute | solution.py:647
  26.3 4.3 %collective-permute-start.3 = (f32[24,384]{1,0:T(8,128)S(1)}, f32[24,384]{1,0:T(8,128)S(1)}, u32[]{:S(2)}, u32[]{:S(2)}) collective-permute-start(f32[24,384]{1,0:T(8,128)S(1)} %get-tuple-element.29.m0), channel_id=1, source_target_pairs={{0,1},{1,0},{2,3},{3,2},{4,5},{5,4},{6,7},{7,6},{8,9},{9,8},{10,11... | collective-permute-start | bytes 110600 | tf_op jit(solution)/shard_map/ppermute | solution.py:646
  36.0 6.0 %collective-permute-start.6 = (f32[16,384]{1,0:T(8,128)S(1)}, f32[16,384]{1,0:T(8,128)S(1)}, u32[]{:S(2)}, u32[]{:S(2)}) collective-permute-start(f32[16,384]{1,0:T(8,128)S(1)} %get-tuple-element.33.mu), channel_id=1, source_target_pairs={{1,2},{2,1},{3,4},{4,3},{5,6},{6,5},{7,8},{8,7},{9,10},{10,9},{11,... | collective-permute-start | bytes 73736 | tf_op jit(solution)/shard_map/ppermute | solution.py:647
  38.1 3.9 %collective-permute-start.5 = (f32[16,384]{1,0:T(8,128)S(1)}, f32[16,384]{1,0:T(8,128)S(1)}, u32[]{:S(2)}, u32[]{:S(2)}) collective-permute-start(f32[16,384]{1,0:T(8,128)S(1)} %get-tuple-element.33.mu), channel_id=1, source_target_pairs={{0,1},{1,0},{2,3},{3,2},{4,5},{5,4},{6,7},{7,6},{8,9},{9,8},{10,11... | collective-permute-start | bytes 73736 | tf_op jit(solution)/shard_map/ppermute | solution.py:646
  44.0 6.0 %collective-permute-start.8 = (f32[16,384]{1,0:T(8,128)S(1)}, f32[16,384]{1,0:T(8,128)S(1)}, u32[]{:S(2)}, u32[]{:S(2)}) collective-permute-start(f32[16,384]{1,0:T(8,128)S(1)} %get-tuple-element.39.mu), channel_id=1, source_target_pairs={{1,2},{2,1},{3,4},{4,3},{5,6},{6,5},{7,8},{8,7},{9,10},{10,9},{11,... | collective-permute-start | bytes 73736 | tf_op jit(solution)/shard_map/ppermute | solution.py:647
  46.0 4.0 %collective-permute-start.7 = (f32[16,384]{1,0:T(8,128)S(1)}, f32[16,384]{1,0:T(8,128)S(1)}, u32[]{:S(2)}, u32[]{:S(2)}) collective-permute-start(f32[16,384]{1,0:T(8,128)S(1)} %get-tuple-element.39.mu), channel_id=1, source_target_pairs={{0,1},{1,0},{2,3},{3,2},{4,5},{5,4},{6,7},{7,6},{8,9},{9,8},{10,11... | collective-permute-start | bytes 73736 | tf_op jit(solution)/shard_map/ppermute | solution.py:646

commit v4 on v3

--- a/solution.py
+++ b/solution.py
@@ -63,11 +63,6 @@
     return parts + list(split3(n)) + [jnp.ones_like(n)]
 
 
-def store_rows(ref, tile, row, stride, value):
-    for i in range(value.shape[1] // L):
-        ref[tile + i, pl.ds(row, value.shape[0], stride=stride), :] = value[:, i * L : (i + 1) * L]
-
-
 def slot_stack(pieces, slots, g):
     lo = g // 2 * 8
     top = lax.broadcasted_iota(jnp.int32, (8, pieces[0].shape[1]), 0) < 4
@@ -93,7 +88,7 @@
 
 def source_features(pieces, fs, s, w, count):
     for g in range(-(-count // 4)):
-        fs[g, s * w : (s + 1) * w, :] = jnp.transpose(slot_stack(pieces, S_SLOTS, g)).astype(BF16)
+        fs[g, s * w : (s + 1) * w, :] = jnp.transpose(slot_stack(pieces, S_SLOTS, g).astype(BF16))
 
 
 def sum_select(rows, count):
@@ -189,13 +184,14 @@
     return jnp.dot(a, b, precision=lax.Precision.HIGHEST, preferred_element_type=F32)
 
 
-def pack_kernel(nb, nbp, w, pos, charge, polar, mol, out, scr, posv, chargev, polarv, molv, sem):
+def pack_kernel(nb, nbp, w, pos, charge, polar, mol, out, sel, scr, posv, chargev, polarv, molv, sem):
     copies = [
         pltpu.make_async_copy(src, dst, sem.at[i])
         for i, (src, dst) in enumerate(((pos, posv), (charge, chargev), (polar, polarv), (mol, molv)))
     ]
     for c in copies:
         c.start()
+    sel[...] = sum_select(nbp, nb)
     scr[...] = jnp.zeros_like(scr)
     for c in copies:
         c.wait()
@@ -242,10 +238,10 @@
             r0 = (it.g * 4 + j) * SLOT
             r = rt[r0 : r0 + SLOT, pl.ds(it.s0, L)]
             pair = f[j]
-            acc[r0 : r0 + SLOT, pl.ds(it.t0, L)] += dot(jnp.concatenate([r, r], 1), pair)
+            acc[it.t0 // L, r0 : r0 + SLOT, :] += dot(jnp.concatenate([r, r], 1), pair)
             if it.sym:
                 back = dot(rt[r0 : r0 + SLOT, pl.ds(it.t0, L)], pair, 1, 1)
-                acc[r0 : r0 + SLOT, pl.ds(it.s0, L)] += back[:, :L] + back[:, L:]
+                acc[it.s0 // L, r0 : r0 + SLOT, :] += back[:, :L] + back[:, L:]
 
     def functions(it, r2, f):
         for j in range(4):
@@ -346,10 +342,10 @@
         lst[1 + size + e] = t * L
 
 
-def perm_own_kernel(nb, nbp, w, tgt, acc, ft, order, keep, fs, rt, cols, qrow, qbuf, r2a, r2b, fa, fb, lst):
+def perm_own_kernel(nb, nbp, w, tgt, sel, acc, ft, order, keep, fs, rt, cols, qrow, qbuf, r2a, r2b, fa, fb, lst):
     nt = w // L
     base = 3 * nbp
-    sel_r = sum_select(nbp, nb)
+    sel_r = sel[...]
     acc[...] = jnp.zeros_like(acc)
     order[...] = perm_matrix(tgt[base + 3 : base + 4, :], w)
     keep[...] = tgt[...]
@@ -367,7 +363,7 @@
 
 
 def perm_near_kernel(
-    nb, nbp, w, tgt, srca, srcb, ft, acc_in, order, perm_out, msg_out, acc,
+    nb, nbp, w, tgt, srca, srcb, sel, ft, acc_in, order, perm_out, msg_out, acc,
     fs, rt, cols, qrow, qbuf, r2a, r2b, fa, fb, lst,
 ):
     nt = w // L
@@ -375,7 +371,7 @@
     coords = [tgt[a * nbp : (a + 1) * nbp, :] for a in range(3)]
     center = center_of(coords, nb)
     xt = [x - c for x, c in zip(coords, center)]
-    sel_r = sum_select(nbp, nb)
+    sel_r = sel[...]
     sranges = []
     for s, src in enumerate((srca, srcb)):
         xs = [src[a * nbp : (a + 1) * nbp, :] - center[a] for a in range(3)]
@@ -389,12 +385,14 @@
     perm_near_pairs(n, lst, size, nb, fs, ft, rt, qbuf, acc, (r2a, r2b), (fa, fb))
     if nb < nbp:
         perm_out[...] = jnp.zeros_like(perm_out)
-    for b in range(nb):
-        s = acc[b * 32 : b * 32 + 8, :] + acc[b * 32 + 8 : b * 32 + 16, :]
-        s = s + acc[b * 32 + 16 : b * 32 + 24, :]
+    for i in range(nt):
+        tile = slice(i * L, (i + 1) * L)
+        sums = []
+        for f in range(4):
+            h, m, l = (acc[i, pl.ds(p * 8 + f, nb, stride=SLOT), :] for p in range(3))
+            sums.append((h + m) + l)
         for a in range(3):
-            row = xt[a][b : b + 1] * s[3:4] - s[a : a + 1]
-            perm_out[a * nbp + b : a * nbp + b + 1, :] = row
+            perm_out[a * nbp : a * nbp + nb, tile] = xt[a][:nb, tile] * sums[3] - sums[a]
     wc = weights(nb, (KP, nbp), lax.axis_index("bead"), 1) * (1.0 / BEADS)
     parts = [hdot(wc, perm_out[a * nbp : (a + 1) * nbp, :]) for a in range(3)]
     parts += [hdot(wc, coords[a]) for a in range(3)]
@@ -459,16 +457,21 @@
     dotted = x[0] * m[0] + x[1] * m[1] + x[2] * m[2]
     feats = m + [dotted] + [x[a] * m[b] for a in range(3) for b in range(3)]
     feats += [x[a] * dotted for a in range(3)]
-    tile = s * (w // L)
+    nt = w // L
     for f, v in enumerate(feats):
         for p, piece in enumerate(split3(v)):
-            store_rows(le, tile, p * 16 + f, L, piece[:CONTR])
-            if f < 3:
-                store_rows(le, tile, 64 + p * 8 + f, L, piece[:CONTR])
+            row = (p * 16 + f) * KP
+            for i in range(nt):
+                le[s * nt + i, row : row + KP, :] = piece[:, i * L : (i + 1) * L]
+
+
+def features_of(le, tile, k):
+    first = le[tile, pl.ds(k, 48, stride=KP), :]
+    second = [le[tile, pl.ds(p * 16 * KP + k, 8, stride=KP), :] for p in range(3)]
+    return first.astype(BF16), jnp.concatenate(second, 0).astype(BF16)
 
 
 def twice(x):
-    x = x.astype(BF16)
     return jnp.concatenate([x, x], 1)
 
 
@@ -481,16 +484,17 @@
     for e, (s, t) in enumerate(diag + off):
         s0, t0 = s * L, t * L
         for k in range(CONTR):
-            ra, rb = k * L, k * L + 64
             pa, pb = tensors[k, e, 0 : 2 * L, :], tensors[k, e, 2 * L : 4 * L, :]
-            a0, b0 = k * 48, k * 32
-            acc_a[a0 : a0 + 48, t0 : t0 + L] += dot(twice(le[s, ra : ra + 48, :]), pa)
-            acc_b[b0 : b0 + 32, t0 : t0 + L] += dot(twice(le[s, rb : rb + 32, :]), pb)
+            a0, b0 = k * 48, k * 24
+            fa, fb = features_of(le, s, k)
+            acc_a[a0 : a0 + 48, t0 : t0 + L] += dot(twice(fa), pa)
+            acc_b[b0 : b0 + 24, t0 : t0 + L] += dot(twice(fb), pb)
             if s != t:
-                back = dot(le[t, ra : ra + 48, :].astype(BF16), pa, 1, 1)
+                fa, fb = features_of(le, t, k)
+                back = dot(fa, pa, 1, 1)
                 acc_a[a0 : a0 + 48, s0 : s0 + L] += back[:, :L] + back[:, L:]
-                back = dot(le[t, rb : rb + 32, :].astype(BF16), pb, 1, 1)
-                acc_b[b0 : b0 + 32, s0 : s0 + L] += back[:, :L] + back[:, L:]
+                back = dot(fb, pb, 1, 1)
+                acc_b[b0 : b0 + 24, s0 : s0 + L] += back[:, :L] + back[:, L:]
 
 
 def near_sums(w, mus, cps, m0, tensors, lst, acc_a, acc_b, le, ev, bring=None):
@@ -502,24 +506,32 @@
     if bring is not None:
         bring.wait()
 
-    def step(e, carry):
+    def add(e):
         tile = lst[1 + e] // L
         t0 = pl.multiple_of(lst[1 + size + e], L)
         for k in range(CONTR):
-            ra, rb = k * L, k * L + 64
-            a0, b0 = k * 48, k * 32
-            fa, fb = twice(le[tile, ra : ra + 48, :]), twice(le[tile, rb : rb + 32, :])
-            acc_a[a0 : a0 + 48, pl.ds(t0, L)] += dot(fa, tensors[k, e, 0 : 2 * L, :])
-            acc_b[b0 : b0 + 32, pl.ds(t0, L)] += dot(fb, tensors[k, e, 2 * L : 4 * L, :])
+            a0, b0 = k * 48, k * 24
+            fa, fb = features_of(le, tile, k)
+            acc_a[a0 : a0 + 48, pl.ds(t0, L)] += dot(twice(fa), tensors[k, e, 0 : 2 * L, :])
+            acc_b[b0 : b0 + 24, pl.ds(t0, L)] += dot(twice(fb), tensors[k, e, 2 * L : 4 * L, :])
+
+    def both(i, carry):
+        add(2 * i)
+        add(2 * i + 1)
         return carry
 
-    lax.fori_loop(0, lst[0], step, 0)
+    def single(i, carry):
+        add(lst[0] - 1)
+        return carry
+
+    lax.fori_loop(0, lst[0] // 2, both, 0)
+    lax.fori_loop(0, lst[0] % 2, single, 0)
     ev[...] = jnp.zeros_like(ev)
     xt = centered(m0, center)
     for k in range(CONTR):
         o = k * 48
         sa = acc_a[o : o + 16, :] + acc_a[o + 16 : o + 32, :] + acc_a[o + 32 : o + 48, :]
-        o = k * 32
+        o = k * 24
         sb = acc_b[o : o + 8, :] + acc_b[o + 8 : o + 16, :] + acc_b[o + 16 : o + 24, :]
         x = [v[k : k + 1] for v in xt]
         along = x[0] * sa[0:1] + x[1] * sa[1:2] + x[2] * sa[2:3] - sa[3:4]
@@ -554,7 +566,7 @@
 
 def near_first_kernel(
     nbp, w, m0, m0a, m0b, pack, packa, packb, cf, acc_a_in, acc_b_in,
-    mu_out, tensors, lst, acc_a, acc_b, fs, ft, cols, qrow, qbuf, r2a, r2b, le, ev,
+    mu_out, tensors, lst_out, acc_a, acc_b, fs, ft, cols, qrow, qbuf, r2a, r2b, le, ev, lst, sem,
 ):
     nt = w // L
     base = 3 * nbp
@@ -571,12 +583,15 @@
     misc = pack[base : base + 8, :]
     size = 2 * nt * nt
     near_list(lst, size, ranges(xt[0], misc[1:2], CONTR, w), sranges)
+    leave = pltpu.make_async_copy(lst, lst_out, sem)
+    leave.start()
     q_rows(misc, qrow)
     n = lst[0]
     block_q(n, 0, lst, size, False, cols, qrow, qbuf)
     tensor_pairs(n, lst, size, fs, ft, qbuf, r2a, r2b, tensors)
     near_sums(w, [m0a, m0b], [m0a, m0b], m0, tensors, lst, acc_a, acc_b, le, ev)
     mu_out[...] = update(pack, nbp, cf, ev)
+    leave.wait()
 
 
 def near_kernel(
@@ -615,15 +630,14 @@
     return pairs
 
 
-def call(kernel, outs, name, scratch, args, any_in=(), smem_out=(), hbm_in=(), alias=None):
-    smem = pl.BlockSpec(memory_space=pltpu.SMEM)
+def call(kernel, outs, name, scratch, args, any_in=(), any_out=(), hbm_in=(), alias=None):
     vmem = pl.BlockSpec(memory_space=pltpu.VMEM)
     hbm = pl.BlockSpec(memory_space=pltpu.HBM)
     return pl.pallas_call(
         kernel,
         out_shape=[jax.ShapeDtypeStruct(s, d) for s, d in outs],
         in_specs=[pl.BlockSpec(memory_space=pl.ANY) if i in any_in else hbm if i in hbm_in else vmem for i in range(len(args))],
-        out_specs=[smem if i in smem_out else vmem for i in range(len(outs))],
+        out_specs=[pl.BlockSpec(memory_space=pl.ANY) if i in any_out else vmem for i in range(len(outs))],
         scratch_shapes=list(scratch),
         input_output_aliases=alias or {},
         compiler_params=pltpu.CompilerParams(vmem_limit_bytes=VMEM_LIMIT),
@@ -648,8 +662,8 @@
         return near, far
 
     raw = (jnp.transpose(positions, (1, 0, 2)), charges, polar, molecule)
-    (pack,) = call(
-        part(pack_kernel, nb, nbp, w), [((rows, w), F32)], "pack",
+    pack, sel = call(
+        part(pack_kernel, nb, nbp, w), [((rows, w), F32), ((12 * nbp, max(nb * SLOT, L)), BF16)], "pack",
         [
             pltpu.VMEM((rows, w), F32),
             pltpu.VMEM((3, nb, w), F32),
@@ -683,12 +697,12 @@
 
     acc, ft, order, pack = call(
         part(perm_own_kernel, nb, nbp, w),
-        [((nb * SLOT, w), F32), ((nb, DEEP, w), BF16), ((w, w), BF16), ((rows, w), F32)], "perm_own",
-        perm_scratch(1, own_size), (pack,),
+        [((nt, nb * SLOT, L), F32), ((nb, DEEP, w), BF16), ((w, w), BF16), ((rows, w), F32)], "perm_own",
+        perm_scratch(1, own_size), (pack, sel),
     )
     perm, msg, _ = call(
-        part(perm_near_kernel, nb, nbp, w), [((3 * nbp, w), F32), ((6 * CONTR, w), F32), ((nb * SLOT, w), F32)],
-        "perm_near", perm_scratch(2, near_size), (pack, packa, packb, ft, acc, order), alias={4: 2},
+        part(perm_near_kernel, nb, nbp, w), [((3 * nbp, w), F32), ((6 * CONTR, w), F32), ((nt, nb * SLOT, L), F32)],
+        "perm_near", perm_scratch(2, near_size), (pack, packa, packb, sel, ft, acc, order), alias={5: 2},
     )
 
     if nbead == 2:
@@ -707,10 +721,10 @@
             *pair_scratch(nsrc, blocks),
         ]
 
-    accs = [((CONTR * 48, w), F32), ((CONTR * 32, w), F32)]
-    near_scratch = [pltpu.VMEM((2 * nt, CONTR * L, L), F32), pltpu.VMEM((2 * KP, w), F32)]
+    accs = [((CONTR * 48, w), F32), ((CONTR * 24, w), F32)]
+    near_scratch = [pltpu.VMEM((2 * nt, 48 * KP, L), F32), pltpu.VMEM((2 * KP, w), F32)]
     list_scratch = [pltpu.SMEM((2 + 2 * near_size,), jnp.int32), pltpu.SemaphoreType.DMA]
-    own_scratch = [pltpu.VMEM((nt, CONTR * L, L), F32)]
+    own_scratch = [pltpu.VMEM((nt, 48 * KP, L), F32)]
     t_own, acc_a, acc_b = call(
         part(own_first_kernel, nbp, w), [((CONTR, own_size, 4 * L, L), BF16)] + accs, "own_0",
         own_scratch + tensor_scratch(1, own_size) + [pltpu.SMEM((2 + 2 * own_size,), jnp.int32)],
@@ -719,8 +733,8 @@
     mu, t_nbr, lst, _, _ = call(
         part(near_first_kernel, nbp, w),
         [((2 * KP, w), F32), ((CONTR, near_size, 4 * L, L), BF16), ((2 + 2 * near_size,), jnp.int32)] + accs, "near_0",
-        tensor_scratch(2, near_size) + near_scratch,
-        (m0, m0a, m0b, pack, packa, packb, cf, acc_a, acc_b), smem_out=(2,), alias={7: 3, 8: 4},
+        tensor_scratch(2, near_size) + near_scratch + list_scratch,
+        (m0, m0a, m0b, pack, packa, packb, cf, acc_a, acc_b), any_out=(2,), alias={7: 3, 8: 4},
     )
     for step in range(1, ITERS):
         mua, mub = exchange(mu)

time: 53.5 us -> 51.3 us (0.959)
  Pallas kernels: 31.6 us -> 29.2 us
    pallas_call x10, Pallas kernels: 31.6 us -> 29.2 us  [call(): pl.pallas_call(kernel, out_shape=[jax.ShapeDtypeStruct(s, d) for s, d in...]
where the time goes in v4:
time: 51.3 us; the launch traced here: 51.1 us
  Pallas kernels  29.2 us (57%)
  starting transfers between devices  14.6 us (28%)
  waiting for transfers between devices  6.31 us (12%)
  between operations  0.94 us (2%)
    pallas_call x10, Pallas kernels, call(): pl.pallas_call(kernel, out_shape=[jax.ShapeDtypeStruct(s, d) for s, d in...  29.2 us
    ppermute x4, starting transfers between devices, exchange(): far = lax.ppermute(x, 'space', swap_pairs(nspace, 1))  12.4 us
    ppermute x4, waiting for transfers between devices, exchange(): far = lax.ppermute(x, 'space', swap_pairs(nspace, 1))  4.7 us
    ppermute x1, waiting for transfers between devices, body(): other = lax.ppermute(msg, 'bead', [(0, 1), (1, 0)])  1.6 us
    ppermute x1, starting transfers between devices, body(): other = lax.ppermute(msg, 'bead', [(0, 1), (1, 0)])  1.27 us
  transfers between devices with their start and end apart: 9, of which 3 were waited for; matrix products, arithmetic and copies ran while one was open for 0% of the time, Pallas kernels for 24%

profile of v4, /device:TPU:21, one launch (start us, length us, event | category | flops | bytes accessed | tf_op | source)
XLA Modules:
  0.0 51.1 jit_solution(6548746510239402224)
XLA Ops:
  0.6 1.5 %pack.1 = (f32[56,384]{1,0:T(8,128)S(1)}, bf16[192,512]{1,0:T(8,128)(2,1)S(1)}) custom-call(f32[3,16,384]{2,1,0:T(8,128)} %bitcast.3, f32[384]{0:T(512)} %charge.1, f32[384]{0:T(512)} %polar.1, s32[384]{0:T(512)} %mol.1), custom_call_target="tpu_custom_call" | custom-call | tf_op jit(solution)/shard_map/pack/pallas_call | solution.py:636
  2.1 3.7 %collective-permute-start.1 = (f32[56,384]{1,0:T(8,128)S(1)}, f32[56,384]{1,0:T(8,128)S(1)}, u32[]{:S(2)}, u32[]{:S(2)}) collective-permute-start(f32[56,384]{1,0:T(8,128)S(1)} %get-tuple-element.26.tgt), channel_id=1, source_target_pairs={{1,2},{2,1},{3,4},{4,3},{5,6},{6,5},{7,8},{8,7},{9,10},{10,9},{11,... | collective-permute-start | bytes 258056 | tf_op jit(solution)/shard_map/ppermute | solution.py:661
  5.8 0.1 collective-permute-start
  5.9 5.6 %perm_own.1 = (f32[3,512,128]{2,1,0:T(8,128)S(1)}, bf16[16,96,384]{2,1,0:T(8,128)(2,1)S(1)}, bf16[384,384]{1,0:T(8,128)(2,1)S(1)}, f32[56,384]{1,0:T(8,128)S(1)}) custom-call(f32[56,384]{1,0:T(8,128)S(1)} %get-tuple-element.26.tgt, bf16[192,512]{1,0:T(8,128)(2,1)S(1)} %get-tuple-element.27.sel), custom_call_target="tpu_custom_call" | custom-call | tf_op jit(solution)/shard_map/perm_own/pallas_call | solution.py:636
  11.5 0.0 collective-permute-done.1.srcb.packb
  11.5 0.0 collective-permute-done.srca.packa
  11.5 6.9 %perm_near.1 = (f32[48,384]{1,0:T(8,128)S(1)}, f32[24,384]{1,0:T(8,128)S(1)}, f32[3,512,128]{2,1,0:T(8,128)S(1)}) custom-call(f32[56,384]{1,0:T(8,128)S(1)} %get-tuple-element.28.tgt.pack, f32[56,384]{1,0:T(8,128)S(1)} %collective-permute-done.srca.packa, f32[56,384]{1,0:T(8,128)S(1)} %collective-permute-done.1.srcb.packb, ...), custom_call_target="tpu_custom_call", output_to_operand_aliasing={{2}: (5, {})} | custom-call | tf_op jit(solution)/shard_map/perm_near/pallas_call | solution.py:636
  18.4 1.3 %collective-permute-start.2 = (f32[24,384]{1,0:T(8,128)S(1)}, f32[24,384]{1,0:T(8,128)S(1)}, u32[]{:S(2)}, u32[]{:S(2)}) collective-permute-start(f32[24,384]{1,0:T(8,128)S(1)} %get-tuple-element.32.msg), channel_id=1, source_target_pairs={{0,16},{16,0},{1,17},{17,1},{2,18},{18,2},{3,19},{19,3},{4,20},{20... | collective-permute-start | bytes 110600 | tf_op jit(solution)/shard_map/ppermute | solution.py:709
  19.7 1.6 %collective-permute-done.2.other = f32[24,384]{1,0:T(8,128)S(1)} collective-permute-done((f32[24,384]{1,0:T(8,128)S(1)}, f32[24,384]{1,0:T(8,128)S(1)}, u32[]{:S(2)}, u32[]{:S(2)}) %collective-permute-start.2) | collective-permute-done | bytes 36896 | tf_op jit(solution)/shard_map/ppermute | solution.py:709
  21.3 0.2 start.1
  21.6 4.7 %collective-permute-start.4 = (f32[24,384]{1,0:T(8,128)S(1)}, f32[24,384]{1,0:T(8,128)S(1)}, u32[]{:S(2)}, u32[]{:S(2)}) collective-permute-start(f32[24,384]{1,0:T(8,128)S(1)} %get-tuple-element.33.m0), channel_id=1, source_target_pairs={{1,2},{2,1},{3,4},{4,3},{5,6},{6,5},{7,8},{8,7},{9,10},{10,9},{11,... | collective-permute-start | bytes 110600 | tf_op jit(solution)/shard_map/ppermute | solution.py:661
  26.2 0.1 collective-permute-start.3
  26.3 4.1 %own_0.1 = (bf16[4,6,512,128]{3,2,1,0:T(8,128)(2,1)S(1)}, f32[192,384]{1,0:T(8,128)S(1)}, f32[96,384]{1,0:T(8,128)S(1)}) custom-call(f32[24,384]{1,0:T(8,128)S(1)} %get-tuple-element.33.m0, f32[56,384]{1,0:T(8,128)S(1)} %get-tuple-element.28.tgt.pack), custom_call_target="tpu_custom_call" | custom-call | tf_op jit(solution)/shard_map/own_0/pallas_call | solution.py:636
  30.4 0.0 collective-permute-done.4.m0b
  30.4 0.0 collective-permute-done.3.m0a
  30.5 4.2 %near_0.1 = (f32[16,384]{1,0:T(8,128)S(1)}, bf16[4,18,512,128]{3,2,1,0:T(8,128)(2,1)S(1)}, s32[38]{0:T(128)S(1)}, f32[192,384]{1,0:T(8,128)S(1)}, f32[96,384]{1,0:T(8,128)S(1)}) custom-call(f32[24,384]{1,0:T(8,128)S(1)} %get-tuple-element.33.m0, f32[24,384]{1,0:T(8,128)S(1)} %collective-permute-done.3.m0a, ...), custom_call_target="tpu_custom_call", output_to_operand_aliasing={{3}: (7, {}), {4}: (8, {})} | custom-call | tf_op jit(solution)/shard_map/near_0/pallas_call | solution.py:636
  34.7 2.1 %collective-permute-start.6 = (f32[16,384]{1,0:T(8,128)S(1)}, f32[16,384]{1,0:T(8,128)S(1)}, u32[]{:S(2)}, u32[]{:S(2)}) collective-permute-start(f32[16,384]{1,0:T(8,128)S(1)} %get-tuple-element.37.mu), channel_id=1, source_target_pairs={{1,2},{2,1},{3,4},{4,3},{5,6},{6,5},{7,8},{8,7},{9,10},{10,9},{11,... | collective-permute-start | bytes 73736 | tf_op jit(solution)/shard_map/ppermute | solution.py:661
  36.8 0.7 %collective-permute-start.5 = (f32[16,384]{1,0:T(8,128)S(1)}, f32[16,384]{1,0:T(8,128)S(1)}, u32[]{:S(2)}, u32[]{:S(2)}) collective-permute-start(f32[16,384]{1,0:T(8,128)S(1)} %get-tuple-element.37.mu), channel_id=1, source_target_pairs={{0,1},{1,0},{2,3},{3,2},{4,5},{5,4},{6,7},{7,6},{8,9},{9,8},{10,11... | collective-permute-start | bytes 73736 | tf_op jit(solution)/shard_map/ppermute | solution.py:660
  37.4 1.2 %own_1.1 = (f32[192,384]{1,0:T(8,128)S(1)}, f32[96,384]{1,0:T(8,128)S(1)}) custom-call(f32[16,384]{1,0:T(8,128)S(1)} %get-tuple-element.37.mu, f32[24,384]{1,0:T(8,128)S(1)} %get-tuple-element.33.m0, bf16[4,6,512,128]{3,2,1,0:T(8,128)(2,1)S(1)} %get-tuple-element.38.tensors), custom_call_target="tpu_custom_call" | custom-call | tf_op jit(solution)/shard_map/own_1/pallas_call | solution.py:636
  38.7 2.0 %collective-permute-done.6.mub = f32[16,384]{1,0:T(8,128)S(1)} collective-permute-done((f32[16,384]{1,0:T(8,128)S(1)}, f32[16,384]{1,0:T(8,128)S(1)}, u32[]{:S(2)}, u32[]{:S(2)}) %collective-permute-start.6) | collective-permute-done | bytes 24608 | tf_op jit(solution)/shard_map/ppermute | solution.py:661
  40.7 0.0 collective-permute-done.5.mua
  40.7 1.5 %near_1.1 = (f32[16,384]{1,0:T(8,128)S(1)}, f32[192,384]{1,0:T(8,128)S(1)}, f32[96,384]{1,0:T(8,128)S(1)}) custom-call(f32[16,384]{1,0:T(8,128)S(1)} %collective-permute-done.5.mua, f32[16,384]{1,0:T(8,128)S(1)} %collective-permute-done.6.mub, f32[24,384]{1,0:T(8,128)S(1)} %get-tuple-element.33.m0, ...), custom_call_target="tpu_custom_call", output_to_operand_aliasing={{1}: (7, {}), {2}: (8, {})} | custom-call | tf_op jit(solution)/shard_map/near_1/pallas_call | solution.py:636
  42.3 2.0 %collective-permute-start.8 = (f32[16,384]{1,0:T(8,128)S(1)}, f32[16,384]{1,0:T(8,128)S(1)}, u32[]{:S(2)}, u32[]{:S(2)}) collective-permute-start(f32[16,384]{1,0:T(8,128)S(1)} %get-tuple-element.43.mu), channel_id=1, source_target_pairs={{1,2},{2,1},{3,4},{4,3},{5,6},{6,5},{7,8},{8,7},{9,10},{10,9},{11,... | collective-permute-start | bytes 73736 | tf_op jit(solution)/shard_map/ppermute | solution.py:661
  44.2 0.1 collective-permute-start.7
  44.3 1.3 %own_last.1 = (f32[192,384]{1,0:T(8,128)S(1)}, f32[96,384]{1,0:T(8,128)S(1)}, f32[48,384]{1,0:T(8,128)S(1)}) custom-call(f32[16,384]{1,0:T(8,128)S(1)} %get-tuple-element.43.mu, f32[24,384]{1,0:T(8,128)S(1)} %get-tuple-element.33.m0, bf16[4,6,512,128]{3,2,1,0:T(8,128)(2,1)S(1)} %get-tuple-element.38.tensors, f32[48,384]{1,0:T(8,128)S(1)} %get-tuple-element.44.perm, ...), custom_call_target="tpu_custom_call" | custom-call | tf_op jit(solution)/shard_map/own_last/pallas_call | solution.py:636
  45.6 2.7 %collective-permute-done.8.mub = f32[16,384]{1,0:T(8,128)S(1)} collective-permute-done((f32[16,384]{1,0:T(8,128)S(1)}, f32[16,384]{1,0:T(8,128)S(1)}, u32[]{:S(2)}, u32[]{:S(2)}) %collective-permute-start.8) | collective-permute-done | bytes 24608 | tf_op jit(solution)/shard_map/ppermute | solution.py:661
  48.3 0.0 collective-permute-done.7.mua
  48.3 2.6 %final.1 = (f32[3,16,384]{2,1,0:T(8,128)}, f32[3,4,384]{2,1,0:T(4,128)}, f32[192,384]{1,0:T(8,128)S(1)}, f32[96,384]{1,0:T(8,128)S(1)}) custom-call(f32[16,384]{1,0:T(8,128)S(1)} %collective-permute-done.7.mua, f32[16,384]{1,0:T(8,128)S(1)} %collective-permute-done.8.mub, ...), custom_call_target="tpu_custom_call", output_to_operand_aliasing={{2}: (8, {}), {3}: (9, {})} | custom-call | tf_op jit(solution)/shard_map/final/pallas_call | solution.py:636
Async XLA Ops:
  2.1 9.4 %collective-permute-start.1 = (f32[56,384]{1,0:T(8,128)S(1)}, f32[56,384]{1,0:T(8,128)S(1)}, u32[]{:S(2)}, u32[]{:S(2)}) collective-permute-start(f32[56,384]{1,0:T(8,128)S(1)} %get-tuple-element.26.tgt), channel_id=1, source_target_pairs={{1,2},{2,1},{3,4},{4,3},{5,6},{6,5},{7,8},{8,7},{9,10},{10,9},{11,... | collective-permute-start | bytes 258056 | tf_op jit(solution)/shard_map/ppermute | solution.py:661
  5.8 5.7 %collective-permute-start = (f32[56,384]{1,0:T(8,128)S(1)}, f32[56,384]{1,0:T(8,128)S(1)}, u32[]{:S(2)}, u32[]{:S(2)}) collective-permute-start(f32[56,384]{1,0:T(8,128)S(1)} %get-tuple-element.26.tgt), channel_id=1, source_target_pairs={{0,1},{1,0},{2,3},{3,2},{4,5},{5,4},{6,7},{7,6},{8,9},{9,8},{10,11... | collective-permute-start | bytes 258056 | tf_op jit(solution)/shard_map/ppermute | solution.py:660
  18.4 2.9 %collective-permute-start.2 = (f32[24,384]{1,0:T(8,128)S(1)}, f32[24,384]{1,0:T(8,128)S(1)}, u32[]{:S(2)}, u32[]{:S(2)}) collective-permute-start(f32[24,384]{1,0:T(8,128)S(1)} %get-tuple-element.32.msg), channel_id=1, source_target_pairs={{0,16},{16,0},{1,17},{17,1},{2,18},{18,2},{3,19},{19,3},{4,20},{20... | collective-permute-start | bytes 110600 | tf_op jit(solution)/shard_map/ppermute | solution.py:709
  21.6 8.9 %collective-permute-start.4 = (f32[24,384]{1,0:T(8,128)S(1)}, f32[24,384]{1,0:T(8,128)S(1)}, u32[]{:S(2)}, u32[]{:S(2)}) collective-permute-start(f32[24,384]{1,0:T(8,128)S(1)} %get-tuple-element.33.m0), channel_id=1, source_target_pairs={{1,2},{2,1},{3,4},{4,3},{5,6},{6,5},{7,8},{8,7},{9,10},{10,9},{11,... | collective-permute-start | bytes 110600 | tf_op jit(solution)/shard_map/ppermute | solution.py:661
  26.2 4.2 %collective-permute-start.3 = (f32[24,384]{1,0:T(8,128)S(1)}, f32[24,384]{1,0:T(8,128)S(1)}, u32[]{:S(2)}, u32[]{:S(2)}) collective-permute-start(f32[24,384]{1,0:T(8,128)S(1)} %get-tuple-element.33.m0), channel_id=1, source_target_pairs={{0,1},{1,0},{2,3},{3,2},{4,5},{5,4},{6,7},{7,6},{8,9},{9,8},{10,11... | collective-permute-start | bytes 110600 | tf_op jit(solution)/shard_map/ppermute | solution.py:660
  34.7 6.0 %collective-permute-start.6 = (f32[16,384]{1,0:T(8,128)S(1)}, f32[16,384]{1,0:T(8,128)S(1)}, u32[]{:S(2)}, u32[]{:S(2)}) collective-permute-start(f32[16,384]{1,0:T(8,128)S(1)} %get-tuple-element.37.mu), channel_id=1, source_target_pairs={{1,2},{2,1},{3,4},{4,3},{5,6},{6,5},{7,8},{8,7},{9,10},{10,9},{11,... | collective-permute-start | bytes 73736 | tf_op jit(solution)/shard_map/ppermute | solution.py:661
  36.8 3.9 %collective-permute-start.5 = (f32[16,384]{1,0:T(8,128)S(1)}, f32[16,384]{1,0:T(8,128)S(1)}, u32[]{:S(2)}, u32[]{:S(2)}) collective-permute-start(f32[16,384]{1,0:T(8,128)S(1)} %get-tuple-element.37.mu), channel_id=1, source_target_pairs={{0,1},{1,0},{2,3},{3,2},{4,5},{5,4},{6,7},{7,6},{8,9},{9,8},{10,11... | collective-permute-start | bytes 73736 | tf_op jit(solution)/shard_map/ppermute | solution.py:660
  42.3 6.0 %collective-permute-start.8 = (f32[16,384]{1,0:T(8,128)S(1)}, f32[16,384]{1,0:T(8,128)S(1)}, u32[]{:S(2)}, u32[]{:S(2)}) collective-permute-start(f32[16,384]{1,0:T(8,128)S(1)} %get-tuple-element.43.mu), channel_id=1, source_target_pairs={{1,2},{2,1},{3,4},{4,3},{5,6},{6,5},{7,8},{8,7},{9,10},{10,9},{11,... | collective-permute-start | bytes 73736 | tf_op jit(solution)/shard_map/ppermute | solution.py:661
  44.2 4.1 %collective-permute-start.7 = (f32[16,384]{1,0:T(8,128)S(1)}, f32[16,384]{1,0:T(8,128)S(1)}, u32[]{:S(2)}, u32[]{:S(2)}) collective-permute-start(f32[16,384]{1,0:T(8,128)S(1)} %get-tuple-element.43.mu), channel_id=1, source_target_pairs={{0,1},{1,0},{2,3},{3,2},{4,5},{5,4},{6,7},{7,6},{8,9},{9,8},{10,11... | collective-permute-start | bytes 73736 | tf_op jit(solution)/shard_map/ppermute | solution.py:660

commit v5 on v4

--- a/solution.py
+++ b/solution.py
@@ -233,15 +233,20 @@
 
 
 def perm_run(items, head, tail, nb, fs, ft, rt, qbuf, acc, r2s, fbs):
+    def gather(tile, b, out):
+        for p in range(3):
+            row = (p * nb + b) * 8
+            acc[tile, row : row + 8, :] += out[p * 8 : p * 8 + 8]
+
     def sums(it, f):
         for j in range(4):
             r0 = (it.g * 4 + j) * SLOT
             r = rt[r0 : r0 + SLOT, pl.ds(it.s0, L)]
             pair = f[j]
-            acc[it.t0 // L, r0 : r0 + SLOT, :] += dot(jnp.concatenate([r, r], 1), pair)
+            gather(it.t0 // L, it.g * 4 + j, dot(jnp.concatenate([r, r], 1), pair))
             if it.sym:
                 back = dot(rt[r0 : r0 + SLOT, pl.ds(it.t0, L)], pair, 1, 1)
-                acc[it.s0 // L, r0 : r0 + SLOT, :] += back[:, :L] + back[:, L:]
+                gather(it.s0 // L, it.g * 4 + j, back[:, :L] + back[:, L:])
 
     def functions(it, r2, f):
         for j in range(4):
@@ -286,47 +291,44 @@
     perm_run([], items[-1], None, nb, *args)
 
 
-def perm_near_pairs(n, lst, size, nb, *rest):
-    fbs = rest[-1]
+def perm_near_pairs(n, lst, size, nb, cols, qrow, *rest):
+    qbuf, fbs = rest[3], rest[-1]
     fbs[1][...] = jnp.zeros_like(fbs[1])
     groups = nb // 4
 
     def entry(i):
         good = i < n
         e = jnp.where(good, i, 0)
-        return jnp.where(good, e, size), lst[1 + e], lst[1 + size + e]
-
-    def item(it):
-        return Item(it[0], pl.multiple_of(it[1], L), pl.multiple_of(it[2], L))
+        return jnp.where(good, 1.0, 0.0), lst[1 + e], lst[1 + size + e]
+
+    def item(e, it):
+        return Item(e, pl.multiple_of(it[1], L), pl.multiple_of(it[2], L))
 
     def step(i, carry):
         before, first, second, after = carry
         later = (entry(2 * i + 3), entry(2 * i + 4))
-        items = [item(it).at(g) for it in (first, second) for g in range(groups)]
-        perm_run(items, item(before).at(groups - 1), item(after).at(0), nb, *rest)
+        items = []
+        for e, it in enumerate((first, second)):
+            block = item(e, it)
+            qbuf[e] = near_q(block.s0, block.t0, cols, qrow) * it[0]
+            items += [block.at(g) for g in range(groups)]
+        perm_run(items, item(1, before).at(groups - 1), item(0, after).at(0), nb, *rest)
         return (second, after) + later
 
     start = entry(0)
-    perm_run([], None, item(start).at(0), nb, *rest)
+    perm_run([], None, item(0, start).at(0), nb, *rest)
     last = lax.fori_loop(0, (n + 1) // 2, step, (start, start, entry(1), entry(2)))[0]
-    perm_run([], item(last).at(groups - 1), None, nb, *rest)
-
-
-def block_q(n, first, lst, size, own, cols, qrow, qbuf):
-    def one(i, carry):
-        e = first + i
-        s0 = pl.multiple_of(lst[1 + e], L)
-        t0 = pl.multiple_of(lst[1 + size + e], L)
-        cc = cols[pl.ds(s0, L), :]
-        row = qrow[:, pl.ds(t0, L)]
-        q = cc[:, 0:1] * row[0:1]
-        if own:
-            q = jnp.where(cc[:, 1:2] == row[1:2], 0.0, q)
-        qbuf[e] = q
-        return carry
-
-    lax.fori_loop(0, n, one, 0)
-    qbuf[size] = jnp.zeros_like(qbuf[size])
+    perm_run([], item(1, last).at(groups - 1), None, nb, *rest)
+
+
+def own_q(s, t, cols, qrow):
+    cc = cols[s * L : (s + 1) * L, :]
+    row = qrow[:, t * L : (t + 1) * L]
+    return jnp.where(cc[:, 1:2] == row[1:2], 0.0, cc[:, 0:1] * row[0:1])
+
+
+def near_q(s0, t0, cols, qrow):
+    return cols[pl.ds(s0, L), :][:, 0:1] * qrow[0:1, pl.ds(t0, L)]
 
 
 def q_rows(misc, qrow):
@@ -335,14 +337,7 @@
     qrow[0:1, :] = c[0:1] * (-THOLE * LOG2E)
 
 
-def fixed_list(lst, size, blocks):
-    lst[0] = len(blocks)
-    for e, (s, t) in enumerate(blocks):
-        lst[1 + e] = s * L
-        lst[1 + size + e] = t * L
-
-
-def perm_own_kernel(nb, nbp, w, tgt, sel, acc, ft, order, keep, fs, rt, cols, qrow, qbuf, r2a, r2b, fa, fb, lst):
+def perm_own_kernel(nb, nbp, w, tgt, sel, acc, ft, order, keep, fs, rt, cols, qrow, r2a, r2b, qbuf, fa, fb, lst):
     nt = w // L
     base = 3 * nbp
     sel_r = sel[...]
@@ -356,15 +351,14 @@
     perm_sources(nb, nbp, w, tgt, pieces, xt, 0, sel_r, fs, rt, cols)
     q_rows(tgt[base : base + 8, :], qrow)
     diag, off = own_blocks(nt)
-    size = len(diag) + len(off)
-    fixed_list(lst, size, diag + off)
-    block_q(size, 0, lst, size, True, cols, qrow, qbuf)
+    for e, (a, b) in enumerate(diag + off):
+        qbuf[e] = own_q(a, b, cols, qrow)
     perm_own_pairs(diag + off, nb, fs, ft, rt, qbuf, acc, (r2a, r2b), (fa, fb))
 
 
 def perm_near_kernel(
     nb, nbp, w, tgt, srca, srcb, sel, ft, acc_in, order, perm_out, msg_out, acc,
-    fs, rt, cols, qrow, qbuf, r2a, r2b, fa, fb, lst,
+    fs, rt, cols, qrow, r2a, r2b, qbuf, fa, fb, lst,
 ):
     nt = w // L
     base = 3 * nbp
@@ -381,15 +375,14 @@
     near_list(lst, size, ranges(xt[0], tgt[base + 1 : base + 2, :], nb, w), sranges)
     q_rows(tgt[base : base + 8, :], qrow)
     n = lst[0]
-    block_q(n, 0, lst, size, False, cols, qrow, qbuf)
-    perm_near_pairs(n, lst, size, nb, fs, ft, rt, qbuf, acc, (r2a, r2b), (fa, fb))
+    perm_near_pairs(n, lst, size, nb, cols, qrow, fs, ft, rt, qbuf, acc, (r2a, r2b), (fa, fb))
     if nb < nbp:
         perm_out[...] = jnp.zeros_like(perm_out)
     for i in range(nt):
         tile = slice(i * L, (i + 1) * L)
         sums = []
         for f in range(4):
-            h, m, l = (acc[i, pl.ds(p * 8 + f, nb, stride=SLOT), :] for p in range(3))
+            h, m, l = (acc[i, pl.ds(p * nb * 8 + f, nb, stride=8), :] for p in range(3))
             sums.append((h + m) + l)
         for a in range(3):
             perm_out[a * nbp : a * nbp + nb, tile] = xt[a][:nb, tile] * sums[3] - sums[a]
@@ -414,31 +407,47 @@
     return center_of(comps(m, 3), CONTR)
 
 
-def tensor_pairs(n, lst, size, fs, ft, qbuf, r2a, r2b, tensors):
+def tensor_of(e, r2, q, tensors):
+    for k in range(CONTR):
+        c, decay, inv, v = pair_basis(r2[k], q)
+        l3 = 1.0 - decay
+        l5 = l3 + (c * LN2) * decay
+        w3 = (v * v) * inv
+        w5 = w3 * (inv * inv)
+        a_hi, a_lo = two(w5 * l5)
+        b_hi, b_lo = two(w3 * l3)
+        tensors[k, e, 0:L, :] = a_hi
+        tensors[k, e, L : 2 * L, :] = a_lo
+        tensors[k, e, 2 * L : 3 * L, :] = b_hi
+        tensors[k, e, 3 * L : 4 * L, :] = b_lo
+
+
+def tensor_distances(s0, t0, fs, ft, r2):
+    lhs = fs[0, pl.ds(s0, L), :]
+    for k in range(CONTR):
+        r2[k] = dot(lhs, ft[k, :, pl.ds(t0, L)])
+
+
+def own_tensors(blocks, fs, ft, cols, qrow, r2s, tensors):
+    tensor_distances(blocks[0][0] * L, blocks[0][1] * L, fs, ft, r2s[0])
+    for e, (s, t) in enumerate(blocks):
+        if e + 1 < len(blocks):
+            tensor_distances(blocks[e + 1][0] * L, blocks[e + 1][1] * L, fs, ft, r2s[(e + 1) % 2])
+        tensor_of(e, r2s[e % 2], own_q(s, t, cols, qrow), tensors)
+
+
+def near_tensors(n, lst, size, fs, ft, cols, qrow, r2a, r2b, tensors):
     def where_is(i):
         e = jnp.maximum(jnp.minimum(i, n - 1), 0)
         return e, pl.multiple_of(lst[1 + e], L), pl.multiple_of(lst[1 + size + e], L)
 
     def tensor(i, r2):
-        e, _, _ = where_is(i)
-        for k in range(CONTR):
-            c, decay, inv, v = pair_basis(r2[k], qbuf[e])
-            l3 = 1.0 - decay
-            l5 = l3 + (c * LN2) * decay
-            w3 = (v * v) * inv
-            w5 = w3 * (inv * inv)
-            a_hi, a_lo = two(w5 * l5)
-            b_hi, b_lo = two(w3 * l3)
-            tensors[k, e, 0:L, :] = a_hi
-            tensors[k, e, L : 2 * L, :] = a_lo
-            tensors[k, e, 2 * L : 3 * L, :] = b_hi
-            tensors[k, e, 3 * L : 4 * L, :] = b_lo
+        e, s0, t0 = where_is(i)
+        tensor_of(e, r2, near_q(s0, t0, cols, qrow), tensors)
 
     def distances(i, r2):
         _, s0, t0 = where_is(i)
-        lhs = fs[0, pl.ds(s0, L), :]
-        for k in range(CONTR):
-            r2[k] = dot(lhs, ft[k, :, pl.ds(t0, L)])
+        tensor_distances(s0, t0, fs, ft, r2)
 
     def step(p, carry):
         distances(2 * p + 1, r2b)
@@ -541,7 +550,7 @@
             ev[a * CONTR + k : a * CONTR + k + 1, :] = 3.0 * full - sb[a : a + 1]
 
 
-def own_first_kernel(nbp, w, m0, pack, tensors, acc_a, acc_b, le, fs, ft, cols, qrow, qbuf, r2a, r2b, lst):
+def own_first_kernel(nbp, w, m0, pack, tensors, acc_a, acc_b, le, fs, ft, cols, qrow, r2a, r2b):
     misc = pack[3 * nbp : 3 * nbp + 8, :]
     pieces = pair_pieces(centered(m0, own_center(m0)))
     target_features(pieces, ft, CONTR)
@@ -549,10 +558,7 @@
     cols[...] = jnp.transpose(columns(misc))
     q_rows(misc, qrow)
     diag, off = own_blocks(w // L)
-    size = len(diag) + len(off)
-    fixed_list(lst, size, diag + off)
-    block_q(size, 0, lst, size, True, cols, qrow, qbuf)
-    tensor_pairs(size, lst, size, fs, ft, qbuf, r2a, r2b, tensors)
+    own_tensors(diag + off, fs, ft, cols, qrow, (r2a, r2b), tensors)
     own_sums(w, m0, m0, tensors, acc_a, acc_b, le)
 
 
@@ -566,7 +572,7 @@
 
 def near_first_kernel(
     nbp, w, m0, m0a, m0b, pack, packa, packb, cf, acc_a_in, acc_b_in,
-    mu_out, tensors, lst_out, acc_a, acc_b, fs, ft, cols, qrow, qbuf, r2a, r2b, le, ev, lst, sem,
+    mu_out, tensors, lst_out, acc_a, acc_b, fs, ft, cols, qrow, r2a, r2b, le, ev, lst, sem,
 ):
     nt = w // L
     base = 3 * nbp
@@ -584,11 +590,10 @@
     size = 2 * nt * nt
     near_list(lst, size, ranges(xt[0], misc[1:2], CONTR, w), sranges)
     leave = pltpu.make_async_copy(lst, lst_out, sem)
-    leave.start()
     q_rows(misc, qrow)
     n = lst[0]
-    block_q(n, 0, lst, size, False, cols, qrow, qbuf)
-    tensor_pairs(n, lst, size, fs, ft, qbuf, r2a, r2b, tensors)
+    leave.start()
+    near_tensors(n, lst, size, fs, ft, cols, qrow, r2a, r2b, tensors)
     near_sums(w, [m0a, m0b], [m0a, m0b], m0, tensors, lst, acc_a, acc_b, le, ev)
     mu_out[...] = update(pack, nbp, cf, ev)
     leave.wait()
@@ -676,11 +681,10 @@
     )
     packa, packb = exchange(pack)
 
-    def pair_scratch(nsrc, blocks):
+    def pair_scratch(nsrc):
         return [
             pltpu.VMEM((nsrc * w, 8), F32),
             pltpu.VMEM((8, w), F32),
-            pltpu.VMEM((blocks + 1, L, L), F32),
             pltpu.VMEM((4, L, L), F32),
             pltpu.VMEM((4, L, L), F32),
         ]
@@ -689,7 +693,8 @@
         return [
             pltpu.VMEM((-(-nb // 4), nsrc * w, DEEP), BF16),
             pltpu.VMEM((nb * SLOT, nsrc * w), BF16),
-            *pair_scratch(nsrc, blocks),
+            *pair_scratch(nsrc),
+            pltpu.VMEM((max(own_size, 2), L, L), F32),
             pltpu.VMEM((4, 2 * L, L), BF16),
             pltpu.VMEM((4, 2 * L, L), BF16),
             pltpu.SMEM((2 + 2 * blocks,), jnp.int32),
@@ -697,11 +702,11 @@
 
     acc, ft, order, pack = call(
         part(perm_own_kernel, nb, nbp, w),
-        [((nt, nb * SLOT, L), F32), ((nb, DEEP, w), BF16), ((w, w), BF16), ((rows, w), F32)], "perm_own",
+        [((nt, nb * 24, L), F32), ((nb, DEEP, w), BF16), ((w, w), BF16), ((rows, w), F32)], "perm_own",
         perm_scratch(1, own_size), (pack, sel),
     )
     perm, msg, _ = call(
-        part(perm_near_kernel, nb, nbp, w), [((3 * nbp, w), F32), ((6 * CONTR, w), F32), ((nt, nb * SLOT, L), F32)],
+        part(perm_near_kernel, nb, nbp, w), [((3 * nbp, w), F32), ((6 * CONTR, w), F32), ((nt, nb * 24, L), F32)],
         "perm_near", perm_scratch(2, near_size), (pack, packa, packb, sel, ft, acc, order), alias={5: 2},
     )
 
@@ -714,11 +719,11 @@
     )
     m0a, m0b = exchange(m0)
 
-    def tensor_scratch(nsrc, blocks):
+    def tensor_scratch(nsrc):
         return [
             pltpu.VMEM((1, nsrc * w, DEEP), BF16),
             pltpu.VMEM((CONTR, DEEP, w), BF16),
-            *pair_scratch(nsrc, blocks),
+            *pair_scratch(nsrc),
         ]
 
     accs = [((CONTR * 48, w), F32), ((CONTR * 24, w), F32)]
@@ -727,13 +732,13 @@
     own_scratch = [pltpu.VMEM((nt, 48 * KP, L), F32)]
     t_own, acc_a, acc_b = call(
         part(own_first_kernel, nbp, w), [((CONTR, own_size, 4 * L, L), BF16)] + accs, "own_0",
-        own_scratch + tensor_scratch(1, own_size) + [pltpu.SMEM((2 + 2 * own_size,), jnp.int32)],
+        own_scratch + tensor_scratch(1),
         (m0, pack),
     )
     mu, t_nbr, lst, _, _ = call(
         part(near_first_kernel, nbp, w),
         [((2 * KP, w), F32), ((CONTR, near_size, 4 * L, L), BF16), ((2 + 2 * near_size,), jnp.int32)] + accs, "near_0",
-        tensor_scratch(2, near_size) + near_scratch + list_scratch,
+        tensor_scratch(2) + near_scratch + list_scratch,
         (m0, m0a, m0b, pack, packa, packb, cf, acc_a, acc_b), any_out=(2,), alias={7: 3, 8: 4},
     )
     for step in range(1, ITERS):

time: 51.3 us -> 47.9 us (0.934)
  Pallas kernels: 29.2 us -> 25.9 us
  starting transfers between devices: 14.6 us -> 16.7 us
  waiting for transfers between devices: 6.31 us -> 4.21 us
    pallas_call x10, Pallas kernels: 29.2 us -> 25.9 us  [call(): pl.pallas_call(kernel, out_shape=[jax.ShapeDtypeStruct(s, d) for s, d in...]
    ppermute x4, starting transfers between devices: 12.4 us -> 15.1 us  [exchange(): far = lax.ppermute(x, 'space', swap_pairs(nspace, 1))]
    ppermute x4, waiting for transfers between devices: 4.7 us -> 2.6 us  [exchange(): far = lax.ppermute(x, 'space', swap_pairs(nspace, 1))]
    ppermute x4, starting transfers between devices: 0.87 us -> 0.28 us  [exchange(): near = lax.ppermute(x, 'space', swap_pairs(nspace, 0))]
  transfers between devices with their start and end apart: 9 -> 9, of which waited for: 3 -> 3; matrix products, arithmetic and copies ran while one was open for 0% -> 0% of each run, Pallas kernels for 24% -> 22%
where the time goes in v5:
time: 47.9 us; the launch traced here: 47.7 us
  Pallas kernels  25.9 us (54%)
  starting transfers between devices  16.7 us (35%)
  waiting for transfers between devices  4.21 us (9%)
  between operations  0.94 us (2%)
    pallas_call x10, Pallas kernels, call(): pl.pallas_call(kernel, out_shape=[jax.ShapeDtypeStruct(s, d) for s, d in...  25.9 us
    ppermute x4, starting transfers between devices, exchange(): far = lax.ppermute(x, 'space', swap_pairs(nspace, 1))  15.1 us
    ppermute x4, waiting for transfers between devices, exchange(): far = lax.ppermute(x, 'space', swap_pairs(nspace, 1))  2.6 us
    ppermute x1, waiting for transfers between devices, body(): other = lax.ppermute(msg, 'bead', [(0, 1), (1, 0)])  1.6 us
    ppermute x1, starting transfers between devices, body(): other = lax.ppermute(msg, 'bead', [(0, 1), (1, 0)])  1.27 us
  transfers between devices with their start and end apart: 9, of which 3 were waited for; matrix products, arithmetic and copies ran while one was open for 0% of the time, Pallas kernels for 22%

profile of v5, /device:TPU:21, one launch (start us, length us, event | category | flops | bytes accessed | tf_op | source)
XLA Modules:
  0.0 47.7 jit_solution(17278698632109184912)
XLA Ops:
  0.6 1.5 %pack.1 = (f32[56,384]{1,0:T(8,128)S(1)}, bf16[192,512]{1,0:T(8,128)(2,1)S(1)}) custom-call(f32[3,16,384]{2,1,0:T(8,128)} %bitcast.3, f32[384]{0:T(512)} %charge.1, f32[384]{0:T(512)} %polar.1, s32[384]{0:T(512)} %mol.1), custom_call_target="tpu_custom_call" | custom-call | tf_op jit(solution)/shard_map/pack/pallas_call | solution.py:641
  2.1 3.7 %collective-permute-start.1 = (f32[56,384]{1,0:T(8,128)S(1)}, f32[56,384]{1,0:T(8,128)S(1)}, u32[]{:S(2)}, u32[]{:S(2)}) collective-permute-start(f32[56,384]{1,0:T(8,128)S(1)} %get-tuple-element.26.tgt), channel_id=1, source_target_pairs={{1,2},{2,1},{3,4},{4,3},{5,6},{6,5},{7,8},{8,7},{9,10},{10,9},{11,... | collective-permute-start | bytes 258056 | tf_op jit(solution)/shard_map/ppermute | solution.py:666
  5.8 0.1 collective-permute-start
  5.9 5.0 %perm_own.1 = (f32[3,384,128]{2,1,0:T(8,128)S(1)}, bf16[16,96,384]{2,1,0:T(8,128)(2,1)S(1)}, bf16[384,384]{1,0:T(8,128)(2,1)S(1)}, f32[56,384]{1,0:T(8,128)S(1)}) custom-call(f32[56,384]{1,0:T(8,128)S(1)} %get-tuple-element.26.tgt, bf16[192,512]{1,0:T(8,128)(2,1)S(1)} %get-tuple-element.27.sel), custom_call_target="tpu_custom_call" | custom-call | tf_op jit(solution)/shard_map/perm_own/pallas_call | solution.py:641
  10.9 0.0 collective-permute-done.1.srcb.packb
  10.9 0.0 collective-permute-done.srca.packa
  10.9 6.1 %perm_near.1 = (f32[48,384]{1,0:T(8,128)S(1)}, f32[24,384]{1,0:T(8,128)S(1)}, f32[3,384,128]{2,1,0:T(8,128)S(1)}) custom-call(f32[56,384]{1,0:T(8,128)S(1)} %get-tuple-element.28.tgt.pack, f32[56,384]{1,0:T(8,128)S(1)} %collective-permute-done.srca.packa, f32[56,384]{1,0:T(8,128)S(1)} %collective-permute-done.1.srcb.packb, ...), custom_call_target="tpu_custom_call", output_to_operand_aliasing={{2}: (5, {})} | custom-call | tf_op jit(solution)/shard_map/perm_near/pallas_call | solution.py:641
  17.1 1.3 %collective-permute-start.2 = (f32[24,384]{1,0:T(8,128)S(1)}, f32[24,384]{1,0:T(8,128)S(1)}, u32[]{:S(2)}, u32[]{:S(2)}) collective-permute-start(f32[24,384]{1,0:T(8,128)S(1)} %get-tuple-element.32.msg), channel_id=1, source_target_pairs={{0,16},{16,0},{1,17},{17,1},{2,18},{18,2},{3,19},{19,3},{4,20},{20... | collective-permute-start | bytes 110600 | tf_op jit(solution)/shard_map/ppermute | solution.py:714
  18.3 1.6 %collective-permute-done.2.other = f32[24,384]{1,0:T(8,128)S(1)} collective-permute-done((f32[24,384]{1,0:T(8,128)S(1)}, f32[24,384]{1,0:T(8,128)S(1)}, u32[]{:S(2)}, u32[]{:S(2)}) %collective-permute-start.2) | collective-permute-done | bytes 36896 | tf_op jit(solution)/shard_map/ppermute | solution.py:714
  19.9 0.2 start.1
  20.2 4.7 %collective-permute-start.4 = (f32[24,384]{1,0:T(8,128)S(1)}, f32[24,384]{1,0:T(8,128)S(1)}, u32[]{:S(2)}, u32[]{:S(2)}) collective-permute-start(f32[24,384]{1,0:T(8,128)S(1)} %get-tuple-element.33.m0), channel_id=1, source_target_pairs={{1,2},{2,1},{3,4},{4,3},{5,6},{6,5},{7,8},{8,7},{9,10},{10,9},{11,... | collective-permute-start | bytes 110600 | tf_op jit(solution)/shard_map/ppermute | solution.py:666
  24.9 0.1 collective-permute-start.3
  24.9 2.8 %own_0.1 = (bf16[4,6,512,128]{3,2,1,0:T(8,128)(2,1)S(1)}, f32[192,384]{1,0:T(8,128)S(1)}, f32[96,384]{1,0:T(8,128)S(1)}) custom-call(f32[24,384]{1,0:T(8,128)S(1)} %get-tuple-element.33.m0, f32[56,384]{1,0:T(8,128)S(1)} %get-tuple-element.28.tgt.pack), custom_call_target="tpu_custom_call" | custom-call | tf_op jit(solution)/shard_map/own_0/pallas_call | solution.py:641
  27.7 0.0 collective-permute-done.4.m0b
  27.7 0.0 collective-permute-done.3.m0a
  27.8 3.5 %near_0.1 = (f32[16,384]{1,0:T(8,128)S(1)}, bf16[4,18,512,128]{3,2,1,0:T(8,128)(2,1)S(1)}, s32[38]{0:T(128)S(1)}, f32[192,384]{1,0:T(8,128)S(1)}, f32[96,384]{1,0:T(8,128)S(1)}) custom-call(f32[24,384]{1,0:T(8,128)S(1)} %get-tuple-element.33.m0, f32[24,384]{1,0:T(8,128)S(1)} %collective-permute-done.3.m0a, ...), custom_call_target="tpu_custom_call", output_to_operand_aliasing={{3}: (7, {}), {4}: (8, {})} | custom-call | tf_op jit(solution)/shard_map/near_0/pallas_call | solution.py:641
  31.3 3.5 %collective-permute-start.6 = (f32[16,384]{1,0:T(8,128)S(1)}, f32[16,384]{1,0:T(8,128)S(1)}, u32[]{:S(2)}, u32[]{:S(2)}) collective-permute-start(f32[16,384]{1,0:T(8,128)S(1)} %get-tuple-element.37.mu), channel_id=1, source_target_pairs={{1,2},{2,1},{3,4},{4,3},{5,6},{6,5},{7,8},{8,7},{9,10},{10,9},{11,... | collective-permute-start | bytes 73736 | tf_op jit(solution)/shard_map/ppermute | solution.py:666
  34.8 0.1 collective-permute-start.5
  34.8 1.2 %own_1.1 = (f32[192,384]{1,0:T(8,128)S(1)}, f32[96,384]{1,0:T(8,128)S(1)}) custom-call(f32[16,384]{1,0:T(8,128)S(1)} %get-tuple-element.37.mu, f32[24,384]{1,0:T(8,128)S(1)} %get-tuple-element.33.m0, bf16[4,6,512,128]{3,2,1,0:T(8,128)(2,1)S(1)} %get-tuple-element.38.tensors), custom_call_target="tpu_custom_call" | custom-call | tf_op jit(solution)/shard_map/own_1/pallas_call | solution.py:641
  36.1 1.3 %collective-permute-done.6.mub = f32[16,384]{1,0:T(8,128)S(1)} collective-permute-done((f32[16,384]{1,0:T(8,128)S(1)}, f32[16,384]{1,0:T(8,128)S(1)}, u32[]{:S(2)}, u32[]{:S(2)}) %collective-permute-start.6) | collective-permute-done | bytes 24608 | tf_op jit(solution)/shard_map/ppermute | solution.py:666
  37.3 0.0 collective-permute-done.5.mua
  37.3 1.5 %near_1.1 = (f32[16,384]{1,0:T(8,128)S(1)}, f32[192,384]{1,0:T(8,128)S(1)}, f32[96,384]{1,0:T(8,128)S(1)}) custom-call(f32[16,384]{1,0:T(8,128)S(1)} %collective-permute-done.5.mua, f32[16,384]{1,0:T(8,128)S(1)} %collective-permute-done.6.mub, f32[24,384]{1,0:T(8,128)S(1)} %get-tuple-element.33.m0, ...), custom_call_target="tpu_custom_call", output_to_operand_aliasing={{1}: (7, {}), {2}: (8, {})} | custom-call | tf_op jit(solution)/shard_map/near_1/pallas_call | solution.py:641
  38.9 3.3 %collective-permute-start.8 = (f32[16,384]{1,0:T(8,128)S(1)}, f32[16,384]{1,0:T(8,128)S(1)}, u32[]{:S(2)}, u32[]{:S(2)}) collective-permute-start(f32[16,384]{1,0:T(8,128)S(1)} %get-tuple-element.43.mu), channel_id=1, source_target_pairs={{1,2},{2,1},{3,4},{4,3},{5,6},{6,5},{7,8},{8,7},{9,10},{10,9},{11,... | collective-permute-start | bytes 73736 | tf_op jit(solution)/shard_map/ppermute | solution.py:666
  42.2 0.1 collective-permute-start.7
  42.3 1.3 %own_last.1 = (f32[192,384]{1,0:T(8,128)S(1)}, f32[96,384]{1,0:T(8,128)S(1)}, f32[48,384]{1,0:T(8,128)S(1)}) custom-call(f32[16,384]{1,0:T(8,128)S(1)} %get-tuple-element.43.mu, f32[24,384]{1,0:T(8,128)S(1)} %get-tuple-element.33.m0, bf16[4,6,512,128]{3,2,1,0:T(8,128)(2,1)S(1)} %get-tuple-element.38.tensors, f32[48,384]{1,0:T(8,128)S(1)} %get-tuple-element.44.perm, ...), custom_call_target="tpu_custom_call" | custom-call | tf_op jit(solution)/shard_map/own_last/pallas_call | solution.py:641
  43.6 1.3 %collective-permute-done.8.mub = f32[16,384]{1,0:T(8,128)S(1)} collective-permute-done((f32[16,384]{1,0:T(8,128)S(1)}, f32[16,384]{1,0:T(8,128)S(1)}, u32[]{:S(2)}, u32[]{:S(2)}) %collective-permute-start.8) | collective-permute-done | bytes 24608 | tf_op jit(solution)/shard_map/ppermute | solution.py:666
  44.9 0.0 collective-permute-done.7.mua
  44.9 2.6 %final.1 = (f32[3,16,384]{2,1,0:T(8,128)}, f32[3,4,384]{2,1,0:T(4,128)}, f32[192,384]{1,0:T(8,128)S(1)}, f32[96,384]{1,0:T(8,128)S(1)}) custom-call(f32[16,384]{1,0:T(8,128)S(1)} %collective-permute-done.7.mua, f32[16,384]{1,0:T(8,128)S(1)} %collective-permute-done.8.mub, ...), custom_call_target="tpu_custom_call", output_to_operand_aliasing={{2}: (8, {}), {3}: (9, {})} | custom-call | tf_op jit(solution)/shard_map/final/pallas_call | solution.py:641
Async XLA Ops:
  2.1 8.8 %collective-permute-start.1 = (f32[56,384]{1,0:T(8,128)S(1)}, f32[56,384]{1,0:T(8,128)S(1)}, u32[]{:S(2)}, u32[]{:S(2)}) collective-permute-start(f32[56,384]{1,0:T(8,128)S(1)} %get-tuple-element.26.tgt), channel_id=1, source_target_pairs={{1,2},{2,1},{3,4},{4,3},{5,6},{6,5},{7,8},{8,7},{9,10},{10,9},{11,... | collective-permute-start | bytes 258056 | tf_op jit(solution)/shard_map/ppermute | solution.py:666
  5.8 5.1 %collective-permute-start = (f32[56,384]{1,0:T(8,128)S(1)}, f32[56,384]{1,0:T(8,128)S(1)}, u32[]{:S(2)}, u32[]{:S(2)}) collective-permute-start(f32[56,384]{1,0:T(8,128)S(1)} %get-tuple-element.26.tgt), channel_id=1, source_target_pairs={{0,1},{1,0},{2,3},{3,2},{4,5},{5,4},{6,7},{7,6},{8,9},{9,8},{10,11... | collective-permute-start | bytes 258056 | tf_op jit(solution)/shard_map/ppermute | solution.py:665
  17.1 2.9 %collective-permute-start.2 = (f32[24,384]{1,0:T(8,128)S(1)}, f32[24,384]{1,0:T(8,128)S(1)}, u32[]{:S(2)}, u32[]{:S(2)}) collective-permute-start(f32[24,384]{1,0:T(8,128)S(1)} %get-tuple-element.32.msg), channel_id=1, source_target_pairs={{0,16},{16,0},{1,17},{17,1},{2,18},{18,2},{3,19},{19,3},{4,20},{20... | collective-permute-start | bytes 110600 | tf_op jit(solution)/shard_map/ppermute | solution.py:714
  20.2 7.6 %collective-permute-start.4 = (f32[24,384]{1,0:T(8,128)S(1)}, f32[24,384]{1,0:T(8,128)S(1)}, u32[]{:S(2)}, u32[]{:S(2)}) collective-permute-start(f32[24,384]{1,0:T(8,128)S(1)} %get-tuple-element.33.m0), channel_id=1, source_target_pairs={{1,2},{2,1},{3,4},{4,3},{5,6},{6,5},{7,8},{8,7},{9,10},{10,9},{11,... | collective-permute-start | bytes 110600 | tf_op jit(solution)/shard_map/ppermute | solution.py:666
  24.9 2.9 %collective-permute-start.3 = (f32[24,384]{1,0:T(8,128)S(1)}, f32[24,384]{1,0:T(8,128)S(1)}, u32[]{:S(2)}, u32[]{:S(2)}) collective-permute-start(f32[24,384]{1,0:T(8,128)S(1)} %get-tuple-element.33.m0), channel_id=1, source_target_pairs={{0,1},{1,0},{2,3},{3,2},{4,5},{5,4},{6,7},{7,6},{8,9},{9,8},{10,11... | collective-permute-start | bytes 110600 | tf_op jit(solution)/shard_map/ppermute | solution.py:665
  31.3 6.0 %collective-permute-start.6 = (f32[16,384]{1,0:T(8,128)S(1)}, f32[16,384]{1,0:T(8,128)S(1)}, u32[]{:S(2)}, u32[]{:S(2)}) collective-permute-start(f32[16,384]{1,0:T(8,128)S(1)} %get-tuple-element.37.mu), channel_id=1, source_target_pairs={{1,2},{2,1},{3,4},{4,3},{5,6},{6,5},{7,8},{8,7},{9,10},{10,9},{11,... | collective-permute-start | bytes 73736 | tf_op jit(solution)/shard_map/ppermute | solution.py:666
  34.8 2.6 %collective-permute-start.5 = (f32[16,384]{1,0:T(8,128)S(1)}, f32[16,384]{1,0:T(8,128)S(1)}, u32[]{:S(2)}, u32[]{:S(2)}) collective-permute-start(f32[16,384]{1,0:T(8,128)S(1)} %get-tuple-element.37.mu), channel_id=1, source_target_pairs={{0,1},{1,0},{2,3},{3,2},{4,5},{5,4},{6,7},{7,6},{8,9},{9,8},{10,11... | collective-permute-start | bytes 73736 | tf_op jit(solution)/shard_map/ppermute | solution.py:665
  38.9 6.0 %collective-permute-start.8 = (f32[16,384]{1,0:T(8,128)S(1)}, f32[16,384]{1,0:T(8,128)S(1)}, u32[]{:S(2)}, u32[]{:S(2)}) collective-permute-start(f32[16,384]{1,0:T(8,128)S(1)} %get-tuple-element.43.mu), channel_id=1, source_target_pairs={{1,2},{2,1},{3,4},{4,3},{5,6},{6,5},{7,8},{8,7},{9,10},{10,9},{11,... | collective-permute-start | bytes 73736 | tf_op jit(solution)/shard_map/ppermute | solution.py:666
  42.2 2.8 %collective-permute-start.7 = (f32[16,384]{1,0:T(8,128)S(1)}, f32[16,384]{1,0:T(8,128)S(1)}, u32[]{:S(2)}, u32[]{:S(2)}) collective-permute-start(f32[16,384]{1,0:T(8,128)S(1)} %get-tuple-element.43.mu), channel_id=1, source_target_pairs={{0,1},{1,0},{2,3},{3,2},{4,5},{5,4},{6,7},{7,6},{8,9},{9,8},{10,11... | collective-permute-start | bytes 73736 | tf_op jit(solution)/shard_map/ppermute | solution.py:665

commit v6 on v5

--- a/solution.py
+++ b/solution.py
@@ -81,9 +81,10 @@
 def target_features(pieces, ft, count):
     for g in range(-(-count // 4)):
         stack = slot_stack(pieces, T_SLOTS, g)
+        stack = stack.astype(BF16)
         row = lax.broadcasted_iota(jnp.int32, stack.shape, 0) % 4
         for i in range(min(4, count - g * 4)):
-            ft[g * 4 + i] = jnp.where(row == i, stack, 0.0).astype(BF16)
+            ft[g * 4 + i] = stack * jnp.where(row == i, 1.0, 0.0).astype(BF16)
 
 
 def source_features(pieces, fs, s, w, count):
@@ -524,17 +525,17 @@
             acc_a[a0 : a0 + 48, pl.ds(t0, L)] += dot(twice(fa), tensors[k, e, 0 : 2 * L, :])
             acc_b[b0 : b0 + 24, pl.ds(t0, L)] += dot(twice(fb), tensors[k, e, 2 * L : 4 * L, :])
 
-    def both(i, carry):
-        add(2 * i)
-        add(2 * i + 1)
+    def three(i, carry):
+        for j in range(3):
+            add(3 * i + j)
         return carry
 
     def single(i, carry):
-        add(lst[0] - 1)
+        add(lst[0] // 3 * 3 + i)
         return carry
 
-    lax.fori_loop(0, lst[0] // 2, both, 0)
-    lax.fori_loop(0, lst[0] % 2, single, 0)
+    lax.fori_loop(0, lst[0] // 3, three, 0)
+    lax.fori_loop(0, lst[0] % 3, single, 0)
     ev[...] = jnp.zeros_like(ev)
     xt = centered(m0, center)
     for k in range(CONTR):

time: 47.9 us -> 47.6 us (level)
  no operation moved by 1% of the time
where the time goes in v6:
time: 47.6 us; the launch traced here: 47.3 us
  Pallas kernels  25.5 us (54%)
  starting transfers between devices  16.7 us (35%)
  waiting for transfers between devices  4.21 us (9%)
  between operations  0.94 us (2%)
    pallas_call x10, Pallas kernels, call(): pl.pallas_call(kernel, out_shape=[jax.ShapeDtypeStruct(s, d) for s, d in...  25.5 us
    ppermute x4, starting transfers between devices, exchange(): far = lax.ppermute(x, 'space', swap_pairs(nspace, 1))  15.1 us
    ppermute x4, waiting for transfers between devices, exchange(): far = lax.ppermute(x, 'space', swap_pairs(nspace, 1))  2.6 us
    ppermute x1, waiting for transfers between devices, body(): other = lax.ppermute(msg, 'bead', [(0, 1), (1, 0)])  1.6 us
    ppermute x1, starting transfers between devices, body(): other = lax.ppermute(msg, 'bead', [(0, 1), (1, 0)])  1.27 us
  transfers between devices with their start and end apart: 9, of which 3 were waited for; matrix products, arithmetic and copies ran while one was open for 0% of the time, Pallas kernels for 22%

profile of v6, /device:TPU:21, one launch (start us, length us, event | category | flops | bytes accessed | tf_op | source)
XLA Modules:
  0.0 47.3 jit_solution(8564611760005197845)
XLA Ops:
  0.6 1.5 %pack.1 = (f32[56,384]{1,0:T(8,128)S(1)}, bf16[192,512]{1,0:T(8,128)(2,1)S(1)}) custom-call(f32[3,16,384]{2,1,0:T(8,128)} %bitcast.3, f32[384]{0:T(512)} %charge.1, f32[384]{0:T(512)} %polar.1, s32[384]{0:T(512)} %mol.1), custom_call_target="tpu_custom_call" | custom-call | tf_op jit(solution)/shard_map/pack/pallas_call | solution.py:642
  2.1 3.7 %collective-permute-start.1 = (f32[56,384]{1,0:T(8,128)S(1)}, f32[56,384]{1,0:T(8,128)S(1)}, u32[]{:S(2)}, u32[]{:S(2)}) collective-permute-start(f32[56,384]{1,0:T(8,128)S(1)} %get-tuple-element.26.tgt), channel_id=1, source_target_pairs={{1,2},{2,1},{3,4},{4,3},{5,6},{6,5},{7,8},{8,7},{9,10},{10,9},{11,... | collective-permute-start | bytes 258056 | tf_op jit(solution)/shard_map/ppermute | solution.py:667
  5.8 0.1 collective-permute-start
  5.9 4.9 %perm_own.1 = (f32[3,384,128]{2,1,0:T(8,128)S(1)}, bf16[16,96,384]{2,1,0:T(8,128)(2,1)S(1)}, bf16[384,384]{1,0:T(8,128)(2,1)S(1)}, f32[56,384]{1,0:T(8,128)S(1)}) custom-call(f32[56,384]{1,0:T(8,128)S(1)} %get-tuple-element.26.tgt, bf16[192,512]{1,0:T(8,128)(2,1)S(1)} %get-tuple-element.27.sel), custom_call_target="tpu_custom_call" | custom-call | tf_op jit(solution)/shard_map/perm_own/pallas_call | solution.py:642
  10.9 0.0 collective-permute-done.1.srcb.packb
  10.9 0.0 collective-permute-done.srca.packa
  10.9 6.1 %perm_near.1 = (f32[48,384]{1,0:T(8,128)S(1)}, f32[24,384]{1,0:T(8,128)S(1)}, f32[3,384,128]{2,1,0:T(8,128)S(1)}) custom-call(f32[56,384]{1,0:T(8,128)S(1)} %get-tuple-element.28.tgt.pack, f32[56,384]{1,0:T(8,128)S(1)} %collective-permute-done.srca.packa, f32[56,384]{1,0:T(8,128)S(1)} %collective-permute-done.1.srcb.packb, ...), custom_call_target="tpu_custom_call", output_to_operand_aliasing={{2}: (5, {})} | custom-call | tf_op jit(solution)/shard_map/perm_near/pallas_call | solution.py:642
  17.0 1.3 %collective-permute-start.2 = (f32[24,384]{1,0:T(8,128)S(1)}, f32[24,384]{1,0:T(8,128)S(1)}, u32[]{:S(2)}, u32[]{:S(2)}) collective-permute-start(f32[24,384]{1,0:T(8,128)S(1)} %get-tuple-element.32.msg), channel_id=1, source_target_pairs={{0,16},{16,0},{1,17},{17,1},{2,18},{18,2},{3,19},{19,3},{4,20},{20... | collective-permute-start | bytes 110600 | tf_op jit(solution)/shard_map/ppermute | solution.py:715
  18.3 1.6 %collective-permute-done.2.other = f32[24,384]{1,0:T(8,128)S(1)} collective-permute-done((f32[24,384]{1,0:T(8,128)S(1)}, f32[24,384]{1,0:T(8,128)S(1)}, u32[]{:S(2)}, u32[]{:S(2)}) %collective-permute-start.2) | collective-permute-done | bytes 36896 | tf_op jit(solution)/shard_map/ppermute | solution.py:715
  19.9 0.2 start.1
  20.1 4.7 %collective-permute-start.4 = (f32[24,384]{1,0:T(8,128)S(1)}, f32[24,384]{1,0:T(8,128)S(1)}, u32[]{:S(2)}, u32[]{:S(2)}) collective-permute-start(f32[24,384]{1,0:T(8,128)S(1)} %get-tuple-element.33.m0), channel_id=1, source_target_pairs={{1,2},{2,1},{3,4},{4,3},{5,6},{6,5},{7,8},{8,7},{9,10},{10,9},{11,... | collective-permute-start | bytes 110600 | tf_op jit(solution)/shard_map/ppermute | solution.py:667
  24.8 0.1 collective-permute-start.3
  24.9 2.8 %own_0.1 = (bf16[4,6,512,128]{3,2,1,0:T(8,128)(2,1)S(1)}, f32[192,384]{1,0:T(8,128)S(1)}, f32[96,384]{1,0:T(8,128)S(1)}) custom-call(f32[24,384]{1,0:T(8,128)S(1)} %get-tuple-element.33.m0, f32[56,384]{1,0:T(8,128)S(1)} %get-tuple-element.28.tgt.pack), custom_call_target="tpu_custom_call" | custom-call | tf_op jit(solution)/shard_map/own_0/pallas_call | solution.py:642
  27.7 0.0 collective-permute-done.4.m0b
  27.7 0.0 collective-permute-done.3.m0a
  27.7 3.4 %near_0.1 = (f32[16,384]{1,0:T(8,128)S(1)}, bf16[4,18,512,128]{3,2,1,0:T(8,128)(2,1)S(1)}, s32[38]{0:T(128)S(1)}, f32[192,384]{1,0:T(8,128)S(1)}, f32[96,384]{1,0:T(8,128)S(1)}) custom-call(f32[24,384]{1,0:T(8,128)S(1)} %get-tuple-element.33.m0, f32[24,384]{1,0:T(8,128)S(1)} %collective-permute-done.3.m0a, ...), custom_call_target="tpu_custom_call", output_to_operand_aliasing={{3}: (7, {}), {4}: (8, {})} | custom-call | tf_op jit(solution)/shard_map/near_0/pallas_call | solution.py:642
  31.1 3.5 %collective-permute-start.6 = (f32[16,384]{1,0:T(8,128)S(1)}, f32[16,384]{1,0:T(8,128)S(1)}, u32[]{:S(2)}, u32[]{:S(2)}) collective-permute-start(f32[16,384]{1,0:T(8,128)S(1)} %get-tuple-element.37.mu), channel_id=1, source_target_pairs={{1,2},{2,1},{3,4},{4,3},{5,6},{6,5},{7,8},{8,7},{9,10},{10,9},{11,... | collective-permute-start | bytes 73736 | tf_op jit(solution)/shard_map/ppermute | solution.py:667
  34.6 0.1 collective-permute-start.5
  34.7 1.2 %own_1.1 = (f32[192,384]{1,0:T(8,128)S(1)}, f32[96,384]{1,0:T(8,128)S(1)}) custom-call(f32[16,384]{1,0:T(8,128)S(1)} %get-tuple-element.37.mu, f32[24,384]{1,0:T(8,128)S(1)} %get-tuple-element.33.m0, bf16[4,6,512,128]{3,2,1,0:T(8,128)(2,1)S(1)} %get-tuple-element.38.tensors), custom_call_target="tpu_custom_call" | custom-call | tf_op jit(solution)/shard_map/own_1/pallas_call | solution.py:642
  35.9 1.3 %collective-permute-done.6.mub = f32[16,384]{1,0:T(8,128)S(1)} collective-permute-done((f32[16,384]{1,0:T(8,128)S(1)}, f32[16,384]{1,0:T(8,128)S(1)}, u32[]{:S(2)}, u32[]{:S(2)}) %collective-permute-start.6) | collective-permute-done | bytes 24608 | tf_op jit(solution)/shard_map/ppermute | solution.py:667
  37.2 0.0 collective-permute-done.5.mua
  37.2 1.4 %near_1.1 = (f32[16,384]{1,0:T(8,128)S(1)}, f32[192,384]{1,0:T(8,128)S(1)}, f32[96,384]{1,0:T(8,128)S(1)}) custom-call(f32[16,384]{1,0:T(8,128)S(1)} %collective-permute-done.5.mua, f32[16,384]{1,0:T(8,128)S(1)} %collective-permute-done.6.mub, f32[24,384]{1,0:T(8,128)S(1)} %get-tuple-element.33.m0, ...), custom_call_target="tpu_custom_call", output_to_operand_aliasing={{1}: (7, {}), {2}: (8, {})} | custom-call | tf_op jit(solution)/shard_map/near_1/pallas_call | solution.py:642
  38.6 3.3 %collective-permute-start.8 = (f32[16,384]{1,0:T(8,128)S(1)}, f32[16,384]{1,0:T(8,128)S(1)}, u32[]{:S(2)}, u32[]{:S(2)}) collective-permute-start(f32[16,384]{1,0:T(8,128)S(1)} %get-tuple-element.43.mu), channel_id=1, source_target_pairs={{1,2},{2,1},{3,4},{4,3},{5,6},{6,5},{7,8},{8,7},{9,10},{10,9},{11,... | collective-permute-start | bytes 73736 | tf_op jit(solution)/shard_map/ppermute | solution.py:667
  41.9 0.1 collective-permute-start.7
  42.0 1.3 %own_last.1 = (f32[192,384]{1,0:T(8,128)S(1)}, f32[96,384]{1,0:T(8,128)S(1)}, f32[48,384]{1,0:T(8,128)S(1)}) custom-call(f32[16,384]{1,0:T(8,128)S(1)} %get-tuple-element.43.mu, f32[24,384]{1,0:T(8,128)S(1)} %get-tuple-element.33.m0, bf16[4,6,512,128]{3,2,1,0:T(8,128)(2,1)S(1)} %get-tuple-element.38.tensors, f32[48,384]{1,0:T(8,128)S(1)} %get-tuple-element.44.perm, ...), custom_call_target="tpu_custom_call" | custom-call | tf_op jit(solution)/shard_map/own_last/pallas_call | solution.py:642
  43.3 1.3 %collective-permute-done.8.mub = f32[16,384]{1,0:T(8,128)S(1)} collective-permute-done((f32[16,384]{1,0:T(8,128)S(1)}, f32[16,384]{1,0:T(8,128)S(1)}, u32[]{:S(2)}, u32[]{:S(2)}) %collective-permute-start.8) | collective-permute-done | bytes 24608 | tf_op jit(solution)/shard_map/ppermute | solution.py:667
  44.7 0.0 collective-permute-done.7.mua
  44.7 2.5 %final.1 = (f32[3,16,384]{2,1,0:T(8,128)}, f32[3,4,384]{2,1,0:T(4,128)}, f32[192,384]{1,0:T(8,128)S(1)}, f32[96,384]{1,0:T(8,128)S(1)}) custom-call(f32[16,384]{1,0:T(8,128)S(1)} %collective-permute-done.7.mua, f32[16,384]{1,0:T(8,128)S(1)} %collective-permute-done.8.mub, ...), custom_call_target="tpu_custom_call", output_to_operand_aliasing={{2}: (8, {}), {3}: (9, {})} | custom-call | tf_op jit(solution)/shard_map/final/pallas_call | solution.py:642
Async XLA Ops:
  2.1 8.7 %collective-permute-start.1 = (f32[56,384]{1,0:T(8,128)S(1)}, f32[56,384]{1,0:T(8,128)S(1)}, u32[]{:S(2)}, u32[]{:S(2)}) collective-permute-start(f32[56,384]{1,0:T(8,128)S(1)} %get-tuple-element.26.tgt), channel_id=1, source_target_pairs={{1,2},{2,1},{3,4},{4,3},{5,6},{6,5},{7,8},{8,7},{9,10},{10,9},{11,... | collective-permute-start | bytes 258056 | tf_op jit(solution)/shard_map/ppermute | solution.py:667
  5.8 5.0 %collective-permute-start = (f32[56,384]{1,0:T(8,128)S(1)}, f32[56,384]{1,0:T(8,128)S(1)}, u32[]{:S(2)}, u32[]{:S(2)}) collective-permute-start(f32[56,384]{1,0:T(8,128)S(1)} %get-tuple-element.26.tgt), channel_id=1, source_target_pairs={{0,1},{1,0},{2,3},{3,2},{4,5},{5,4},{6,7},{7,6},{8,9},{9,8},{10,11... | collective-permute-start | bytes 258056 | tf_op jit(solution)/shard_map/ppermute | solution.py:666
  17.0 2.9 %collective-permute-start.2 = (f32[24,384]{1,0:T(8,128)S(1)}, f32[24,384]{1,0:T(8,128)S(1)}, u32[]{:S(2)}, u32[]{:S(2)}) collective-permute-start(f32[24,384]{1,0:T(8,128)S(1)} %get-tuple-element.32.msg), channel_id=1, source_target_pairs={{0,16},{16,0},{1,17},{17,1},{2,18},{18,2},{3,19},{19,3},{4,20},{20... | collective-permute-start | bytes 110600 | tf_op jit(solution)/shard_map/ppermute | solution.py:715
  20.1 7.6 %collective-permute-start.4 = (f32[24,384]{1,0:T(8,128)S(1)}, f32[24,384]{1,0:T(8,128)S(1)}, u32[]{:S(2)}, u32[]{:S(2)}) collective-permute-start(f32[24,384]{1,0:T(8,128)S(1)} %get-tuple-element.33.m0), channel_id=1, source_target_pairs={{1,2},{2,1},{3,4},{4,3},{5,6},{6,5},{7,8},{8,7},{9,10},{10,9},{11,... | collective-permute-start | bytes 110600 | tf_op jit(solution)/shard_map/ppermute | solution.py:667
  24.8 2.9 %collective-permute-start.3 = (f32[24,384]{1,0:T(8,128)S(1)}, f32[24,384]{1,0:T(8,128)S(1)}, u32[]{:S(2)}, u32[]{:S(2)}) collective-permute-start(f32[24,384]{1,0:T(8,128)S(1)} %get-tuple-element.33.m0), channel_id=1, source_target_pairs={{0,1},{1,0},{2,3},{3,2},{4,5},{5,4},{6,7},{7,6},{8,9},{9,8},{10,11... | collective-permute-start | bytes 110600 | tf_op jit(solution)/shard_map/ppermute | solution.py:666
  31.1 6.0 %collective-permute-start.6 = (f32[16,384]{1,0:T(8,128)S(1)}, f32[16,384]{1,0:T(8,128)S(1)}, u32[]{:S(2)}, u32[]{:S(2)}) collective-permute-start(f32[16,384]{1,0:T(8,128)S(1)} %get-tuple-element.37.mu), channel_id=1, source_target_pairs={{1,2},{2,1},{3,4},{4,3},{5,6},{6,5},{7,8},{8,7},{9,10},{10,9},{11,... | collective-permute-start | bytes 73736 | tf_op jit(solution)/shard_map/ppermute | solution.py:667
  34.6 2.6 %collective-permute-start.5 = (f32[16,384]{1,0:T(8,128)S(1)}, f32[16,384]{1,0:T(8,128)S(1)}, u32[]{:S(2)}, u32[]{:S(2)}) collective-permute-start(f32[16,384]{1,0:T(8,128)S(1)} %get-tuple-element.37.mu), channel_id=1, source_target_pairs={{0,1},{1,0},{2,3},{3,2},{4,5},{5,4},{6,7},{7,6},{8,9},{9,8},{10,11... | collective-permute-start | bytes 73736 | tf_op jit(solution)/shard_map/ppermute | solution.py:666
  38.6 6.0 %collective-permute-start.8 = (f32[16,384]{1,0:T(8,128)S(1)}, f32[16,384]{1,0:T(8,128)S(1)}, u32[]{:S(2)}, u32[]{:S(2)}) collective-permute-start(f32[16,384]{1,0:T(8,128)S(1)} %get-tuple-element.43.mu), channel_id=1, source_target_pairs={{1,2},{2,1},{3,4},{4,3},{5,6},{6,5},{7,8},{8,7},{9,10},{10,9},{11,... | collective-permute-start | bytes 73736 | tf_op jit(solution)/shard_map/ppermute | solution.py:667
  41.9 2.8 %collective-permute-start.7 = (f32[16,384]{1,0:T(8,128)S(1)}, f32[16,384]{1,0:T(8,128)S(1)}, u32[]{:S(2)}, u32[]{:S(2)}) collective-permute-start(f32[16,384]{1,0:T(8,128)S(1)} %get-tuple-element.43.mu), channel_id=1, source_target_pairs={{0,1},{1,0},{2,3},{3,2},{4,5},{5,4},{6,7},{7,6},{8,9},{9,8},{10,11... | collective-permute-start | bytes 73736 | tf_op jit(solution)/shard_map/ppermute | solution.py:666

commit v7 on v6

--- a/solution.py
+++ b/solution.py
@@ -437,7 +437,7 @@
         tensor_of(e, r2s[e % 2], own_q(s, t, cols, qrow), tensors)
 
 
-def near_tensors(n, lst, size, fs, ft, cols, qrow, r2a, r2b, tensors):
+def near_tensors(n, lst, size, fs, ft, cols, qrow, r2a, r2b, r2c, tensors):
     def where_is(i):
         e = jnp.maximum(jnp.minimum(i, n - 1), 0)
         return e, pl.multiple_of(lst[1 + e], L), pl.multiple_of(lst[1 + size + e], L)
@@ -451,14 +451,23 @@
         tensor_distances(s0, t0, fs, ft, r2)
 
     def step(p, carry):
-        distances(2 * p + 1, r2b)
-        tensor(2 * p, r2a)
-        distances(2 * p + 2, r2a)
-        tensor(2 * p + 1, r2b)
+        distances(3 * p + 1, r2b)
+        tensor(3 * p, r2a)
+        distances(3 * p + 2, r2c)
+        tensor(3 * p + 1, r2b)
+        distances(3 * p + 3, r2a)
+        tensor(3 * p + 2, r2c)
         return carry
 
+    def single(i, carry):
+        e = n // 3 * 3 + i
+        tensor(e, r2a)
+        distances(e + 1, r2a)
+        return carry
+
     distances(0, r2a)
-    lax.fori_loop(0, (n + 1) // 2, step, 0)
+    lax.fori_loop(0, n // 3, step, 0)
+    lax.fori_loop(0, n % 3, single, 0)
 
 
 def induce_features(mu, x, le, s, w):
@@ -573,7 +582,7 @@
 
 def near_first_kernel(
     nbp, w, m0, m0a, m0b, pack, packa, packb, cf, acc_a_in, acc_b_in,
-    mu_out, tensors, lst_out, acc_a, acc_b, fs, ft, cols, qrow, r2a, r2b, le, ev, lst, sem,
+    mu_out, tensors, lst_out, acc_a, acc_b, fs, ft, cols, qrow, r2a, r2b, r2c, le, ev, lst, sem,
 ):
     nt = w // L
     base = 3 * nbp
@@ -594,7 +603,7 @@
     q_rows(misc, qrow)
     n = lst[0]
     leave.start()
-    near_tensors(n, lst, size, fs, ft, cols, qrow, r2a, r2b, tensors)
+    near_tensors(n, lst, size, fs, ft, cols, qrow, r2a, r2b, r2c, tensors)
     near_sums(w, [m0a, m0b], [m0a, m0b], m0, tensors, lst, acc_a, acc_b, le, ev)
     mu_out[...] = update(pack, nbp, cf, ev)
     leave.wait()
@@ -739,7 +748,7 @@
     mu, t_nbr, lst, _, _ = call(
         part(near_first_kernel, nbp, w),
         [((2 * KP, w), F32), ((CONTR, near_size, 4 * L, L), BF16), ((2 + 2 * near_size,), jnp.int32)] + accs, "near_0",
-        tensor_scratch(2) + near_scratch + list_scratch,
+        tensor_scratch(2) + [pltpu.VMEM((4, L, L), F32)] + near_scratch + list_scratch,
         (m0, m0a, m0b, pack, packa, packb, cf, acc_a, acc_b), any_out=(2,), alias={7: 3, 8: 4},
     )
     for step in range(1, ITERS):

time: 47.6 us -> 47.6 us (level)
  no operation moved by 1% of the time
where the time goes in v7:
time: 47.6 us; the launch traced here: 47.4 us
  Pallas kernels  25.6 us (54%)
  starting transfers between devices  16.5 us (35%)
  waiting for transfers between devices  4.38 us (9%)
  between operations  0.94 us (2%)
    pallas_call x10, Pallas kernels, call(): pl.pallas_call(kernel, out_shape=[jax.ShapeDtypeStruct(s, d) for s, d in...  25.6 us
    ppermute x4, starting transfers between devices, exchange(): far = lax.ppermute(x, 'space', swap_pairs(nspace, 1))  15 us
    ppermute x4, waiting for transfers between devices, exchange(): far = lax.ppermute(x, 'space', swap_pairs(nspace, 1))  2.77 us
    ppermute x1, waiting for transfers between devices, body(): other = lax.ppermute(msg, 'bead', [(0, 1), (1, 0)])  1.6 us
    ppermute x1, starting transfers between devices, body(): other = lax.ppermute(msg, 'bead', [(0, 1), (1, 0)])  1.27 us
  transfers between devices with their start and end apart: 9, of which 3 were waited for; matrix products, arithmetic and copies ran while one was open for 0% of the time, Pallas kernels for 22%

profile of v7, /device:TPU:21, one launch (start us, length us, event | category | flops | bytes accessed | tf_op | source)
XLA Modules:
  0.0 47.4 jit_solution(7576884844109393019)
XLA Ops:
  0.6 1.5 %pack.1 = (f32[56,384]{1,0:T(8,128)S(1)}, bf16[192,512]{1,0:T(8,128)(2,1)S(1)}) custom-call(f32[3,16,384]{2,1,0:T(8,128)} %bitcast.3, f32[384]{0:T(512)} %charge.1, f32[384]{0:T(512)} %polar.1, s32[384]{0:T(512)} %mol.1), custom_call_target="tpu_custom_call" | custom-call | tf_op jit(solution)/shard_map/pack/pallas_call | solution.py:651
  2.1 3.7 %collective-permute-start.1 = (f32[56,384]{1,0:T(8,128)S(1)}, f32[56,384]{1,0:T(8,128)S(1)}, u32[]{:S(2)}, u32[]{:S(2)}) collective-permute-start(f32[56,384]{1,0:T(8,128)S(1)} %get-tuple-element.26.tgt), channel_id=1, source_target_pairs={{1,2},{2,1},{3,4},{4,3},{5,6},{6,5},{7,8},{8,7},{9,10},{10,9},{11,... | collective-permute-start | bytes 258056 | tf_op jit(solution)/shard_map/ppermute | solution.py:676
  5.8 0.1 collective-permute-start
  5.9 4.9 %perm_own.1 = (f32[3,384,128]{2,1,0:T(8,128)S(1)}, bf16[16,96,384]{2,1,0:T(8,128)(2,1)S(1)}, bf16[384,384]{1,0:T(8,128)(2,1)S(1)}, f32[56,384]{1,0:T(8,128)S(1)}) custom-call(f32[56,384]{1,0:T(8,128)S(1)} %get-tuple-element.26.tgt, bf16[192,512]{1,0:T(8,128)(2,1)S(1)} %get-tuple-element.27.sel), custom_call_target="tpu_custom_call" | custom-call | tf_op jit(solution)/shard_map/perm_own/pallas_call | solution.py:651
  10.9 0.0 collective-permute-done.1.srcb.packb
  10.9 0.0 collective-permute-done.srca.packa
  10.9 6.1 %perm_near.1 = (f32[48,384]{1,0:T(8,128)S(1)}, f32[24,384]{1,0:T(8,128)S(1)}, f32[3,384,128]{2,1,0:T(8,128)S(1)}) custom-call(f32[56,384]{1,0:T(8,128)S(1)} %get-tuple-element.28.tgt.pack, f32[56,384]{1,0:T(8,128)S(1)} %collective-permute-done.srca.packa, f32[56,384]{1,0:T(8,128)S(1)} %collective-permute-done.1.srcb.packb, ...), custom_call_target="tpu_custom_call", output_to_operand_aliasing={{2}: (5, {})} | custom-call | tf_op jit(solution)/shard_map/perm_near/pallas_call | solution.py:651
  17.0 1.3 %collective-permute-start.2 = (f32[24,384]{1,0:T(8,128)S(1)}, f32[24,384]{1,0:T(8,128)S(1)}, u32[]{:S(2)}, u32[]{:S(2)}) collective-permute-start(f32[24,384]{1,0:T(8,128)S(1)} %get-tuple-element.32.msg), channel_id=1, source_target_pairs={{0,16},{16,0},{1,17},{17,1},{2,18},{18,2},{3,19},{19,3},{4,20},{20... | collective-permute-start | bytes 110600 | tf_op jit(solution)/shard_map/ppermute | solution.py:724
  18.3 1.6 %collective-permute-done.2.other = f32[24,384]{1,0:T(8,128)S(1)} collective-permute-done((f32[24,384]{1,0:T(8,128)S(1)}, f32[24,384]{1,0:T(8,128)S(1)}, u32[]{:S(2)}, u32[]{:S(2)}) %collective-permute-start.2) | collective-permute-done | bytes 36896 | tf_op jit(solution)/shard_map/ppermute | solution.py:724
  19.9 0.2 start.1
  20.1 4.7 %collective-permute-start.4 = (f32[24,384]{1,0:T(8,128)S(1)}, f32[24,384]{1,0:T(8,128)S(1)}, u32[]{:S(2)}, u32[]{:S(2)}) collective-permute-start(f32[24,384]{1,0:T(8,128)S(1)} %get-tuple-element.33.m0), channel_id=1, source_target_pairs={{1,2},{2,1},{3,4},{4,3},{5,6},{6,5},{7,8},{8,7},{9,10},{10,9},{11,... | collective-permute-start | bytes 110600 | tf_op jit(solution)/shard_map/ppermute | solution.py:676
  24.8 0.1 collective-permute-start.3
  24.9 2.8 %own_0.1 = (bf16[4,6,512,128]{3,2,1,0:T(8,128)(2,1)S(1)}, f32[192,384]{1,0:T(8,128)S(1)}, f32[96,384]{1,0:T(8,128)S(1)}) custom-call(f32[24,384]{1,0:T(8,128)S(1)} %get-tuple-element.33.m0, f32[56,384]{1,0:T(8,128)S(1)} %get-tuple-element.28.tgt.pack), custom_call_target="tpu_custom_call" | custom-call | tf_op jit(solution)/shard_map/own_0/pallas_call | solution.py:651
  27.7 0.0 collective-permute-done.4.m0b
  27.7 0.0 collective-permute-done.3.m0a
  27.7 3.5 %near_0.1 = (f32[16,384]{1,0:T(8,128)S(1)}, bf16[4,18,512,128]{3,2,1,0:T(8,128)(2,1)S(1)}, s32[38]{0:T(128)S(1)}, f32[192,384]{1,0:T(8,128)S(1)}, f32[96,384]{1,0:T(8,128)S(1)}) custom-call(f32[24,384]{1,0:T(8,128)S(1)} %get-tuple-element.33.m0, f32[24,384]{1,0:T(8,128)S(1)} %collective-permute-done.3.m0a, ...), custom_call_target="tpu_custom_call", output_to_operand_aliasing={{3}: (7, {}), {4}: (8, {})} | custom-call | tf_op jit(solution)/shard_map/near_0/pallas_call | solution.py:651
  31.2 3.3 %collective-permute-start.6 = (f32[16,384]{1,0:T(8,128)S(1)}, f32[16,384]{1,0:T(8,128)S(1)}, u32[]{:S(2)}, u32[]{:S(2)}) collective-permute-start(f32[16,384]{1,0:T(8,128)S(1)} %get-tuple-element.37.mu), channel_id=1, source_target_pairs={{1,2},{2,1},{3,4},{4,3},{5,6},{6,5},{7,8},{8,7},{9,10},{10,9},{11,... | collective-permute-start | bytes 73736 | tf_op jit(solution)/shard_map/ppermute | solution.py:676
  34.5 0.1 collective-permute-start.5
  34.6 1.2 %own_1.1 = (f32[192,384]{1,0:T(8,128)S(1)}, f32[96,384]{1,0:T(8,128)S(1)}) custom-call(f32[16,384]{1,0:T(8,128)S(1)} %get-tuple-element.37.mu, f32[24,384]{1,0:T(8,128)S(1)} %get-tuple-element.33.m0, bf16[4,6,512,128]{3,2,1,0:T(8,128)(2,1)S(1)} %get-tuple-element.38.tensors), custom_call_target="tpu_custom_call" | custom-call | tf_op jit(solution)/shard_map/own_1/pallas_call | solution.py:651
  35.8 1.4 %collective-permute-done.6.mub = f32[16,384]{1,0:T(8,128)S(1)} collective-permute-done((f32[16,384]{1,0:T(8,128)S(1)}, f32[16,384]{1,0:T(8,128)S(1)}, u32[]{:S(2)}, u32[]{:S(2)}) %collective-permute-start.6) | collective-permute-done | bytes 24608 | tf_op jit(solution)/shard_map/ppermute | solution.py:676
  37.2 0.0 collective-permute-done.5.mua
  37.2 1.4 %near_1.1 = (f32[16,384]{1,0:T(8,128)S(1)}, f32[192,384]{1,0:T(8,128)S(1)}, f32[96,384]{1,0:T(8,128)S(1)}) custom-call(f32[16,384]{1,0:T(8,128)S(1)} %collective-permute-done.5.mua, f32[16,384]{1,0:T(8,128)S(1)} %collective-permute-done.6.mub, f32[24,384]{1,0:T(8,128)S(1)} %get-tuple-element.33.m0, ...), custom_call_target="tpu_custom_call", output_to_operand_aliasing={{1}: (7, {}), {2}: (8, {})} | custom-call | tf_op jit(solution)/shard_map/near_1/pallas_call | solution.py:651
  38.7 3.3 %collective-permute-start.8 = (f32[16,384]{1,0:T(8,128)S(1)}, f32[16,384]{1,0:T(8,128)S(1)}, u32[]{:S(2)}, u32[]{:S(2)}) collective-permute-start(f32[16,384]{1,0:T(8,128)S(1)} %get-tuple-element.43.mu), channel_id=1, source_target_pairs={{1,2},{2,1},{3,4},{4,3},{5,6},{6,5},{7,8},{8,7},{9,10},{10,9},{11,... | collective-permute-start | bytes 73736 | tf_op jit(solution)/shard_map/ppermute | solution.py:676
  42.0 0.1 collective-permute-start.7
  42.1 1.3 %own_last.1 = (f32[192,384]{1,0:T(8,128)S(1)}, f32[96,384]{1,0:T(8,128)S(1)}, f32[48,384]{1,0:T(8,128)S(1)}) custom-call(f32[16,384]{1,0:T(8,128)S(1)} %get-tuple-element.43.mu, f32[24,384]{1,0:T(8,128)S(1)} %get-tuple-element.33.m0, bf16[4,6,512,128]{3,2,1,0:T(8,128)(2,1)S(1)} %get-tuple-element.38.tensors, f32[48,384]{1,0:T(8,128)S(1)} %get-tuple-element.44.perm, ...), custom_call_target="tpu_custom_call" | custom-call | tf_op jit(solution)/shard_map/own_last/pallas_call | solution.py:651
  43.4 1.3 %collective-permute-done.8.mub = f32[16,384]{1,0:T(8,128)S(1)} collective-permute-done((f32[16,384]{1,0:T(8,128)S(1)}, f32[16,384]{1,0:T(8,128)S(1)}, u32[]{:S(2)}, u32[]{:S(2)}) %collective-permute-start.8) | collective-permute-done | bytes 24608 | tf_op jit(solution)/shard_map/ppermute | solution.py:676
  44.7 0.0 collective-permute-done.7.mua
  44.7 2.5 %final.1 = (f32[3,16,384]{2,1,0:T(8,128)}, f32[3,4,384]{2,1,0:T(4,128)}, f32[192,384]{1,0:T(8,128)S(1)}, f32[96,384]{1,0:T(8,128)S(1)}) custom-call(f32[16,384]{1,0:T(8,128)S(1)} %collective-permute-done.7.mua, f32[16,384]{1,0:T(8,128)S(1)} %collective-permute-done.8.mub, ...), custom_call_target="tpu_custom_call", output_to_operand_aliasing={{2}: (8, {}), {3}: (9, {})} | custom-call | tf_op jit(solution)/shard_map/final/pallas_call | solution.py:651
Async XLA Ops:
  2.1 8.7 %collective-permute-start.1 = (f32[56,384]{1,0:T(8,128)S(1)}, f32[56,384]{1,0:T(8,128)S(1)}, u32[]{:S(2)}, u32[]{:S(2)}) collective-permute-start(f32[56,384]{1,0:T(8,128)S(1)} %get-tuple-element.26.tgt), channel_id=1, source_target_pairs={{1,2},{2,1},{3,4},{4,3},{5,6},{6,5},{7,8},{8,7},{9,10},{10,9},{11,... | collective-permute-start | bytes 258056 | tf_op jit(solution)/shard_map/ppermute | solution.py:676
  5.8 5.0 %collective-permute-start = (f32[56,384]{1,0:T(8,128)S(1)}, f32[56,384]{1,0:T(8,128)S(1)}, u32[]{:S(2)}, u32[]{:S(2)}) collective-permute-start(f32[56,384]{1,0:T(8,128)S(1)} %get-tuple-element.26.tgt), channel_id=1, source_target_pairs={{0,1},{1,0},{2,3},{3,2},{4,5},{5,4},{6,7},{7,6},{8,9},{9,8},{10,11... | collective-permute-start | bytes 258056 | tf_op jit(solution)/shard_map/ppermute | solution.py:675
  17.0 2.9 %collective-permute-start.2 = (f32[24,384]{1,0:T(8,128)S(1)}, f32[24,384]{1,0:T(8,128)S(1)}, u32[]{:S(2)}, u32[]{:S(2)}) collective-permute-start(f32[24,384]{1,0:T(8,128)S(1)} %get-tuple-element.32.msg), channel_id=1, source_target_pairs={{0,16},{16,0},{1,17},{17,1},{2,18},{18,2},{3,19},{19,3},{4,20},{20... | collective-permute-start | bytes 110600 | tf_op jit(solution)/shard_map/ppermute | solution.py:724
  20.1 7.6 %collective-permute-start.4 = (f32[24,384]{1,0:T(8,128)S(1)}, f32[24,384]{1,0:T(8,128)S(1)}, u32[]{:S(2)}, u32[]{:S(2)}) collective-permute-start(f32[24,384]{1,0:T(8,128)S(1)} %get-tuple-element.33.m0), channel_id=1, source_target_pairs={{1,2},{2,1},{3,4},{4,3},{5,6},{6,5},{7,8},{8,7},{9,10},{10,9},{11,... | collective-permute-start | bytes 110600 | tf_op jit(solution)/shard_map/ppermute | solution.py:676
  24.8 2.9 %collective-permute-start.3 = (f32[24,384]{1,0:T(8,128)S(1)}, f32[24,384]{1,0:T(8,128)S(1)}, u32[]{:S(2)}, u32[]{:S(2)}) collective-permute-start(f32[24,384]{1,0:T(8,128)S(1)} %get-tuple-element.33.m0), channel_id=1, source_target_pairs={{0,1},{1,0},{2,3},{3,2},{4,5},{5,4},{6,7},{7,6},{8,9},{9,8},{10,11... | collective-permute-start | bytes 110600 | tf_op jit(solution)/shard_map/ppermute | solution.py:675
  31.2 6.0 %collective-permute-start.6 = (f32[16,384]{1,0:T(8,128)S(1)}, f32[16,384]{1,0:T(8,128)S(1)}, u32[]{:S(2)}, u32[]{:S(2)}) collective-permute-start(f32[16,384]{1,0:T(8,128)S(1)} %get-tuple-element.37.mu), channel_id=1, source_target_pairs={{1,2},{2,1},{3,4},{4,3},{5,6},{6,5},{7,8},{8,7},{9,10},{10,9},{11,... | collective-permute-start | bytes 73736 | tf_op jit(solution)/shard_map/ppermute | solution.py:676
  34.5 2.8 %collective-permute-start.5 = (f32[16,384]{1,0:T(8,128)S(1)}, f32[16,384]{1,0:T(8,128)S(1)}, u32[]{:S(2)}, u32[]{:S(2)}) collective-permute-start(f32[16,384]{1,0:T(8,128)S(1)} %get-tuple-element.37.mu), channel_id=1, source_target_pairs={{0,1},{1,0},{2,3},{3,2},{4,5},{5,4},{6,7},{7,6},{8,9},{9,8},{10,11... | collective-permute-start | bytes 73736 | tf_op jit(solution)/shard_map/ppermute | solution.py:675
  38.7 6.0 %collective-permute-start.8 = (f32[16,384]{1,0:T(8,128)S(1)}, f32[16,384]{1,0:T(8,128)S(1)}, u32[]{:S(2)}, u32[]{:S(2)}) collective-permute-start(f32[16,384]{1,0:T(8,128)S(1)} %get-tuple-element.43.mu), channel_id=1, source_target_pairs={{1,2},{2,1},{3,4},{4,3},{5,6},{6,5},{7,8},{8,7},{9,10},{10,9},{11,... | collective-permute-start | bytes 73736 | tf_op jit(solution)/shard_map/ppermute | solution.py:676
  42.0 2.8 %collective-permute-start.7 = (f32[16,384]{1,0:T(8,128)S(1)}, f32[16,384]{1,0:T(8,128)S(1)}, u32[]{:S(2)}, u32[]{:S(2)}) collective-permute-start(f32[16,384]{1,0:T(8,128)S(1)} %get-tuple-element.43.mu), channel_id=1, source_target_pairs={{0,1},{1,0},{2,3},{3,2},{4,5},{5,4},{6,7},{7,6},{8,9},{9,8},{10,11... | collective-permute-start | bytes 73736 | tf_op jit(solution)/shard_map/ppermute | solution.py:675
